TPU v7x, 512 devices: a whole 4x4x16 slice. The times are simulated.
512 devices in a mesh: gx: 32 (over z, core), vert: 16 (over y, x).
Axes of the slice: x: 4, y: 4, z: 16, core: 2. Of those that a mesh axis runs over, the one named last changes fastest.
Arguments:
- distribution: float32 [4096, 32, 256], P('vert', 'gx'), may hold values from -6 to 6
- relax_rate: float32 [32, 256], P('gx'), may hold values from 0.3 to 3
- node_weight: float32 [4096], P('vert'), may hold values from 0.05 to 1
- kernel_tiles: bfloat16 [32, 128, 1536], P('vert'), may hold values from -0.15625 to 0.15625
- tile_cols: int32 [32, 12], P('vert'), may hold values from 0 to 31, as said below
Outputs:
- new_distribution: float32 [4096, 32, 256], P('vert', 'gx')
Inputs may be any that keep to these rules, and one draw needn't show every extreme that they name: `tile_cols`: row block r lists its own block r first; the 12 column blocks listed for one row block are distinct.
All inputs are finite; a program needn't handle non-finite values.
Results may differ from a plain program's by a relative error of at most 0.0021.
Values may be sent and summed in bfloat16 or wider, within the bound.
No kernel may reach another device: no remote copies, remote signals or barrier semaphores. Data moves between devices by JAX's collectives and lax.ppermute only.
A program may use at most 64 MiB of HBM per device.

v0:
```python
import jax
import jax.numpy as jnp
from jax import lax
from jax.sharding import PartitionSpec as P

Q = 16
TILE = 128
NZ = 4
STEPS = 2
V = 4096
RBLK = 32


COURANT_SCALE = 0.3
KERNEL_STEP = 0.5
PRECISE = lax.Precision.HIGHEST


def extended(block, sides, width):
    for axis, dim in sides:
        count = lax.axis_size(axis)
        forward = [(i, i + 1) for i in range(count - 1)]
        forward.append((count - 1, 0))
        backward = [(target, source) for source, target in forward]
        low = lax.ppermute(
            lax.slice_in_dim(block, block.shape[dim] - width, None, axis=dim), axis, forward
        )
        high = lax.ppermute(lax.slice_in_dim(block, 0, width, axis=dim), axis, backward)
        block = jnp.concatenate([low, block, high], axis=dim)
    return block


def node_components(first_node, node_count):
    node_index = first_node + jnp.arange(node_count, dtype=jnp.int32)
    middle = (Q - 1) / 2.0
    speed_x = ((node_index % Q).astype(jnp.float32) - middle) / middle
    speed_y = ((node_index // Q % Q).astype(jnp.float32) - middle) / middle
    speed_z = ((node_index // (Q * Q)).astype(jnp.float32) - middle) / middle
    courant = COURANT_SCALE * jnp.stack([speed_x, speed_y, speed_z])
    squares = speed_x * speed_x + speed_y * speed_y + speed_z * speed_z
    invariants = jnp.stack([jnp.ones_like(speed_x), speed_x, speed_y, speed_z, squares])
    return (courant, invariants)


def gram_inverse(weighted, invariants):
    gram_matrix = jnp.dot(weighted, invariants.T, precision=PRECISE)
    factor = jnp.linalg.cholesky(gram_matrix)
    return jax.scipy.linalg.cho_solve((factor, True), jnp.eye(5, dtype=gram_matrix.dtype))


def advect(source, lower_x, upper_x, courant):
    plane_size = source.shape[-1]
    z_index = jnp.arange(plane_size, dtype=jnp.int32) % NZ
    lower_y = jnp.roll(source, NZ, axis=-1)
    upper_y = jnp.roll(source, -NZ, axis=-1)
    lower_z = jnp.where(
        z_index == 0, jnp.roll(source, 1 - NZ, axis=-1), jnp.roll(source, 1, axis=-1)
    )
    upper_z = jnp.where(
        z_index == NZ - 1, jnp.roll(source, NZ - 1, axis=-1), jnp.roll(source, -1, axis=-1)
    )
    total_flux = jnp.zeros_like(source)
    for component, below, above in (
        (0, lower_x, upper_x),
        (1, lower_y, upper_y),
        (2, lower_z, upper_z),
    ):
        node_speed = courant[component][:, None, None]
        total_flux = (
            total_flux
            + jnp.maximum(node_speed, 0.0) * (source - below)
            + jnp.minimum(node_speed, 0.0) * (above - source)
        )
    return source - total_flux


def apply_kernel(blocks, tile_rows, column_lists):
    cell_count = blocks.shape[-1]

    def one_block(tile_pair):
        tile_row, column_list = tile_pair
        picked = jnp.take(blocks, column_list, axis=0).reshape(-1, cell_count)
        return jnp.dot(tile_row, picked, preferred_element_type=jnp.float32)

    return lax.map(one_block, (tile_rows, column_lists))


def per_device(distribution, relax_rate, node_weight, kernel_tiles, tile_cols):
    node_local, slab_depth, plane_cells = distribution.shape
    cell_count = slab_depth * plane_cells
    first_node = lax.axis_index("vert") * node_local
    courant, invariants = node_components(first_node, node_local)
    all_weights = lax.all_gather(node_weight, "vert", axis=0, tiled=True)
    all_speeds, all_invariants = node_components(0, V)
    all_weighted = all_invariants * all_weights[None, :]
    inverse = gram_inverse(all_weighted, all_invariants)
    relax_share = relax_rate / (1.0 + relax_rate)
    current = distribution
    for step_index in range(STEPS):
        rounded = current.astype(jnp.bfloat16)
        padded = extended(current, (("gx", 1),), 1)
        lower_x = padded[:, :-2]
        upper_x = padded[:, 2:]
        advected = advect(current, lower_x, upper_x, courant)
        gathered = lax.all_gather(
            rounded.reshape(node_local, cell_count), "vert", axis=0, tiled=True
        )
        kernel_term = apply_kernel(
            gathered.reshape(RBLK, TILE, cell_count), kernel_tiles, tile_cols
        )
        explicit = advected + KERNEL_STEP * kernel_term.reshape(current.shape)
        local_weighted = invariants * node_weight[None, :]
        partial_moments = jnp.dot(
            local_weighted, explicit.reshape(node_local, cell_count), precision=PRECISE
        )
        moments = lax.psum(partial_moments, "vert")
        coeffs = jnp.dot(inverse, moments, precision=PRECISE)
        equilibrium = jnp.dot(invariants.T, coeffs, precision=PRECISE).reshape(current.shape)
        current = explicit - relax_share[None] * (explicit - equilibrium)
    return current


def solution(mesh):
    placed = (
        P("vert", "gx", None),
        P("gx", None),
        P("vert"),
        P("vert", None, None),
        P("vert", None),
    )
    return jax.shard_map(
        per_device, mesh=mesh, in_specs=placed, out_specs=P("vert", "gx", None), check_vma=False
    )
```

profile of v0, /device:TPU:32, one launch (start us, length us, event | category | flops | bytes accessed | tf_op | source)
XLA Modules:
  0.0 240.1 jit_solution(10722678696788781217)
XLA Ops:
  6.5 1.1 copy.54
  7.6 0.0 collective-permute-start.1
  7.6 0.5 collective-permute-start
  8.1 1.6 copy.68
  9.8 0.0 all-gather.6.cloned.1.call-update
  9.8 0.0 copy-start
  9.8 0.0 copy-start.1
  9.8 0.0 all-gather.8.cloned.1.call-start
  9.9 0.1 fusion.55
  10.0 0.1 fusion.49
  10.1 0.1 stack.8
  10.2 23.6 %all-gather.2 = f32[16,1,256]{2,1,0:T(1,128)S(1)} all-gather(f32[1,1,256]{2,1,0:T(1,128)} %bitcast.109), channel_id=1, replica_groups=mesh['gx'=32,'vert'=16] {'vert'}, dimensions={0}, use_global_device_ids=true | all-gather | bytes 17408 | tf_op jit(solution)/shard_map/all_gather | solution.py:93
  33.8 0.4 fusion.44
  34.1 0.1 copy.57
  34.2 0.5 cholesky.17
  34.7 0.1 select_reduce_fusion
  34.8 0.6 compare_reduce_fusion
  35.4 0.6 fusion.59
  36.1 0.4 custom-call.10
  36.6 0.7 add_divide_fusion
  37.3 0.2 fusion.60
  37.5 0.1 fusion.62
  37.7 0.7 fusion.82
  38.5 36.6 %all-gather.6.cloned.1.call-done = bf16[4096,1,256]{2,0,1:T(8,128)(2,1)} async-done(((bf16[256,1,256]{2,0,1:T(8,128)(2,1)}), bf16[4096,1,256]{2,0,1:T(8,128)(2,1)}) %all-gather.6.cloned.1.call-update) | async-done | bytes 2097168 | tf_op jit(solution)/shard_map/all_gather | solution.py:105
  75.1 0.0 copy-done
  75.1 0.0 copy-done.1
  75.1 5.3 %while.20 = (s32[]{:T(128)}, f32[2,128,256]{2,1,0:T(8,128)S(1)}, bf16[2,128,1536]{2,1,0:T(8,128)(2,1)S(1)}, s32[2,12]{1,0:T(2,128)S(1)}, bf16[32,128,256]{2,1,0:T(8,128)(2,1)}, /*index=5*/s32[]{:T(128)}) while((s32[]{:T(128)}, f32[2,128,256]{2,1,0:T(8,128)S(1)}, bf16[2,128,1536]{2,1,0:T(8,128)(2,1)S(1)}, s32[2,12]{1,0:T(2,128)S(1)}, ...), condition=%wide.region_1.3_spmd, body=%wide.region_0.2_spmd.sunk | while | flops 101057608 | bytes 4461865 | solution.py:85
  75.1 2.2 gather_fusion
  77.3 0.1 broadcast_select_fusion.4
  77.5 0.3 fusion.111
  77.8 2.2 gather_fusion
  80.0 0.1 broadcast_select_fusion.4
  80.2 0.3 fusion.111
  80.4 0.0 copy-start.2
  80.5 0.1 copy.64
  80.6 0.0 collective-permute-done.1
  80.6 0.0 collective-permute-done
  80.6 1.4 fusion.22
  82.0 0.3 fusion.42
  82.3 38.7 %psum.14 = f32[5,256]{1,0:T(8,128)S(1)} all-reduce(f32[5,256]{1,0:T(8,128)S(1)} %fusion.42), channel_id=1, replica_groups=mesh['gx'=32,'vert'=16] {'vert'}, use_global_device_ids=true, to_apply=%region_4.6 | all-reduce | flops 1280 | bytes 10240 | tf_op jit(solution)/shard_map/psum | solution.py:116
  121.0 0.1 fusion.89
  121.1 1.1 fusion.88
  122.2 0.0 all-gather.8.cloned.1.call-update
  122.2 0.0 collective-permute-start.3
  122.3 0.5 collective-permute-start.2
  122.9 0.7 fusion.79
  123.6 58.2 %all-gather.8.cloned.1.call-done = bf16[4096,1,256]{0,2,1:T(8,128)(2,1)} async-done(((bf16[256,1,256]{0,2,1:T(8,128)(2,1)}), bf16[4096,1,256]{0,2,1:T(8,128)(2,1)}) %all-gather.8.cloned.1.call-update) | async-done | bytes 2097168 | tf_op jit(solution)/shard_map/all_gather | solution.py:105
  181.8 4.1 %copy.65 = bf16[4096,1,256]{2,0,1:T(8,128)(2,1)} copy(bf16[4096,1,256]{0,2,1:T(8,128)(2,1)} %all-gather.8.cloned.1.call-done) | data formatting | bytes 4194304 | tf_op jit(solution)/shard_map/while | solution.py:85
  185.9 5.3 %while.21 = (s32[]{:T(128)}, f32[2,128,256]{2,1,0:T(8,128)S(1)}, bf16[2,128,1536]{2,1,0:T(8,128)(2,1)S(1)}, s32[2,12]{1,0:T(2,128)S(1)}, bf16[32,128,256]{2,1,0:T(8,128)(2,1)}, /*index=5*/s32[]{:T(128)}) while((s32[]{:T(128)}, f32[2,128,256]{2,1,0:T(8,128)S(1)}, bf16[2,128,1536]{2,1,0:T(8,128)(2,1)S(1)}, s32[2,12]{1,0:T(2,128)S(1)}, ...), condition=%wide.region_6.8_spmd, body=%wide.region_5.7_spmd.sunk | while | flops 101057608 | bytes 4461865 | solution.py:85
  186.0 2.2 gather_fusion.1
  188.2 0.1 broadcast_select_fusion.5
  188.3 0.3 fusion.114
  188.6 2.2 gather_fusion.1
  190.8 0.1 broadcast_select_fusion.5
  191.0 0.3 fusion.114
  191.3 0.1 copy.66
  191.4 0.0 collective-permute-done.3
  191.4 0.0 collective-permute-done.2
  191.4 1.4 fusion.34
  192.8 0.3 fusion.40
  193.1 38.7 %psum.15 = f32[5,256]{1,0:T(8,128)S(1)} all-reduce(f32[5,256]{1,0:T(8,128)S(1)} %fusion.40), channel_id=1, replica_groups=mesh['gx'=32,'vert'=16] {'vert'}, use_global_device_ids=true, to_apply=%region_7.9 | all-reduce | flops 1280 | bytes 10240 | tf_op jit(solution)/shard_map/psum | solution.py:116
  231.8 0.1 fusion.90
  231.9 0.4 fusion.15
  232.4 0.8 copy.62
  (33 shorter events, 0.5 us)
Async XLA Ops:
  6.5 68.5 %all-gather.6.cloned.1.call-start = ((), (), s32[]{:S(2)}) async-start(), calls=%async_computation | async-start | bytes 2228224 | tf_op jit(solution)/shard_map/all_gather | solution.py:105
  7.6 73.0 %collective-permute-start.1 = (f32[256,1,256]{0,2,1:T(8,128)S(1)}, f32[256,1,256]{0,2,1:T(8,128)}, u32[]{:S(2)}, u32[]{:S(2)}) collective-permute-start(f32[256,1,256]{0,2,1:T(8,128)S(1)} %copy.54), channel_id=1, source_target_pairs={{16,0},{32,16},{48,32},{64,48},{80,64},{96,80},{112,96},{128,112},... | collective-permute-start | bytes 786440 | tf_op jit(solution)/shard_map/ppermute | solution.py:28
  7.6 73.0 %collective-permute-start = (f32[256,1,256]{0,2,1:T(8,128)S(1)}, f32[256,1,256]{0,2,1:T(8,128)}, u32[]{:S(2)}, u32[]{:S(2)}) collective-permute-start(f32[256,1,256]{0,2,1:T(8,128)S(1)} %copy.54), channel_id=1, source_target_pairs={{0,16},{16,32},{32,48},{48,64},{64,80},{80,96},{96,112},{112,128},... | collective-permute-start | bytes 786440 | tf_op jit(solution)/shard_map/ppermute | solution.py:25
  9.8 65.3 %copy-start = (bf16[2,128,1536]{2,1,0:T(8,128)(2,1)S(1)}, bf16[2,128,1536]{2,1,0:T(8,128)(2,1)}, u32[]{:S(2)}) copy-start(bf16[2,128,1536]{2,1,0:T(8,128)(2,1)} %param.14) | copy-start | bytes 2359300
  9.8 65.3 %copy-start.1 = (s32[2,12]{1,0:T(2,128)S(1)}, s32[2,12]{1,0:T(2,128)}, u32[]{:S(2)}) copy-start(s32[2,12]{1,0:T(2,128)} %param.15) | copy-start | bytes 292
  9.8 172.0 %all-gather.8.cloned.1.call-start = ((), (), s32[]{:S(2)}) async-start(), calls=%async_computation.1 | async-start | bytes 2228224 | tf_op jit(solution)/shard_map/all_gather | solution.py:105
  80.4 1.6 copy-start.2
  122.2 69.2 %collective-permute-start.3 = (f32[256,1,256]{0,2,1:T(8,128)S(1)}, f32[256,1,256]{0,2,1:T(8,128)}, u32[]{:S(2)}, u32[]{:S(2)}) collective-permute-start(f32[256,1,256]{0,2,1:T(8,128)S(1)} %get-tuple-element.127), channel_id=1, source_target_pairs={{16,0},{32,16},{48,32},{64,48},{80,64},{96,80},{112,96},{128,112},... | collective-permute-start | bytes 786440 | tf_op jit(solution)/shard_map/ppermute | solution.py:28
  122.3 69.2 %collective-permute-start.2 = (f32[256,1,256]{0,2,1:T(8,128)S(1)}, f32[256,1,256]{0,2,1:T(8,128)}, u32[]{:S(2)}, u32[]{:S(2)}) collective-permute-start(f32[256,1,256]{0,2,1:T(8,128)S(1)} %get-tuple-element.127), channel_id=1, source_target_pairs={{0,16},{16,32},{32,48},{48,64},{64,80},{80,96},{96,112},{112,128},... | collective-permute-start | bytes 786440 | tf_op jit(solution)/shard_map/ppermute | solution.py:25
Sparse Core Ops, SparseCore 0:
  10.4 64.6 all-gather.5
  122.3 59.4 all-gather.7
where the time goes:
time: 241 us; the launch traced here: 240 us
  blocking collectives  101 us (42%)
  waiting for transfers between devices  94.9 us (39%)
  local copies, waits for them, and re-layouts  18.6 us (8%)
  between operations  13.7 us (6%)
  other arithmetic  6.55 us (3%)
  matrix products  4.07 us (2%)
    all_gather x2, waiting for transfers between devices, per_device(): lax.all_gather(rounded.reshape(node_local, cell_count), 'vert', axis=0, t...  94.8 us
    psum x2, blocking collectives, per_device(): moments = lax.psum(partial_moments, 'vert')  77.4 us
    all_gather x1, blocking collectives, per_device(): all_weights = lax.all_gather(node_weight, 'vert', axis=0, tiled=True)  23.6 us
    gather x4, local copies, waits for them, and re-layouts, one_block(): picked = jnp.take(blocks, column_list, axis=0).reshape(-1, cell_count)  8.75 us
  transfers between devices with their start and end apart: 6, of which 2 were waited for; matrix products, arithmetic and copies ran while one was open for 9% of the time, Pallas kernels for 0%

commit v1 on v0

v1 whole, which is shorter than its diff:
```python
import functools

import jax
import jax.numpy as jnp
from jax import lax
from jax.experimental import pallas as pl
from jax.experimental.pallas import tpu as pltpu
from jax.sharding import PartitionSpec as P

Q = 16
TILE = 128
NB = 12
NZ = 4
CELLS = 256
NODES = 256
PARTS = 16
COURANT_SCALE = 0.3
KERNEL_STEP = 0.5
MIDDLE = (Q - 1) / 2.0
EXTRA = 16
PAYLOAD = 32
GROUPS = 7
F32 = jnp.float32
BF16 = jnp.bfloat16
HIGHEST = lax.Precision.HIGHEST
VMEM_BYTES = 48 * 1024 * 1024


def iota(shape, dim):
    return lax.broadcasted_iota(jnp.int32, shape, dim)


def speed_of(index):
    return (index.astype(F32) - MIDDLE) / MIDDLE


def from_below_y(a):
    return pltpu.roll(a, NZ, 1)


def from_above_y(a):
    return pltpu.roll(a, CELLS - NZ, 1)


def from_below_z(a):
    first = iota(a.shape, 1) % NZ == 0
    return jnp.where(first, pltpu.roll(a, CELLS - (NZ - 1), 1), pltpu.roll(a, 1, 1))


def from_above_z(a):
    last = iota(a.shape, 1) % NZ == NZ - 1
    return jnp.where(last, pltpu.roll(a, NZ - 1, 1), pltpu.roll(a, CELLS - 1, 1))


def split(a, pieces):
    out = []
    for _ in range(pieces):
        out.append(a.astype(BF16))
        a = a - out[-1].astype(F32)
    return out


def three_sum(a):
    return a[0:8] + a[8:16] + a[16:24]


def node_rows(z_speed):
    node = iota((8, NODES), 1)
    k = iota((8, NODES), 0)
    x, y = speed_of(node % Q), speed_of(node // Q)
    z = jnp.full((8, NODES), z_speed)
    invariants = jnp.where(k == 0, 1.0, 0.0)
    for row, value in ((1, x), (2, y), (3, z), (4, x * x + y * y + z * z)):
        invariants = jnp.where(k == row, value, invariants)
    factors = [None]
    for speed in (x, y, z):
        factors.append(COURANT_SCALE * jnp.maximum(speed, 0.0))
        factors.append(COURANT_SCALE * jnp.maximum(-speed, 0.0))
    return invariants, factors


def kernel_product(gathered_ref, stride, tiles_ref, cols_ref, acc_ref):
    for r in range(2):
        blocks = []
        for j in range(NB):
            col = cols_ref[r, j]
            start = (col // 2) * stride + (col % 2) * TILE
            blocks.append(gathered_ref[pl.ds(pl.multiple_of(start, 16), TILE), :])
        acc_ref[r * TILE : (r + 1) * TILE, :] = jnp.dot(
            tiles_ref[r], jnp.concatenate(blocks, axis=0), preferred_element_type=F32
        )


def explicit_rows(m, s, below, above, kernel_term, z_speed):
    row = iota((Q, CELLS), 0)
    lane = iota((Q, CELLS), 1)
    x_courant = COURANT_SCALE * jnp.abs(speed_of(row))
    y_courant = COURANT_SCALE * abs((m - MIDDLE) / MIDDLE)
    z_courant = COURANT_SCALE * jnp.abs(z_speed)
    up = z_speed > 0
    edge = jnp.where(up, 0, NZ - 1)
    near = pltpu.roll(s, jnp.where(up, 1, CELLS - 1), 1)
    far = pltpu.roll(s, jnp.where(up, CELLS - (NZ - 1), NZ - 1), 1)
    z_side = jnp.where(lane % NZ == edge, far, near)
    y_side = from_below_y(s) if m >= Q // 2 else from_above_y(s)
    x_side = jnp.concatenate([above, below], axis=0)
    flux = x_courant * (s - x_side) + y_courant * (s - y_side) + z_courant * (s - z_side)
    return s - flux + KERNEL_STEP * kernel_term


def equilibrium_rows(m, coeffs, z_speed):
    y = (m - MIDDLE) / MIDDLE
    x = speed_of(iota((Q, CELLS), 0))
    common = coeffs[0:1] + y * coeffs[2:3] + z_speed * coeffs[3:4]
    common = common + (y * y + z_speed * z_speed) * coeffs[4:5]
    return common + x * coeffs[1:2] + (x * x) * coeffs[4:5]


def apply_small(matrix, first, rows):
    total = matrix[:, first : first + 1] * rows[0:1]
    for k in range(1, 5):
        total = total + matrix[:, first + k : first + k + 1] * rows[k : k + 1]
    return total


def inverse_of(gram):
    row, lane = iota((8, 128), 0), iota((8, 128), 1)
    work = jnp.where((row < 5) & (lane < 5), gram, 0.0)
    work = jnp.where((lane == row + 8) | ((lane == row) & (row >= 5)), 1.0, work)
    for i in range(5):
        pivot = work[i : i + 1, :] / work[i : i + 1, i : i + 1]
        work = jnp.where(row == i, pivot, work - work[:, i : i + 1] * pivot)
    return work


def load_state(ref, m):
    halves = [ref[pl.ds(2 * Q * m + h, Q, stride=2), :] for h in range(2)]
    return jnp.concatenate(halves, axis=1)


def store_sides(m, s, low_ref, high_ref):
    low_ref[8 * m : 8 * m + 8, :] = s[0:8]
    high_ref[8 * m : 8 * m + 8, :] = s[8:16]


def prologue_kernel(state_ref, copies_ref, low_ref, high_ref):
    for m in range(Q):
        s = load_state(state_ref, m)
        store_sides(m, s, low_ref, high_ref)
        rounded = s.astype(BF16)
        for part in range(PARTS):
            copies_ref[part * NODES + Q * m : part * NODES + Q * m + Q, :] = rounded


def first_kernel(
    cols_ref, z_ref, state_ref, rate_ref, weight_ref, tiles_ref, gathered_ref, above_ref, below_ref,
    scaled_ref, payload_ref, acc_ref, wk_ref,
):
    z_speed = z_ref[0]
    invariants, factors = node_rows(z_speed)
    base = weight_ref[...] * invariants
    phi = jnp.concatenate([base] + [base * f for f in factors[1:]], axis=0)
    kernel_product(gathered_ref, NODES, tiles_ref, cols_ref, acc_ref)
    keep = 1.0 / (1.0 + rate_ref[...])
    for m in range(Q):
        rows = slice(Q * m, Q * m + Q)
        half = slice(8 * m, 8 * m + 8)
        s = load_state(state_ref, m)
        e = explicit_rows(m, s, below_ref[half, :], above_ref[half, :], acc_ref[rows, :], z_speed)
        scaled_ref[rows, :] = keep * e
    moments = jnp.dot(phi, scaled_ref[...], precision=HIGHEST, preferred_element_type=F32)
    group = [moments[8 * t : 8 * t + 8] for t in range(GROUPS)]
    flux = group[1] + group[2]
    for t, shift in ((3, from_below_y), (4, from_above_y), (5, from_below_z), (6, from_above_z)):
        flux = flux + (group[t] - shift(group[t]))
    padded = jnp.concatenate([phi, jnp.zeros((TILE - 8 * GROUPS, NODES), F32)], axis=0)
    small = lax.dot_general(
        invariants, padded, (((1,), (1,)), ((), ())), precision=HIGHEST, preferred_element_type=F32
    )
    small = jnp.concatenate([small, jnp.zeros((8, CELLS - TILE), F32)], axis=1)
    wk_ref[...] = jnp.zeros_like(wk_ref)
    pieces = jnp.concatenate([p.astype(F32) for p in split(base, 3)], axis=0).astype(BF16)
    for r in range(2):
        part = three_sum(
            jnp.dot(pieces[:, r * TILE : (r + 1) * TILE], tiles_ref[r], preferred_element_type=F32)
        )
        for j in range(NB):
            col = cols_ref[r, j]
            wk_ref[col] = wk_ref[col] + part[:, j * TILE : (j + 1) * TILE]
    mine = iota((8, CELLS), 0) < 5
    third = jnp.where(mine, group[1], pltpu.roll(small, 5, 0))
    fourth = jnp.where(mine, group[2], pltpu.roll(small, 2, 0))
    for part in range(PARTS):
        wk = jnp.concatenate([wk_ref[2 * part], wk_ref[2 * part + 1]], axis=1)
        start = part * PAYLOAD
        payload_ref[start : start + 8, :] = jnp.where(mine, group[0], pltpu.roll(wk, 5, 0))
        payload_ref[start + 8 : start + 16, :] = jnp.where(mine, flux, pltpu.roll(wk, 2, 0))
        payload_ref[start + 16 : start + 24, :] = third
        payload_ref[start + 24 : start + 32, :] = fourth


def middle_kernel(
    z_ref, payload_ref, rate_ref, scaled_ref,
    state_ref, copies_ref, low_ref, high_ref, moments_ref, inverse_ref, rounded_ref,
):
    z_speed = z_ref[0]
    total = payload_ref[0:PAYLOAD, :]
    for part in range(1, PARTS):
        total = total + payload_ref[part * PAYLOAD : (part + 1) * PAYLOAD, :]
    group = [total[8 * t : 8 * t + 8] for t in range(4)]
    k = iota((8, CELLS), 0)
    mine = k < 5

    def spare(first, second):
        return jnp.where(
            k < 3, pltpu.roll(first, 3, 0), jnp.where(mine, pltpu.roll(second, 6, 0), 0.0)
        )

    wk = spare(group[0], group[1])
    small = spare(group[2], group[3])
    group = [jnp.where(mine, g, 0.0) for g in group]
    rate = rate_ref[...]
    share = rate / (1.0 + rate)
    inverse = inverse_of(small[:, 0:128])
    inverse_ref[...] = inverse
    coeffs = share * apply_small(inverse, 8, (1.0 + rate) * group[0])
    from_eq = [apply_small(small, 8 * t, coeffs) for t in range(GROUPS)]
    flux = group[1] + from_eq[1] + from_eq[2]
    for t, shift in ((3, from_below_y), (4, from_above_y), (5, from_below_z), (6, from_above_z)):
        flux = flux + (from_eq[t] - shift(from_eq[t]))
    moments_ref[...] = group[0] + from_eq[0] - flux
    high_ref[NODES // 2 :, :] = group[2] + from_eq[1]
    low_ref[NODES // 2 :, :] = group[3] + from_eq[2]
    for m in range(Q):
        rows = slice(Q * m, Q * m + Q)
        s = scaled_ref[rows, :] + equilibrium_rows(m, coeffs, z_speed)
        state_ref[rows, :] = s
        store_sides(m, s, low_ref, high_ref)
        rounded = s.astype(BF16)
        rounded_ref[rows, :] = rounded
        for part in range(PARTS):
            start = part * (NODES + EXTRA) + Q * m
            copies_ref[start : start + Q, :] = rounded
    pieces = jnp.concatenate([p.astype(F32) for p in split(wk, 3)], axis=0).astype(BF16)
    own = KERNEL_STEP * three_sum(jnp.dot(pieces, rounded_ref[...], preferred_element_type=F32))
    own = jnp.concatenate([p.astype(F32) for p in split(own, 2)], axis=0).astype(BF16)
    for part in range(PARTS):
        start = part * (NODES + EXTRA) + NODES
        copies_ref[start : start + EXTRA, :] = own


def last_kernel(
    cols_ref, z_ref, state_ref, rate_ref, tiles_ref, gathered_ref, above_ref, below_ref, moments_ref, inverse_ref,
    out_ref, acc_ref,
):
    z_speed = z_ref[0]
    kernel_product(gathered_ref, NODES + EXTRA, tiles_ref, cols_ref, acc_ref)
    total = moments_ref[...] + above_ref[NODES // 2 :, :] + below_ref[NODES // 2 :, :]
    for part in range(PARTS):
        start = part * (NODES + EXTRA) + NODES
        own = gathered_ref[start : start + EXTRA, :].astype(F32)
        total = total + (own[0:8] + own[8:16])
    rate = rate_ref[...]
    keep = 1.0 / (1.0 + rate)
    coeffs = rate * keep * apply_small(inverse_ref[...], 8, total)
    for m in range(Q):
        rows = slice(Q * m, Q * m + Q)
        half = slice(8 * m, 8 * m + 8)
        e = explicit_rows(
            m, state_ref[rows, :], below_ref[half, :], above_ref[half, :], acc_ref[rows, :], z_speed
        )
        new = keep * e + equilibrium_rows(m, coeffs, z_speed)
        for h in range(2):
            out_ref[pl.ds(2 * Q * m + h, Q, stride=2), :] = new[:, 128 * h : 128 * h + 128]


def call(kernel, scalars, arrays, outs, scratch=()):
    vmem = pl.BlockSpec(memory_space=pltpu.VMEM)
    smem = pl.BlockSpec(memory_space=pltpu.SMEM)
    return pl.pallas_call(
        kernel,
        out_shape=[jax.ShapeDtypeStruct(shape, kind) for shape, kind in outs],
        in_specs=[smem] * len(scalars) + [vmem] * len(arrays),
        out_specs=[vmem] * len(outs),
        scratch_shapes=[pltpu.VMEM(shape, kind) for shape, kind in scratch],
        compiler_params=pltpu.CompilerParams(vmem_limit_bytes=VMEM_BYTES),
    )(*scalars, *arrays)


def sides(low, high):
    count = lax.axis_size("gx")
    up = [(i, (i + 1) % count) for i in range(count)]
    down = [(target, source) for source, target in up]
    return lax.ppermute(low, "gx", down), lax.ppermute(high, "gx", up)


def spread(copies):
    return lax.all_to_all(copies, "vert", 0, 0, tiled=True)


def per_device(distribution, relax_rate, node_weight, kernel_tiles, tile_cols):
    state = distribution.reshape(2 * NODES, CELLS // 2)
    weight = node_weight.reshape(1, NODES)
    z_speed = speed_of(lax.axis_index("vert")).reshape(1)
    half = NODES // 2
    copies, low, high = call(
        prologue_kernel, [], [state],
        [((PARTS * NODES, CELLS), BF16), ((half, CELLS), F32), ((half, CELLS), F32)],
    )
    above, below = sides(low, high)
    gathered = spread(copies)
    scaled, payload = call(
        first_kernel, [tile_cols, z_speed],
        [state, relax_rate, weight, kernel_tiles, gathered, above, below],
        [((NODES, CELLS), F32), ((PARTS * PAYLOAD, CELLS), F32)],
        [((NODES, CELLS), F32), ((2 * PARTS, 8, TILE), F32)],
    )
    payload = spread(payload)
    state, copies, low, high, moments, inverse = call(
        middle_kernel, [z_speed], [payload, relax_rate, scaled],
        [
            ((NODES, CELLS), F32), ((PARTS * (NODES + EXTRA), CELLS), BF16), ((half + 8, CELLS), F32),
            ((half + 8, CELLS), F32), ((8, CELLS), F32), ((8, 128), F32),
        ],
        [((NODES, CELLS), BF16)],
    )
    above, below = sides(low, high)
    gathered = spread(copies)
    (out,) = call(
        last_kernel, [tile_cols, z_speed],
        [state, relax_rate, kernel_tiles, gathered, above, below, moments, inverse],
        [((2 * NODES, CELLS // 2), F32)],
        [((NODES, CELLS), F32)],
    )
    return out.reshape(distribution.shape)


def solution(mesh):
    placed = (
        P("vert", "gx", None),
        P("gx", None),
        P("vert"),
        P("vert", None, None),
        P("vert", None),
    )
    return jax.shard_map(
        per_device, mesh=mesh, in_specs=placed, out_specs=P("vert", "gx", None), check_vma=False
    )
```

time: 241 us -> 102 us (0.42)
  the two profiles are of different devices: /device:TPU:32 before, /device:TPU:448 now
where the time goes in v1:
time: 102 us; the launch traced here: 101 us
  waiting for transfers between devices  61.4 us (60%)
  blocking collectives  14.4 us (14%)
  starting transfers between devices  11.8 us (12%)
  local copies, waits for them, and re-layouts  8.25 us (8%)
  Pallas kernels  5.38 us (5%)
    all_to_all x2, waiting for transfers between devices, spread(): return lax.all_to_all(copies, 'vert', 0, 0, tiled=True)  53.1 us
    all_to_all x1, blocking collectives, spread(): return lax.all_to_all(copies, 'vert', 0, 0, tiled=True)  14.4 us
    all_to_all x2, starting transfers between devices, spread(): return lax.all_to_all(copies, 'vert', 0, 0, tiled=True)  10.8 us
    ppermute x4, waiting for transfers between devices, sides(): return (lax.ppermute(low, 'gx', down), lax.ppermute(high, 'gx', up))  8.25 us
    unnamed x30, local copies, waits for them, and re-layouts  8.25 us
    pallas_call x4, Pallas kernels, call(): pl.pallas_call(kernel, out_shape=[jax.ShapeDtypeStruct(shape, kind) for s...  5.38 us
  transfers between devices with their start and end apart: 6, of which 6 were waited for; matrix products, arithmetic and copies ran while one was open for 0% of the time, Pallas kernels for 0%

profile of v1, /device:TPU:448, one launch (start us, length us, event | category | flops | bytes accessed | tf_op | source)
XLA Modules:
  0.0 101.3 jit_solution(5814700659636376738)
XLA Ops:
  0.0 0.0 copy-start.3
  0.0 0.9 copy-done.3
  1.0 0.0 copy-start
  1.0 0.0 copy-start.4
  1.0 0.0 copy-start.5
  1.0 0.0 copy-start.9
  1.0 0.0 copy-start.13
  1.0 0.9 shard_map.55
  1.9 0.0 copy-start.2
  1.9 1.3 %copy-done.2 = bf16[4096,256]{1,0:T(8,128)(2,1)} copy-done((bf16[4096,256]{1,0:T(8,128)(2,1)}, bf16[4096,256]{1,0:T(8,128)(2,1)S(1)}, u32[]{:S(2)}) %copy-start.2) | copy-done | bytes 2097176
  3.2 7.0 %all-to-all-start = ((bf16[16,256,256]{2,1,0:T(8,128)(2,1)}), bf16[16,256,256]{2,1,0:T(8,128)(2,1)S(1)}, u32[]{:S(2)}, u32[]{:S(2)}) async-start(bf16[16,256,256]{2,1,0:T(8,128)(2,1)} %bitcast.13), calls=%async_computation | async-start | bytes 4194304 | tf_op jit(solution)/shard_map/all_to_all | solution.py:298
  10.2 0.2 collective-permute-start
  10.4 0.3 collective-permute-start.1
  10.8 2.5 %collective-permute-done.above_ref = f32[128,256]{1,0:T(8,128)S(1)} collective-permute-done((f32[128,256]{1,0:T(8,128)}, f32[128,256]{1,0:T(8,128)S(1)}, u32[]{:S(2)}, u32[]{:S(2)}) %collective-permute-start) | collective-permute-done | bytes 131104 | tf_op jit(solution)/shard_map/ppermute | solution.py:294
  13.3 1.6 %collective-permute-done.1.below_ref = f32[128,256]{1,0:T(8,128)S(1)} collective-permute-done((f32[128,256]{1,0:T(8,128)S(1)}, f32[128,256]{1,0:T(8,128)S(1)}, u32[]{:S(2)}, u32[]{:S(2)}) %collective-permute-start.1) | collective-permute-done | bytes 131104 | tf_op jit(solution)/shard_map/ppermute | solution.py:294
  14.8 27.1 %all-to-all-done = bf16[16,256,256]{2,1,0:T(8,128)(2,1)S(1)} async-done(((bf16[16,256,256]{2,1,0:T(8,128)(2,1)}), bf16[16,256,256]{2,1,0:T(8,128)(2,1)S(1)}, u32[]{:S(2)}, u32[]{:S(2)}) %all-to-all-start) | async-done | bytes 2097184 | tf_op jit(solution)/shard_map/all_to_all | solution.py:298
  41.9 0.0 copy-done
  41.9 0.0 copy-done.4
  41.9 0.0 copy-done.5
  41.9 0.0 copy-done.9
  41.9 0.0 copy-done.13
  41.9 1.4 %shard_map.56 = (f32[256,256]{1,0:T(8,128)S(1)}, f32[512,256]{1,0:T(8,128)S(1)}) custom-call(s32[2,12]{1,0:T(2,128)S(1)} %copy-done.9, f32[1]{0:T(128)} %bitcast.z_ref, f32[512,128]{1,0:T(8,128)S(1)} %bitcast.16, f32[1,256]{1,0:T(1,128)S(1)} %copy-done.5, f32[1,256]{1,0:T(1,128)S(1)} %bitcast.18, bf16[2,128,1536]{2,1,0:T(8,128)(2,1)S(1)} %copy-done, ...), custom_call_target="tpu_custom_call" | custom-call | tf_op jit(solution)/shard_map/pallas_call | solution.py:280
  43.4 14.4 %all_to_all.33 = f32[16,32,256]{2,1,0:T(8,128)S(1)} all-to-all(f32[16,32,256]{2,1,0:T(8,128)S(1)} %bitcast.17), channel_id=1, replica_groups=mesh['gx'=32,'vert'=16] {'vert'}, dimensions={0} | all-to-all | bytes 1048576 | tf_op jit(solution)/shard_map/all_to_all | solution.py:298
  57.8 1.3 %shard_map.57 = (f32[256,256]{1,0:T(8,128)S(1)}, bf16[4352,256]{1,0:T(8,128)(2,1)S(1)}, f32[136,256]{1,0:T(8,128)}, f32[136,256]{1,0:T(8,128)S(1)}, f32[8,256]{1,0:T(8,128)S(1)}, /*index=5*/f32[8,128]{1,0:T(8,128)S(1)}) custom-call(f32[1]{0:T(128)} %bitcast.z_ref, f32[512,256]{1,0:T(8,128)S(1)} %bitcast.14, f32[1,256]{1,0:T(1,128)S(1)} %copy-done.5, ...), custom_call_target="tpu_custom_call" | custom-call | tf_op jit(solution)/shard_map/pallas_call | solution.py:280
  59.2 0.0 copy-start.1
  59.2 1.4 %copy-done.1 = bf16[4352,256]{1,0:T(8,128)(2,1)} copy-done((bf16[4352,256]{1,0:T(8,128)(2,1)}, bf16[4352,256]{1,0:T(8,128)(2,1)S(1)}, u32[]{:S(2)}) %copy-start.1) | copy-done | bytes 2228248
  60.6 0.0 copy-start.7
  60.6 0.6 copy-done.7
  61.2 0.0 copy-start.11
  61.2 0.6 copy-done.11
  61.7 0.0 copy-start.14
  61.7 0.6 copy-done.14
  62.4 3.7 %all-to-all-start.2 = ((bf16[16,272,256]{2,1,0:T(8,128)(2,1)}), bf16[16,272,256]{2,1,0:T(8,128)(2,1)S(1)}, u32[]{:S(2)}, u32[]{:S(2)}) async-start(bf16[16,272,256]{2,1,0:T(8,128)(2,1)} %bitcast.12), calls=%async_computation.2 | async-start | bytes 4456448 | tf_op jit(solution)/shard_map/all_to_all | solution.py:298
  66.1 0.0 collective-permute-start.2
  66.1 0.5 collective-permute-start.3
  66.6 2.4 %collective-permute-done.2.above_ref = f32[136,256]{1,0:T(8,128)S(1)} collective-permute-done((f32[136,256]{1,0:T(8,128)}, f32[136,256]{1,0:T(8,128)S(1)}, u32[]{:S(2)}, u32[]{:S(2)}) %collective-permute-start.2) | collective-permute-done | bytes 139296 | tf_op jit(solution)/shard_map/ppermute | solution.py:294
  69.1 1.8 %collective-permute-done.3.below_ref = f32[136,256]{1,0:T(8,128)S(1)} collective-permute-done((f32[136,256]{1,0:T(8,128)}, f32[136,256]{1,0:T(8,128)S(1)}, u32[]{:S(2)}, u32[]{:S(2)}) %collective-permute-start.3) | collective-permute-done | bytes 139296 | tf_op jit(solution)/shard_map/ppermute | solution.py:294
  70.8 26.1 %all-to-all-done.2 = bf16[16,272,256]{2,1,0:T(8,128)(2,1)S(1)} async-done(((bf16[16,272,256]{2,1,0:T(8,128)(2,1)}), bf16[16,272,256]{2,1,0:T(8,128)(2,1)S(1)}, u32[]{:S(2)}, u32[]{:S(2)}) %all-to-all-start.2) | async-done | bytes 2228256 | tf_op jit(solution)/shard_map/all_to_all | solution.py:298
  96.9 0.0 copy-start.6
  96.9 0.7 copy-done.6
  97.6 0.0 copy-start.8
  97.6 0.7 copy-done.8
  98.3 0.0 copy-start.10
  98.3 0.7 copy-done.10
  99.0 0.0 copy-start.12
  99.0 0.7 copy-done.12
  99.6 1.7 %shard_map.58 = f32[512,128]{1,0:T(8,128)} custom-call(s32[2,12]{1,0:T(2,128)S(1)} %copy-done.10, f32[1]{0:T(128)} %bitcast.z_ref, f32[256,256]{1,0:T(8,128)S(1)} %get-tuple-element.21.state_ref, f32[1,256]{1,0:T(1,128)S(1)} %copy-done.6, bf16[2,128,1536]{2,1,0:T(8,128)(2,1)S(1)} %copy-done, bf16[4352,256]{1,0:T(8,128)(2,1)S(1)} %bitcast.10, ...), custom_call_target="tpu_custom_call" | custom-call | tf_op jit(solution)/shard_map/pallas_call | solution.py:280
Async XLA Ops:
  0.0 0.9 copy-start.3
  1.0 40.9 %copy-start = (bf16[2,128,1536]{2,1,0:T(8,128)(2,1)S(1)}, bf16[2,128,1536]{2,1,0:T(8,128)(2,1)}, u32[]{:S(2)}) copy-start(bf16[2,128,1536]{2,1,0:T(8,128)(2,1)} %tiles_ref.3) | copy-start | bytes 2359300
  1.0 40.9 %copy-start.4 = (f32[256,1,256]{2,1,0:T(1,128)S(1)}, f32[256,1,256]{2,1,0:T(1,128)}, u32[]{:S(2)}) copy-start(f32[256,1,256]{2,1,0:T(1,128)} %param.5) | copy-start | bytes 786436
  1.0 40.9 %copy-start.5 = (f32[1,256]{1,0:T(1,128)S(1)}, f32[1,256]{1,0:T(1,128)}, u32[]{:S(2)}) copy-start(f32[1,256]{1,0:T(1,128)} %rate_ref.5) | copy-start | bytes 3076
  1.0 41.0 %copy-start.9 = (s32[2,12]{1,0:T(2,128)S(1)}, s32[2,12]{1,0:T(2,128)}, u32[]{:S(2)}) copy-start(s32[2,12]{1,0:T(2,128)} %cols_ref.3) | copy-start | bytes 292
  1.0 41.0 %copy-start.13 = (f32[256]{0:T(256)S(1)}, f32[256]{0:T(256)}, u32[]{:S(2)}) copy-start(f32[256]{0:T(256)} %param.7) | copy-start | bytes 3076
  1.9 1.3 %copy-start.2 = (bf16[4096,256]{1,0:T(8,128)(2,1)}, bf16[4096,256]{1,0:T(8,128)(2,1)S(1)}, u32[]{:S(2)}) copy-start(bf16[4096,256]{1,0:T(8,128)(2,1)S(1)} %get-tuple-element.16) | copy-start | bytes 6291460
  3.2 38.7 %all-to-all-start = ((bf16[16,256,256]{2,1,0:T(8,128)(2,1)}), bf16[16,256,256]{2,1,0:T(8,128)(2,1)S(1)}, u32[]{:S(2)}, u32[]{:S(2)}) async-start(bf16[16,256,256]{2,1,0:T(8,128)(2,1)} %bitcast.13), calls=%async_computation | async-start | bytes 4194304 | tf_op jit(solution)/shard_map/all_to_all | solution.py:298
  10.2 3.0 %collective-permute-start = (f32[128,256]{1,0:T(8,128)}, f32[128,256]{1,0:T(8,128)S(1)}, u32[]{:S(2)}, u32[]{:S(2)}) collective-permute-start(f32[128,256]{1,0:T(8,128)} %get-tuple-element.17), channel_id=1, source_target_pairs={{16,0},{32,16},{48,32},{64,48},{80,64},{96,80},{112,96},{128,112},... | collective-permute-start | bytes 393224 | tf_op jit(solution)/shard_map/ppermute | solution.py:294
  10.4 4.4 %collective-permute-start.1 = (f32[128,256]{1,0:T(8,128)S(1)}, f32[128,256]{1,0:T(8,128)S(1)}, u32[]{:S(2)}, u32[]{:S(2)}) collective-permute-start(f32[128,256]{1,0:T(8,128)S(1)} %get-tuple-element.18), channel_id=1, source_target_pairs={{0,16},{16,32},{32,48},{48,64},{64,80},{80,96},{96,112},{112,128},... | collective-permute-start | bytes 393224 | tf_op jit(solution)/shard_map/ppermute | solution.py:294
  59.2 1.4 %copy-start.1 = (bf16[4352,256]{1,0:T(8,128)(2,1)}, bf16[4352,256]{1,0:T(8,128)(2,1)S(1)}, u32[]{:S(2)}) copy-start(bf16[4352,256]{1,0:T(8,128)(2,1)S(1)} %get-tuple-element.22) | copy-start | bytes 6684676
  60.6 0.6 copy-start.7
  61.2 0.6 copy-start.11
  61.7 0.6 copy-start.14
  62.4 34.5 %all-to-all-start.2 = ((bf16[16,272,256]{2,1,0:T(8,128)(2,1)}), bf16[16,272,256]{2,1,0:T(8,128)(2,1)S(1)}, u32[]{:S(2)}, u32[]{:S(2)}) async-start(bf16[16,272,256]{2,1,0:T(8,128)(2,1)} %bitcast.12), calls=%async_computation.2 | async-start | bytes 4456448 | tf_op jit(solution)/shard_map/all_to_all | solution.py:298
  66.1 2.9 %collective-permute-start.2 = (f32[136,256]{1,0:T(8,128)}, f32[136,256]{1,0:T(8,128)S(1)}, u32[]{:S(2)}, u32[]{:S(2)}) collective-permute-start(f32[136,256]{1,0:T(8,128)} %get-tuple-element.23), channel_id=1, source_target_pairs={{16,0},{32,16},{48,32},{64,48},{80,64},{96,80},{112,96},{128,112},... | collective-permute-start | bytes 417800 | tf_op jit(solution)/shard_map/ppermute | solution.py:294
  66.1 4.7 %collective-permute-start.3 = (f32[136,256]{1,0:T(8,128)}, f32[136,256]{1,0:T(8,128)S(1)}, u32[]{:S(2)}, u32[]{:S(2)}) collective-permute-start(f32[136,256]{1,0:T(8,128)} %copy-done.14), channel_id=1, source_target_pairs={{0,16},{16,32},{32,48},{48,64},{64,80},{80,96},{96,112},{112,128},... | collective-permute-start | bytes 417800 | tf_op jit(solution)/shard_map/ppermute | solution.py:294
  96.9 0.7 copy-start.6
  97.6 0.7 copy-start.8
  98.3 0.7 copy-start.10
  99.0 0.7 copy-start.12

commit v2 on v1

v2 whole, which is shorter than its diff:
```python
import functools

import jax
import jax.numpy as jnp
from jax import lax
from jax.experimental import pallas as pl
from jax.experimental.pallas import tpu as pltpu
from jax.sharding import PartitionSpec as P

Q = 16
TILE = 128
NB = 12
NZ = 4
CELLS = 256
NODES = 256
PARTS = 16
COURANT_SCALE = 0.3
KERNEL_STEP = 0.5
MIDDLE = (Q - 1) / 2.0
EXTRA = 16
PAYLOAD = 32
GROUPS = 7
F32 = jnp.float32
BF16 = jnp.bfloat16
HIGHEST = lax.Precision.HIGHEST
VMEM_BYTES = 24 * 1024 * 1024


def iota(shape, dim):
    return lax.broadcasted_iota(jnp.int32, shape, dim)


def speed_of(index):
    return (index.astype(F32) - MIDDLE) / MIDDLE


def from_below_y(a):
    return pltpu.roll(a, NZ, 1)


def from_above_y(a):
    return pltpu.roll(a, CELLS - NZ, 1)


def from_below_z(a):
    first = iota(a.shape, 1) % NZ == 0
    return jnp.where(first, pltpu.roll(a, CELLS - (NZ - 1), 1), pltpu.roll(a, 1, 1))


def from_above_z(a):
    last = iota(a.shape, 1) % NZ == NZ - 1
    return jnp.where(last, pltpu.roll(a, NZ - 1, 1), pltpu.roll(a, CELLS - 1, 1))


def split(a, pieces):
    out = []
    for _ in range(pieces):
        out.append(a.astype(BF16))
        a = a - out[-1].astype(F32)
    return out


def three_sum(a):
    return a[0:8] + a[8:16] + a[16:24]


def node_rows(z_speed):
    node = iota((8, NODES), 1)
    k = iota((8, NODES), 0)
    x, y = speed_of(node % Q), speed_of(node // Q)
    z = jnp.full((8, NODES), z_speed)
    invariants = jnp.where(k == 0, 1.0, 0.0)
    for row, value in ((1, x), (2, y), (3, z), (4, x * x + y * y + z * z)):
        invariants = jnp.where(k == row, value, invariants)
    factors = [None]
    for speed in (x, y, z):
        factors.append(COURANT_SCALE * jnp.maximum(speed, 0.0))
        factors.append(COURANT_SCALE * jnp.maximum(-speed, 0.0))
    return invariants, factors


def advected_rows(m, s, below, above, z_speed):
    row = iota((Q, CELLS), 0)
    lane = iota((Q, CELLS), 1)
    x_courant = COURANT_SCALE * jnp.abs(speed_of(row))
    y_courant = COURANT_SCALE * abs((m - MIDDLE) / MIDDLE)
    z_courant = COURANT_SCALE * jnp.abs(z_speed)
    up = z_speed > 0
    edge = jnp.where(up, 0, NZ - 1)
    near = pltpu.roll(s, jnp.where(up, 1, CELLS - 1), 1)
    far = pltpu.roll(s, jnp.where(up, CELLS - (NZ - 1), NZ - 1), 1)
    z_side = jnp.where(lane % NZ == edge, far, near)
    y_side = from_below_y(s) if m >= Q // 2 else from_above_y(s)
    x_side = jnp.concatenate([above, below], axis=0)
    flux = x_courant * (s - x_side) + y_courant * (s - y_side) + z_courant * (s - z_side)
    return s - flux


def equilibrium_rows(m, coeffs, z_speed):
    y = (m - MIDDLE) / MIDDLE
    x = speed_of(iota((Q, CELLS), 0))
    common = coeffs[0:1] + y * coeffs[2:3] + z_speed * coeffs[3:4]
    common = common + (y * y + z_speed * z_speed) * coeffs[4:5]
    return common + x * coeffs[1:2] + (x * x) * coeffs[4:5]


def apply_small(matrix, first, rows):
    total = matrix[:, first : first + 1] * rows[0:1]
    for k in range(1, 5):
        total = total + matrix[:, first + k : first + k + 1] * rows[k : k + 1]
    return total


def inverse_of(gram):
    row, lane = iota((8, 128), 0), iota((8, 128), 1)
    work = jnp.where((row < 5) & (lane < 5), gram, 0.0)
    work = jnp.where((lane == row + 8) | ((lane == row) & (row >= 5)), 1.0, work)
    for i in range(5):
        pivot = work[i : i + 1, :] / work[i : i + 1, i : i + 1]
        work = jnp.where(row == i, pivot, work - work[:, i : i + 1] * pivot)
    return work


def load_state(ref, m):
    halves = [ref[pl.ds(2 * Q * m + h, Q, stride=2), :] for h in range(2)]
    return jnp.concatenate(halves, axis=1)


def store_sides(m, s, low_ref, high_ref):
    low_ref[8 * m : 8 * m + 8, :] = s[0:8]
    high_ref[8 * m : 8 * m + 8, :] = s[8:16]


def in_parts(rows_per_part, start, block_ref, copies_ref, sems):
    count = block_ref.shape[0]
    copies = []
    for part in range(PARTS):
        at = part * rows_per_part + start
        copies.append(
            pltpu.make_async_copy(block_ref, copies_ref.at[at : at + count], sems.at[part])
        )
        copies[-1].start()
    return copies


def copies_kernel(state_ref, copies_ref, block_ref, sems):
    for m in range(Q):
        block_ref[Q * m : Q * m + Q, :] = load_state(state_ref, m).astype(BF16)
    for copy in in_parts(NODES, 0, block_ref, copies_ref, sems):
        copy.wait()


def prepare_kernel(
    cols_ref, z_ref, state_ref, weight_ref, tiles_ref,
    low_ref, high_ref, dense_ref, phi_ref, spare_ref, wk_ref,
):
    for m in range(Q):
        store_sides(m, load_state(state_ref, m), low_ref, high_ref)
    invariants, factors = node_rows(z_ref[0])
    base = weight_ref[...] * invariants
    phi = jnp.concatenate([base] + [base * f for f in factors[1:]], axis=0)
    phi_ref[...] = phi
    padded = jnp.concatenate([phi, jnp.zeros((TILE - 8 * GROUPS, NODES), F32)], axis=0)
    small = lax.dot_general(
        invariants, padded, (((1,), (1,)), ((), ())), precision=HIGHEST, preferred_element_type=F32
    )
    small = jnp.concatenate([small, jnp.zeros((8, CELLS - TILE), F32)], axis=1)
    dense_ref[...] = jnp.zeros_like(dense_ref)
    wk_ref[...] = jnp.zeros_like(wk_ref)
    pieces = jnp.concatenate([p.astype(F32) for p in split(base, 3)], axis=0).astype(BF16)
    for r in range(2):
        part = three_sum(
            jnp.dot(pieces[:, r * TILE : (r + 1) * TILE], tiles_ref[r], preferred_element_type=F32)
        )
        for j in range(NB):
            at = slice(j * TILE, (j + 1) * TILE)
            col = cols_ref[r, j]
            wk_ref[col] = wk_ref[col] + part[:, at]
            where = pl.ds(pl.multiple_of(col * TILE, TILE), TILE)
            dense_ref[r * TILE : (r + 1) * TILE, where] = tiles_ref[r, :, at]
    third = pltpu.roll(small, 5, 0)
    fourth = pltpu.roll(small, 2, 0)
    for part in range(PARTS):
        wk = jnp.concatenate([wk_ref[2 * part], wk_ref[2 * part + 1]], axis=1)
        start = part * PAYLOAD
        spare_ref[start : start + 8, :] = pltpu.roll(wk, 5, 0)
        spare_ref[start + 8 : start + 16, :] = pltpu.roll(wk, 2, 0)
        spare_ref[start + 16 : start + 24, :] = third
        spare_ref[start + 24 : start + 32, :] = fourth


def step_rows(rate, z_speed):
    keep = 1.0 / (1.0 + rate)
    rows = [KERNEL_STEP * keep, rate * keep, 1.0 + rate, jnp.full((1, CELLS), z_speed)]
    return jnp.concatenate(rows + [jnp.zeros((4, CELLS), F32)], axis=0)


def base_kernel(z_ref, state_ref, rate_ref, above_ref, below_ref, base_ref):
    z_speed = z_ref[0]
    rate = rate_ref[...]
    keep = 1.0 / (1.0 + rate)
    for m in range(Q):
        half = slice(8 * m, 8 * m + 8)
        s = load_state(state_ref, m)
        e = advected_rows(m, s, below_ref[half, :], above_ref[half, :], z_speed)
        base_ref[Q * m : Q * m + Q, :] = keep * e
    base_ref[NODES:, :] = step_rows(rate, z_speed)


def first_kernel(dense_ref, gathered_ref, base_ref, phi_ref, spare_ref, scaled_ref, payload_ref):
    term = jnp.dot(dense_ref[...], gathered_ref[...], preferred_element_type=F32)
    scaled = base_ref[0:NODES, :] + base_ref[NODES : NODES + 1, :] * term
    scaled_ref[0:NODES, :] = scaled
    scaled_ref[NODES:, :] = base_ref[NODES:, :]
    moments = jnp.dot(phi_ref[...], scaled, precision=HIGHEST, preferred_element_type=F32)
    group = [moments[8 * t : 8 * t + 8] for t in range(GROUPS)]
    flux = group[1] + group[2]
    for t, shift in ((3, from_below_y), (4, from_above_y), (5, from_below_z), (6, from_above_z)):
        flux = flux + (group[t] - shift(group[t]))
    mine = iota((8, CELLS), 0) < 5
    rows = (group[0], flux, group[1], group[2])
    for part in range(PARTS):
        for t in range(4):
            at = slice(part * PAYLOAD + 8 * t, part * PAYLOAD + 8 * t + 8)
            payload_ref[at, :] = jnp.where(mine, rows[t], spare_ref[at, :])


def totals_of(payload_ref, scaled_ref):
    total = payload_ref[0:PAYLOAD, :]
    for part in range(1, PARTS):
        total = total + payload_ref[part * PAYLOAD : (part + 1) * PAYLOAD, :]
    group = [total[8 * t : 8 * t + 8] for t in range(4)]
    k = iota((8, CELLS), 0)
    mine = k < 5

    def spare(first, second):
        return jnp.where(
            k < 3, pltpu.roll(first, 3, 0), jnp.where(mine, pltpu.roll(second, 6, 0), 0.0)
        )

    wk = spare(group[0], group[1])
    small = spare(group[2], group[3])
    group = [jnp.where(mine, g, 0.0) for g in group]
    inverse = inverse_of(small[:, 0:128])
    rows = scaled_ref[NODES:, :]
    coeffs = rows[1:2] * apply_small(inverse, 8, rows[2:3] * group[0])
    return group, wk, small, inverse, coeffs


def middle_kernel(payload_ref, scaled_ref, copies_ref, block_ref, own_ref, sems, own_sems):
    group, wk, small, inverse, coeffs = totals_of(payload_ref, scaled_ref)
    z_speed = scaled_ref[NODES + 3 : NODES + 4, :]
    for m in range(Q):
        rows = slice(Q * m, Q * m + Q)
        s = scaled_ref[rows, :] + equilibrium_rows(m, coeffs, z_speed)
        block_ref[rows, :] = s.astype(BF16)
    copies = in_parts(NODES + EXTRA, 0, block_ref, copies_ref, sems)
    pieces = jnp.concatenate([p.astype(F32) for p in split(wk, 3)], axis=0).astype(BF16)
    own = KERNEL_STEP * three_sum(jnp.dot(pieces, block_ref[...], preferred_element_type=F32))
    own_ref[...] = jnp.concatenate([p.astype(F32) for p in split(own, 2)], axis=0).astype(BF16)
    copies += in_parts(NODES + EXTRA, NODES, own_ref, copies_ref, own_sems)
    for copy in copies:
        copy.wait()


def state_kernel(payload_ref, scaled_ref, state_ref, low_ref, high_ref):
    group, wk, small, inverse, coeffs = totals_of(payload_ref, scaled_ref)
    z_speed = scaled_ref[NODES + 3 : NODES + 4, :]
    from_eq = [apply_small(small, 8 * t, coeffs) for t in range(GROUPS)]
    flux = group[1] + from_eq[1] + from_eq[2]
    for t, shift in ((3, from_below_y), (4, from_above_y), (5, from_below_z), (6, from_above_z)):
        flux = flux + (from_eq[t] - shift(from_eq[t]))
    high_ref[NODES // 2 :, :] = group[2] + from_eq[1]
    low_ref[NODES // 2 :, :] = group[3] + from_eq[2]
    for m in range(Q):
        rows = slice(Q * m, Q * m + Q)
        s = scaled_ref[rows, :] + equilibrium_rows(m, coeffs, z_speed)
        state_ref[rows, :] = s
        store_sides(m, s, low_ref, high_ref)
    state_ref[NODES : NODES + 8, :] = group[0] + from_eq[0] - flux
    state_ref[NODES + 8 :, :] = jnp.concatenate([inverse, inverse], axis=1)


def second_base_kernel(z_ref, state_ref, rate_ref, above_ref, below_ref, base_ref):
    z_speed = z_ref[0]
    rate = rate_ref[...]
    keep = 1.0 / (1.0 + rate)
    for m in range(Q):
        rows = slice(Q * m, Q * m + Q)
        half = slice(8 * m, 8 * m + 8)
        e = advected_rows(m, state_ref[rows, :], below_ref[half, :], above_ref[half, :], z_speed)
        base_ref[rows, :] = keep * e
    sides_part = above_ref[NODES // 2 :, :] + below_ref[NODES // 2 :, :]
    base_ref[NODES : NODES + 8, :] = state_ref[NODES : NODES + 8, :] + sides_part
    base_ref[NODES + 8 : NODES + 16, :] = state_ref[NODES + 8 : NODES + 16, :]
    base_ref[NODES + 16 :, :] = step_rows(rate, z_speed)


def last_kernel(dense_ref, gathered_ref, base_ref, out_ref, term_ref):
    stride = NODES + EXTRA
    term_ref[...] = jnp.dot(
        dense_ref[...],
        jnp.concatenate([gathered_ref[p * stride : p * stride + NODES, :] for p in range(PARTS)], axis=0),
        preferred_element_type=F32,
    )
    total = base_ref[NODES : NODES + 8, :]
    for part in range(PARTS):
        own = gathered_ref[part * stride + NODES : (part + 1) * stride, :].astype(F32)
        total = total + (own[0:8] + own[8:16])
    rows = base_ref[NODES + 16 :, :]
    coeffs = rows[1:2] * apply_small(base_ref[NODES + 8 : NODES + 16, 0:128], 8, total)
    for m in range(Q):
        at = slice(Q * m, Q * m + Q)
        new = base_ref[at, :] + rows[0:1] * term_ref[at, :] + equilibrium_rows(m, coeffs, rows[3:4])
        for h in range(2):
            out_ref[pl.ds(2 * Q * m + h, Q, stride=2), :] = new[:, 128 * h : 128 * h + 128]


VMEM = pl.BlockSpec(memory_space=pltpu.VMEM)
SMEM = pl.BlockSpec(memory_space=pltpu.SMEM)
ANY = pl.BlockSpec(memory_space=pl.ANY)


def call(kernel, scalars, arrays, outs, scratch=(), in_hbm=False):
    make = pltpu.HBM if in_hbm else jax.ShapeDtypeStruct
    return pl.pallas_call(
        kernel,
        out_shape=[make(shape, kind) for shape, kind in outs],
        in_specs=[SMEM] * len(scalars) + [VMEM] * len(arrays),
        out_specs=[ANY if in_hbm else VMEM] * len(outs),
        scratch_shapes=list(scratch),
        compiler_params=pltpu.CompilerParams(vmem_limit_bytes=VMEM_BYTES),
    )(*scalars, *arrays)


def sides(low, high):
    count = lax.axis_size("gx")
    up = [(i, (i + 1) % count) for i in range(count)]
    down = [(target, source) for source, target in up]
    return lax.ppermute(low, "gx", down), lax.ppermute(high, "gx", up)


def spread(copies):
    return lax.all_to_all(copies, "vert", 0, 0, tiled=True)


def per_device(distribution, relax_rate, node_weight, kernel_tiles, tile_cols):
    state = distribution.reshape(2 * NODES, CELLS // 2)
    weight = node_weight.reshape(1, NODES)
    z_speed = speed_of(lax.axis_index("vert")).reshape(1)
    half = NODES // 2
    block = pltpu.VMEM((NODES, CELLS), BF16)
    sems = pltpu.SemaphoreType.DMA((PARTS,))
    (copies,) = call(
        copies_kernel, [], [state], [((PARTS * NODES, CELLS), BF16)], [block, sems], True
    )
    gathered = spread(copies)
    low, high, dense, phi, spare = call(
        prepare_kernel, [tile_cols, z_speed], [state, weight, kernel_tiles],
        [
            ((half, CELLS), F32), ((half, CELLS), F32), ((NODES, PARTS * NODES), BF16),
            ((8 * GROUPS, NODES), F32), ((PARTS * PAYLOAD, CELLS), F32),
        ],
        [pltpu.VMEM((2 * PARTS, 8, TILE), F32)],
    )
    above, below = sides(low, high)
    (base,) = call(
        base_kernel, [z_speed], [state, relax_rate, above, below], [((NODES + 8, CELLS), F32)]
    )
    scaled, payload = call(
        first_kernel, [], [dense, gathered, base, phi, spare],
        [((NODES + 8, CELLS), F32), ((PARTS * PAYLOAD, CELLS), F32)],
    )
    payload = spread(payload)
    (copies,) = call(
        middle_kernel, [], [payload, scaled], [((PARTS * (NODES + EXTRA), CELLS), BF16)],
        [block, pltpu.VMEM((EXTRA, CELLS), BF16), sems, sems], True,
    )
    gathered = spread(copies)
    state, low, high = call(
        state_kernel, [], [payload, scaled],
        [((NODES + 16, CELLS), F32), ((half + 8, CELLS), F32), ((half + 8, CELLS), F32)],
    )
    above, below = sides(low, high)
    (base,) = call(
        second_base_kernel, [z_speed], [state, relax_rate, above, below],
        [((NODES + 24, CELLS), F32)],
    )
    (out,) = call(
        last_kernel, [], [dense, gathered, base], [((2 * NODES, CELLS // 2), F32)],
        [pltpu.VMEM((NODES, CELLS), F32)],
    )
    return out.reshape(distribution.shape)


def solution(mesh):
    placed = (
        P("vert", "gx", None),
        P("gx", None),
        P("vert"),
        P("vert", None, None),
        P("vert", None),
    )
    return jax.shard_map(
        per_device, mesh=mesh, in_specs=placed, out_specs=P("vert", "gx", None), check_vma=False
    )
```

time: 102 us -> 99.9 us (0.979)
  the two profiles are of different devices: /device:TPU:448 before, /device:TPU:96 now
where the time goes in v2:
time: 99.9 us; the launch traced here: 99.6 us
  waiting for transfers between devices  58.3 us (58%)
  blocking collectives  14.5 us (15%)
  starting transfers between devices  12 us (12%)
  Pallas kernels  10.2 us (10%)
  local copies, waits for them, and re-layouts  4.4 us (4%)
    all_to_all x2, waiting for transfers between devices, spread(): return lax.all_to_all(copies, 'vert', 0, 0, tiled=True)  50.5 us
    all_to_all x1, blocking collectives, spread(): return lax.all_to_all(copies, 'vert', 0, 0, tiled=True)  14.5 us
    all_to_all x2, starting transfers between devices, spread(): return lax.all_to_all(copies, 'vert', 0, 0, tiled=True)  11 us
    pallas_call x8, Pallas kernels, call(): pl.pallas_call(kernel, out_shape=[make(shape, kind) for shape, kind in ou...  10.2 us
    ppermute x4, waiting for transfers between devices, sides(): return (lax.ppermute(low, 'gx', down), lax.ppermute(high, 'gx', up))  7.88 us
    unnamed x20, local copies, waits for them, and re-layouts  4.4 us
  transfers between devices with their start and end apart: 6, of which 6 were waited for; matrix products, arithmetic and copies ran while one was open for 0% of the time, Pallas kernels for 2%

profile of v2, /device:TPU:96, one launch (start us, length us, event | category | flops | bytes accessed | tf_op | source)
XLA Modules:
  0.0 99.6 jit_solution(13700856667863299710)
XLA Ops:
  0.0 0.0 copy-start.2
  0.0 0.9 copy-done.2
  1.0 1.5 %shard_map.56 = bf16[4096,256]{1,0:T(8,128)(2,1)} custom-call(f32[512,128]{1,0:T(8,128)S(1)} %bitcast.13), custom_call_target="tpu_custom_call" | custom-call | tf_op jit(solution)/shard_map/pallas_call | solution.py:326
  2.5 0.0 copy-start.3
  2.5 0.0 copy-start.4
  2.5 0.0 copy-start.8
  2.5 0.0 copy-start.9
  2.5 0.0 copy-start.7
  2.5 7.2 %all-to-all-start = ((bf16[16,256,256]{2,1,0:T(8,128)(2,1)}), bf16[16,256,256]{2,1,0:T(8,128)(2,1)}, u32[]{:S(2)}, u32[]{:S(2)}) async-start(bf16[16,256,256]{2,1,0:T(8,128)(2,1)} %bitcast.19), calls=%async_computation | async-start | bytes 4194304 | tf_op jit(solution)/shard_map/all_to_all | solution.py:344
  9.8 0.0 copy-done.3
  9.8 0.0 copy-done.4
  9.8 0.0 copy-done.8
  9.8 0.0 copy-done.9
  9.8 1.1 %shard_map.55 = (f32[128,256]{1,0:T(8,128)S(1)}, f32[128,256]{1,0:T(8,128)S(1)}, bf16[256,4096]{1,0:T(8,128)(2,1)S(1)}, f32[56,256]{1,0:T(8,128)S(1)}, f32[512,256]{1,0:T(8,128)S(1)}) custom-call(s32[2,12]{1,0:T(2,128)S(1)} %copy-done.8, f32[1]{0:T(128)} %bitcast.z_ref, f32[512,128]{1,0:T(8,128)S(1)} %bitcast.14, f32[1,256]{1,0:T(1,128)S(1)} %bitcast.17, ...), custom_call_target="tpu_custom_call" | custom-call | tf_op jit(solution)/shard_map/pallas_call | solution.py:326
  10.9 0.0 copy-start.5
  10.9 0.8 copy-done.5
  11.7 0.0 copy-start
  11.7 0.0 collective-permute-start
  11.7 0.5 collective-permute-start.1
  12.2 2.0 %collective-permute-done.above_ref = f32[128,256]{1,0:T(8,128)S(1)} collective-permute-done((f32[128,256]{1,0:T(8,128)S(1)}, f32[128,256]{1,0:T(8,128)S(1)}, u32[]{:S(2)}, u32[]{:S(2)}) %collective-permute-start) | collective-permute-done | bytes 131104 | tf_op jit(solution)/shard_map/ppermute | solution.py:340
  14.2 1.9 %collective-permute-done.1.below_ref = f32[128,256]{1,0:T(8,128)S(1)} collective-permute-done((f32[128,256]{1,0:T(8,128)S(1)}, f32[128,256]{1,0:T(8,128)S(1)}, u32[]{:S(2)}, u32[]{:S(2)}) %collective-permute-start.1) | collective-permute-done | bytes 131104 | tf_op jit(solution)/shard_map/ppermute | solution.py:340
  16.1 0.0 copy-done.7
  16.1 0.3 shard_map.57.base_ref
  16.4 25.1 %all-to-all-done = bf16[16,256,256]{2,1,0:T(8,128)(2,1)} async-done(((bf16[16,256,256]{2,1,0:T(8,128)(2,1)}), bf16[16,256,256]{2,1,0:T(8,128)(2,1)}, u32[]{:S(2)}, u32[]{:S(2)}) %all-to-all-start) | async-done | bytes 2097184 | tf_op jit(solution)/shard_map/all_to_all | solution.py:344
  41.5 0.0 copy-start.6
  41.5 1.0 %copy-done.6 = f32[512,256]{1,0:T(8,128)S(1)} copy-done((f32[512,256]{1,0:T(8,128)S(1)}, f32[512,256]{1,0:T(8,128)}, u32[]{:S(2)}) %copy-start.6) | copy-done | bytes 524312
  42.5 2.8 %shard_map.58 = (f32[264,256]{1,0:T(8,128)S(1)}, f32[512,256]{1,0:T(8,128)S(1)}) custom-call(bf16[256,4096]{1,0:T(8,128)(2,1)S(1)} %get-tuple-element.15.dense_ref, bf16[4096,256]{1,0:T(8,128)(2,1)} %bitcast.4.gathered_ref, f32[264,256]{1,0:T(8,128)S(1)} %shard_map.57.base_ref, f32[56,256]{1,0:T(8,128)S(1)} %get-tuple-element.18.phi_ref, ...), custom_call_target="tpu_custom_call" | custom-call | tf_op jit(solution)/shard_map/pallas_call | solution.py:326
  45.3 0.0 copy-done
  45.4 14.5 %all_to_all.33 = f32[16,32,256]{2,1,0:T(8,128)S(1)} all-to-all(f32[16,32,256]{2,1,0:T(8,128)S(1)} %bitcast.16), channel_id=1, replica_groups=mesh['gx'=32,'vert'=16] {'vert'}, dimensions={0} | all-to-all | bytes 1048576 | tf_op jit(solution)/shard_map/all_to_all | solution.py:344
  59.8 2.2 %shard_map.59 = bf16[4352,256]{1,0:T(8,128)(2,1)} custom-call(f32[512,256]{1,0:T(8,128)S(1)} %bitcast.11, f32[264,256]{1,0:T(8,128)S(1)} %get-tuple-element.21.scaled_ref), custom_call_target="tpu_custom_call" | custom-call | tf_op jit(solution)/shard_map/pallas_call | solution.py:326
  62.0 3.7 %all-to-all-start.2 = ((bf16[16,272,256]{2,1,0:T(8,128)(2,1)}), bf16[16,272,256]{2,1,0:T(8,128)(2,1)S(1)}, u32[]{:S(2)}, u32[]{:S(2)}) async-start(bf16[16,272,256]{2,1,0:T(8,128)(2,1)} %bitcast.18), calls=%async_computation.2 | async-start | bytes 4456448 | tf_op jit(solution)/shard_map/all_to_all | solution.py:344
  65.8 0.6 shard_map.60
  66.4 0.0 collective-permute-start.2
  66.4 0.5 collective-permute-start.3
  66.9 2.1 %collective-permute-done.2.above_ref = f32[136,256]{1,0:T(8,128)S(1)} collective-permute-done((f32[136,256]{1,0:T(8,128)S(1)}, f32[136,256]{1,0:T(8,128)S(1)}, u32[]{:S(2)}, u32[]{:S(2)}) %collective-permute-start.2) | collective-permute-done | bytes 139296 | tf_op jit(solution)/shard_map/ppermute | solution.py:340
  69.0 1.9 %collective-permute-done.3.below_ref = f32[136,256]{1,0:T(8,128)S(1)} collective-permute-done((f32[136,256]{1,0:T(8,128)S(1)}, f32[136,256]{1,0:T(8,128)S(1)}, u32[]{:S(2)}, u32[]{:S(2)}) %collective-permute-start.3) | collective-permute-done | bytes 139296 | tf_op jit(solution)/shard_map/ppermute | solution.py:340
  70.9 0.3 shard_map.61.base_ref
  71.2 25.3 %all-to-all-done.2 = bf16[16,272,256]{2,1,0:T(8,128)(2,1)S(1)} async-done(((bf16[16,272,256]{2,1,0:T(8,128)(2,1)}), bf16[16,272,256]{2,1,0:T(8,128)(2,1)S(1)}, u32[]{:S(2)}, u32[]{:S(2)}) %all-to-all-start.2) | async-done | bytes 2228256 | tf_op jit(solution)/shard_map/all_to_all | solution.py:344
  96.6 0.0 copy-start.1
  96.6 1.6 %copy-done.1 = bf16[256,4096]{1,0:T(8,128)(2,1)S(1)} copy-done((bf16[256,4096]{1,0:T(8,128)(2,1)S(1)}, bf16[256,4096]{1,0:T(8,128)(2,1)}, u32[]{:S(2)}) %copy-start.1) | copy-done | bytes 2097176
  98.1 1.4 %shard_map.62 = f32[512,128]{1,0:T(8,128)} custom-call(bf16[256,4096]{1,0:T(8,128)(2,1)S(1)} %copy-done.1, bf16[4352,256]{1,0:T(8,128)(2,1)S(1)} %bitcast.10, f32[280,256]{1,0:T(8,128)S(1)} %shard_map.61.base_ref), custom_call_target="tpu_custom_call" | custom-call | tf_op jit(solution)/shard_map/pallas_call | solution.py:326
Async XLA Ops:
  0.0 0.9 copy-start.2
  2.5 7.3 %copy-start.3 = (f32[256,1,256]{2,1,0:T(1,128)S(1)}, f32[256,1,256]{2,1,0:T(1,128)}, u32[]{:S(2)}) copy-start(f32[256,1,256]{2,1,0:T(1,128)} %param.5) | copy-start | bytes 786436
  2.5 7.3 %copy-start.4 = (bf16[2,128,1536]{2,1,0:T(8,128)(2,1)S(1)}, bf16[2,128,1536]{2,1,0:T(8,128)(2,1)}, u32[]{:S(2)}) copy-start(bf16[2,128,1536]{2,1,0:T(8,128)(2,1)} %tiles_ref.1) | copy-start | bytes 2359300
  2.5 7.3 %copy-start.8 = (s32[2,12]{1,0:T(2,128)S(1)}, s32[2,12]{1,0:T(2,128)}, u32[]{:S(2)}) copy-start(s32[2,12]{1,0:T(2,128)} %cols_ref.1) | copy-start | bytes 292
  2.5 7.3 %copy-start.9 = (f32[256]{0:T(256)S(1)}, f32[256]{0:T(256)}, u32[]{:S(2)}) copy-start(f32[256]{0:T(256)} %param.7) | copy-start | bytes 3076
  2.5 13.6 %copy-start.7 = (f32[1,256]{1,0:T(1,128)S(1)}, f32[1,256]{1,0:T(1,128)}, u32[]{:S(2)}) copy-start(f32[1,256]{1,0:T(1,128)} %rate_ref.3) | copy-start | bytes 3076
  2.5 38.9 %all-to-all-start = ((bf16[16,256,256]{2,1,0:T(8,128)(2,1)}), bf16[16,256,256]{2,1,0:T(8,128)(2,1)}, u32[]{:S(2)}, u32[]{:S(2)}) async-start(bf16[16,256,256]{2,1,0:T(8,128)(2,1)} %bitcast.19), calls=%async_computation | async-start | bytes 4194304 | tf_op jit(solution)/shard_map/all_to_all | solution.py:344
  10.9 0.8 copy-start.5
  11.7 33.7 %copy-start = (bf16[256,4096]{1,0:T(8,128)(2,1)}, bf16[256,4096]{1,0:T(8,128)(2,1)S(1)}, u32[]{:S(2)}) copy-start(bf16[256,4096]{1,0:T(8,128)(2,1)S(1)} %get-tuple-element.15.dense_ref) | copy-start | bytes 6291460
  11.7 2.5 %collective-permute-start = (f32[128,256]{1,0:T(8,128)S(1)}, f32[128,256]{1,0:T(8,128)S(1)}, u32[]{:S(2)}, u32[]{:S(2)}) collective-permute-start(f32[128,256]{1,0:T(8,128)S(1)} %get-tuple-element.16), channel_id=1, source_target_pairs={{16,0},{32,16},{48,32},{64,48},{80,64},{96,80},{112,96},{128,112},... | collective-permute-start | bytes 393224 | tf_op jit(solution)/shard_map/ppermute | solution.py:340
  11.7 4.4 %collective-permute-start.1 = (f32[128,256]{1,0:T(8,128)S(1)}, f32[128,256]{1,0:T(8,128)S(1)}, u32[]{:S(2)}, u32[]{:S(2)}) collective-permute-start(f32[128,256]{1,0:T(8,128)S(1)} %get-tuple-element.17), channel_id=1, source_target_pairs={{0,16},{16,32},{32,48},{48,64},{64,80},{80,96},{96,112},{112,128},... | collective-permute-start | bytes 393224 | tf_op jit(solution)/shard_map/ppermute | solution.py:340
  41.5 1.0 %copy-start.6 = (f32[512,256]{1,0:T(8,128)S(1)}, f32[512,256]{1,0:T(8,128)}, u32[]{:S(2)}) copy-start(f32[512,256]{1,0:T(8,128)} %copy-done.5) | copy-start | bytes 1572868
  62.0 34.5 %all-to-all-start.2 = ((bf16[16,272,256]{2,1,0:T(8,128)(2,1)}), bf16[16,272,256]{2,1,0:T(8,128)(2,1)S(1)}, u32[]{:S(2)}, u32[]{:S(2)}) async-start(bf16[16,272,256]{2,1,0:T(8,128)(2,1)} %bitcast.18), calls=%async_computation.2 | async-start | bytes 4456448 | tf_op jit(solution)/shard_map/all_to_all | solution.py:344
  66.4 2.6 %collective-permute-start.2 = (f32[136,256]{1,0:T(8,128)S(1)}, f32[136,256]{1,0:T(8,128)S(1)}, u32[]{:S(2)}, u32[]{:S(2)}) collective-permute-start(f32[136,256]{1,0:T(8,128)S(1)} %get-tuple-element.23), channel_id=1, source_target_pairs={{16,0},{32,16},{48,32},{64,48},{80,64},{96,80},{112,96},{128,112},... | collective-permute-start | bytes 417800 | tf_op jit(solution)/shard_map/ppermute | solution.py:340
  66.4 4.5 %collective-permute-start.3 = (f32[136,256]{1,0:T(8,128)S(1)}, f32[136,256]{1,0:T(8,128)S(1)}, u32[]{:S(2)}, u32[]{:S(2)}) collective-permute-start(f32[136,256]{1,0:T(8,128)S(1)} %get-tuple-element.24), channel_id=1, source_target_pairs={{0,16},{16,32},{32,48},{48,64},{64,80},{80,96},{96,112},{112,128},... | collective-permute-start | bytes 417800 | tf_op jit(solution)/shard_map/ppermute | solution.py:340
  96.6 1.6 %copy-start.1 = (bf16[256,4096]{1,0:T(8,128)(2,1)S(1)}, bf16[256,4096]{1,0:T(8,128)(2,1)}, u32[]{:S(2)}) copy-start(bf16[256,4096]{1,0:T(8,128)(2,1)} %copy-done) | copy-start | bytes 6291460

commit v3 on v2

--- a/solution.py
+++ b/solution.py
@@ -18,7 +18,8 @@
 KERNEL_STEP = 0.5
 MIDDLE = (Q - 1) / 2.0
 EXTRA = 16
-PAYLOAD = 32
+PAYLOAD = 24
+PIECES = 2
 GROUPS = 7
 F32 = jnp.float32
 BF16 = jnp.bfloat16
@@ -131,40 +132,53 @@
     high_ref[8 * m : 8 * m + 8, :] = s[8:16]
 
 
-def in_parts(rows_per_part, start, block_ref, copies_ref, sems):
-    count = block_ref.shape[0]
+def in_parts(rows_per_part, start, piece, pieces, block_ref, copies_ref, sems):
+    count = block_ref.shape[0] // pieces
     copies = []
     for part in range(PARTS):
-        at = part * rows_per_part + start
+        at = part * rows_per_part + start + piece * count
         copies.append(
-            pltpu.make_async_copy(block_ref, copies_ref.at[at : at + count], sems.at[part])
+            pltpu.make_async_copy(
+                block_ref.at[piece * count : (piece + 1) * count],
+                copies_ref.at[at : at + count],
+                sems.at[piece, part],
+            )
         )
         copies[-1].start()
     return copies
 
 
-def copies_kernel(state_ref, copies_ref, block_ref, sems):
-    for m in range(Q):
-        block_ref[Q * m : Q * m + Q, :] = load_state(state_ref, m).astype(BF16)
-    for copy in in_parts(NODES, 0, block_ref, copies_ref, sems):
+def copies_kernel(state_ref, copies_ref, held_ref, block_ref, in_sems, sems):
+    pieces = []
+    for i in range(PIECES):
+        at = pl.ds(i * 2 * NODES // PIECES, 2 * NODES // PIECES)
+        pieces.append(pltpu.make_async_copy(state_ref.at[at], held_ref.at[at], in_sems.at[i]))
+        pieces[-1].start()
+    copies = []
+    for i in range(PIECES):
+        pieces[i].wait()
+        for m in range(i * Q // PIECES, (i + 1) * Q // PIECES):
+            block_ref[Q * m : Q * m + Q, :] = load_state(held_ref, m).astype(BF16)
+        copies += in_parts(NODES, 0, i, PIECES, block_ref, copies_ref, sems)
+    for copy in copies:
         copy.wait()
 
 
 def prepare_kernel(
     cols_ref, z_ref, state_ref, weight_ref, tiles_ref,
-    low_ref, high_ref, dense_ref, phi_ref, spare_ref, wk_ref,
+    low_ref, high_ref, dense_ref, phi_ref, wk_ref,
 ):
     for m in range(Q):
         store_sides(m, load_state(state_ref, m), low_ref, high_ref)
     invariants, factors = node_rows(z_ref[0])
     base = weight_ref[...] * invariants
     phi = jnp.concatenate([base] + [base * f for f in factors[1:]], axis=0)
-    phi_ref[...] = phi
+    phi_ref[0 : 8 * GROUPS, :] = phi
     padded = jnp.concatenate([phi, jnp.zeros((TILE - 8 * GROUPS, NODES), F32)], axis=0)
     small = lax.dot_general(
         invariants, padded, (((1,), (1,)), ((), ())), precision=HIGHEST, preferred_element_type=F32
     )
-    small = jnp.concatenate([small, jnp.zeros((8, CELLS - TILE), F32)], axis=1)
+    phi_ref[8 * GROUPS :, :] = jnp.concatenate([small, jnp.zeros((8, CELLS - TILE), F32)], axis=1)
     dense_ref[...] = jnp.zeros_like(dense_ref)
     wk_ref[...] = jnp.zeros_like(wk_ref)
     pieces = jnp.concatenate([p.astype(F32) for p in split(base, 3)], axis=0).astype(BF16)
@@ -178,15 +192,6 @@
             wk_ref[col] = wk_ref[col] + part[:, at]
             where = pl.ds(pl.multiple_of(col * TILE, TILE), TILE)
             dense_ref[r * TILE : (r + 1) * TILE, where] = tiles_ref[r, :, at]
-    third = pltpu.roll(small, 5, 0)
-    fourth = pltpu.roll(small, 2, 0)
-    for part in range(PARTS):
-        wk = jnp.concatenate([wk_ref[2 * part], wk_ref[2 * part + 1]], axis=1)
-        start = part * PAYLOAD
-        spare_ref[start : start + 8, :] = pltpu.roll(wk, 5, 0)
-        spare_ref[start + 8 : start + 16, :] = pltpu.roll(wk, 2, 0)
-        spare_ref[start + 16 : start + 24, :] = third
-        spare_ref[start + 24 : start + 32, :] = fourth
 
 
 def step_rows(rate, z_speed):
@@ -207,58 +212,87 @@
     base_ref[NODES:, :] = step_rows(rate, z_speed)
 
 
-def first_kernel(dense_ref, gathered_ref, base_ref, phi_ref, spare_ref, scaled_ref, payload_ref):
-    term = jnp.dot(dense_ref[...], gathered_ref[...], preferred_element_type=F32)
+def fetch(gathered_ref, stride, held_ref, sems):
+    copies = []
+    for part in range(PARTS):
+        at = slice(part * NODES, (part + 1) * NODES)
+        source = gathered_ref.at[part * stride : part * stride + NODES]
+        copies.append(pltpu.make_async_copy(source, held_ref.at[at], sems.at[part]))
+        copies[-1].start()
+    return copies
+
+
+def product(dense_ref, held_ref, copies):
+    total = None
+    for i in range(4):
+        for copy in copies[4 * i : 4 * i + 4]:
+            copy.wait()
+        at = slice(4 * i * NODES, 4 * (i + 1) * NODES)
+        part = jnp.dot(dense_ref[:, at], held_ref[at, :], preferred_element_type=F32)
+        total = part if total is None else total + part
+    return total
+
+
+def first_kernel(
+    dense_ref, base_ref, phi_ref, wk_ref, gathered_ref, scaled_ref, payload_ref, held_ref, sems
+):
+    term = product(dense_ref, held_ref, fetch(gathered_ref, NODES, held_ref, sems))
     scaled = base_ref[0:NODES, :] + base_ref[NODES : NODES + 1, :] * term
     scaled_ref[0:NODES, :] = scaled
-    scaled_ref[NODES:, :] = base_ref[NODES:, :]
-    moments = jnp.dot(phi_ref[...], scaled, precision=HIGHEST, preferred_element_type=F32)
+    scaled_ref[NODES : NODES + 8, :] = base_ref[NODES:, :]
+    phi = phi_ref[0 : 8 * GROUPS, :]
+    moments = jnp.dot(phi, scaled, precision=HIGHEST, preferred_element_type=F32)
     group = [moments[8 * t : 8 * t + 8] for t in range(GROUPS)]
     flux = group[1] + group[2]
     for t, shift in ((3, from_below_y), (4, from_above_y), (5, from_below_z), (6, from_above_z)):
         flux = flux + (group[t] - shift(group[t]))
-    mine = iota((8, CELLS), 0) < 5
-    rows = (group[0], flux, group[1], group[2])
+    scaled_ref[NODES + 8 :, :] = flux
+    k = iota((8, CELLS), 0)
+    first = group[0]
+    second = jnp.where(k < 5, group[1], pltpu.roll(group[2], 6, 0))
+    third = jnp.where(k < 5, phi_ref[8 * GROUPS :, :], pltpu.roll(group[2], 3, 0))
     for part in range(PARTS):
-        for t in range(4):
-            at = slice(part * PAYLOAD + 8 * t, part * PAYLOAD + 8 * t + 8)
-            payload_ref[at, :] = jnp.where(mine, rows[t], spare_ref[at, :])
+        wk = jnp.concatenate([wk_ref[2 * part], wk_ref[2 * part + 1]], axis=1)
+        start = part * PAYLOAD
+        payload_ref[start : start + 8, :] = jnp.where(k < 5, first, pltpu.roll(wk, 5, 0))
+        payload_ref[start + 8 : start + 16, :] = jnp.where(
+            (k < 5) | (k == 7), second, pltpu.roll(wk, 2, 0)
+        )
+        payload_ref[start + 16 : start + 24, :] = third
 
 
 def totals_of(payload_ref, scaled_ref):
     total = payload_ref[0:PAYLOAD, :]
     for part in range(1, PARTS):
         total = total + payload_ref[part * PAYLOAD : (part + 1) * PAYLOAD, :]
-    group = [total[8 * t : 8 * t + 8] for t in range(4)]
+    first, second, third = total[0:8], total[8:16], total[16:24]
     k = iota((8, CELLS), 0)
     mine = k < 5
-
-    def spare(first, second):
-        return jnp.where(
-            k < 3, pltpu.roll(first, 3, 0), jnp.where(mine, pltpu.roll(second, 6, 0), 0.0)
-        )
-
-    wk = spare(group[0], group[1])
-    small = spare(group[2], group[3])
-    group = [jnp.where(mine, g, 0.0) for g in group]
+    wk = jnp.where(k < 3, pltpu.roll(first, 3, 0), jnp.where(mine, pltpu.roll(second, 6, 0), 0.0))
+    down = jnp.where(k == 1, pltpu.roll(second, 2, 0), jnp.where(mine, pltpu.roll(third, 5, 0), 0.0))
+    down = jnp.where(k == 0, second - COURANT_SCALE * pltpu.roll(first, 7, 0), down)
+    first, second, small = [jnp.where(mine, g, 0.0) for g in (first, second, third)]
     inverse = inverse_of(small[:, 0:128])
-    rows = scaled_ref[NODES:, :]
-    coeffs = rows[1:2] * apply_small(inverse, 8, rows[2:3] * group[0])
-    return group, wk, small, inverse, coeffs
+    rows = scaled_ref[NODES : NODES + 8, :]
+    coeffs = rows[1:2] * apply_small(inverse, 8, rows[2:3] * first)
+    return (first, second, down), wk, small, inverse, coeffs
 
 
 def middle_kernel(payload_ref, scaled_ref, copies_ref, block_ref, own_ref, sems, own_sems):
     group, wk, small, inverse, coeffs = totals_of(payload_ref, scaled_ref)
     z_speed = scaled_ref[NODES + 3 : NODES + 4, :]
-    for m in range(Q):
-        rows = slice(Q * m, Q * m + Q)
-        s = scaled_ref[rows, :] + equilibrium_rows(m, coeffs, z_speed)
-        block_ref[rows, :] = s.astype(BF16)
-    copies = in_parts(NODES + EXTRA, 0, block_ref, copies_ref, sems)
+    copies = []
+    for i in range(PIECES):
+        for m in range(i * Q // PIECES, (i + 1) * Q // PIECES):
+            rows = slice(Q * m, Q * m + Q)
+            s = scaled_ref[rows, :] + equilibrium_rows(m, coeffs, z_speed)
+            block_ref[rows, :] = s.astype(BF16)
+        copies += in_parts(NODES + EXTRA, 0, i, PIECES, block_ref, copies_ref, sems)
     pieces = jnp.concatenate([p.astype(F32) for p in split(wk, 3)], axis=0).astype(BF16)
     own = KERNEL_STEP * three_sum(jnp.dot(pieces, block_ref[...], preferred_element_type=F32))
+    own = own - scaled_ref[NODES + 8 :, :]
     own_ref[...] = jnp.concatenate([p.astype(F32) for p in split(own, 2)], axis=0).astype(BF16)
-    copies += in_parts(NODES + EXTRA, NODES, own_ref, copies_ref, own_sems)
+    copies += in_parts(NODES + EXTRA, NODES, 0, 1, own_ref, copies_ref, own_sems)
     for copy in copies:
         copy.wait()
 
@@ -267,11 +301,11 @@
     group, wk, small, inverse, coeffs = totals_of(payload_ref, scaled_ref)
     z_speed = scaled_ref[NODES + 3 : NODES + 4, :]
     from_eq = [apply_small(small, 8 * t, coeffs) for t in range(GROUPS)]
-    flux = group[1] + from_eq[1] + from_eq[2]
+    flux = from_eq[1] + from_eq[2]
     for t, shift in ((3, from_below_y), (4, from_above_y), (5, from_below_z), (6, from_above_z)):
         flux = flux + (from_eq[t] - shift(from_eq[t]))
-    high_ref[NODES // 2 :, :] = group[2] + from_eq[1]
-    low_ref[NODES // 2 :, :] = group[3] + from_eq[2]
+    high_ref[NODES // 2 :, :] = group[1] + from_eq[1]
+    low_ref[NODES // 2 :, :] = group[2] + from_eq[2]
     for m in range(Q):
         rows = slice(Q * m, Q * m + Q)
         s = scaled_ref[rows, :] + equilibrium_rows(m, coeffs, z_speed)
@@ -296,16 +330,23 @@
     base_ref[NODES + 16 :, :] = step_rows(rate, z_speed)
 
 
-def last_kernel(dense_ref, gathered_ref, base_ref, out_ref, term_ref):
+def last_kernel(
+    dense_ref, base_ref, gathered_ref, out_ref, term_ref, held_ref, own_ref, sems, own_sems
+):
     stride = NODES + EXTRA
-    term_ref[...] = jnp.dot(
-        dense_ref[...],
-        jnp.concatenate([gathered_ref[p * stride : p * stride + NODES, :] for p in range(PARTS)], axis=0),
-        preferred_element_type=F32,
-    )
+    copies = fetch(gathered_ref, stride, held_ref, sems)
+    extra = []
+    for part in range(PARTS):
+        source = gathered_ref.at[part * stride + NODES : (part + 1) * stride]
+        at = slice(part * EXTRA, (part + 1) * EXTRA)
+        extra.append(pltpu.make_async_copy(source, own_ref.at[at], own_sems.at[part]))
+        extra[-1].start()
+    term_ref[...] = product(dense_ref, held_ref, copies)
+    for copy in extra:
+        copy.wait()
     total = base_ref[NODES : NODES + 8, :]
     for part in range(PARTS):
-        own = gathered_ref[part * stride + NODES : (part + 1) * stride, :].astype(F32)
+        own = own_ref[part * EXTRA : (part + 1) * EXTRA, :].astype(F32)
         total = total + (own[0:8] + own[8:16])
     rows = base_ref[NODES + 16 :, :]
     coeffs = rows[1:2] * apply_small(base_ref[NODES + 8 : NODES + 16, 0:128], 8, total)
@@ -318,19 +359,20 @@
 
 VMEM = pl.BlockSpec(memory_space=pltpu.VMEM)
 SMEM = pl.BlockSpec(memory_space=pltpu.SMEM)
-ANY = pl.BlockSpec(memory_space=pl.ANY)
-
-
-def call(kernel, scalars, arrays, outs, scratch=(), in_hbm=False):
+HBM = pl.BlockSpec(memory_space=pltpu.HBM)
+
+
+def call(kernel, scalars, arrays, outs, scratch=(), in_hbm=False, from_hbm=()):
     make = pltpu.HBM if in_hbm else jax.ShapeDtypeStruct
+    from_hbm = [pltpu.with_memory_space_constraint(a, pltpu.HBM) for a in from_hbm]
     return pl.pallas_call(
         kernel,
         out_shape=[make(shape, kind) for shape, kind in outs],
-        in_specs=[SMEM] * len(scalars) + [VMEM] * len(arrays),
-        out_specs=[ANY if in_hbm else VMEM] * len(outs),
+        in_specs=[SMEM] * len(scalars) + [VMEM] * len(arrays) + [HBM] * len(from_hbm),
+        out_specs=[HBM if in_hbm else VMEM] * len(outs),
         scratch_shapes=list(scratch),
         compiler_params=pltpu.CompilerParams(vmem_limit_bytes=VMEM_BYTES),
-    )(*scalars, *arrays)
+    )(*scalars, *arrays, *from_hbm)
 
 
 def sides(low, high):
@@ -350,31 +392,34 @@
     z_speed = speed_of(lax.axis_index("vert")).reshape(1)
     half = NODES // 2
     block = pltpu.VMEM((NODES, CELLS), BF16)
+    held = pltpu.VMEM((PARTS * NODES, CELLS), BF16)
     sems = pltpu.SemaphoreType.DMA((PARTS,))
+    many = pltpu.SemaphoreType.DMA((PIECES, PARTS))
+    one = pltpu.SemaphoreType.DMA((1, PARTS))
     (copies,) = call(
-        copies_kernel, [], [state], [((PARTS * NODES, CELLS), BF16)], [block, sems], True
+        copies_kernel, [], [], [((PARTS * NODES, CELLS), BF16)],
+        [pltpu.VMEM((2 * NODES, CELLS // 2), F32), block, sems, many], True, [state],
     )
     gathered = spread(copies)
-    low, high, dense, phi, spare = call(
+    low, high, dense, phi, wk = call(
         prepare_kernel, [tile_cols, z_speed], [state, weight, kernel_tiles],
         [
             ((half, CELLS), F32), ((half, CELLS), F32), ((NODES, PARTS * NODES), BF16),
-            ((8 * GROUPS, NODES), F32), ((PARTS * PAYLOAD, CELLS), F32),
+            ((8 * GROUPS + 8, NODES), F32), ((2 * PARTS, 8, TILE), F32),
         ],
-        [pltpu.VMEM((2 * PARTS, 8, TILE), F32)],
     )
     above, below = sides(low, high)
     (base,) = call(
         base_kernel, [z_speed], [state, relax_rate, above, below], [((NODES + 8, CELLS), F32)]
     )
     scaled, payload = call(
-        first_kernel, [], [dense, gathered, base, phi, spare],
-        [((NODES + 8, CELLS), F32), ((PARTS * PAYLOAD, CELLS), F32)],
+        first_kernel, [], [dense, base, phi, wk],
+        [((NODES + 16, CELLS), F32), ((PARTS * PAYLOAD, CELLS), F32)], [held, sems], False, [gathered],
     )
     payload = spread(payload)
     (copies,) = call(
         middle_kernel, [], [payload, scaled], [((PARTS * (NODES + EXTRA), CELLS), BF16)],
-        [block, pltpu.VMEM((EXTRA, CELLS), BF16), sems, sems], True,
+        [block, pltpu.VMEM((EXTRA, CELLS), BF16), many, one], True,
     )
     gathered = spread(copies)
     state, low, high = call(
@@ -387,8 +432,11 @@
         [((NODES + 24, CELLS), F32)],
     )
     (out,) = call(
-        last_kernel, [], [dense, gathered, base], [((2 * NODES, CELLS // 2), F32)],
-        [pltpu.VMEM((NODES, CELLS), F32)],
+        last_kernel, [], [dense, base], [((2 * NODES, CELLS // 2), F32)],
+        [
+            pltpu.VMEM((NODES, CELLS), F32), held, pltpu.VMEM((PARTS * EXTRA, CELLS), BF16), sems, sems,
+        ],
+        False, [gathered],
     )
     return out.reshape(distribution.shape)
 

time: 99.9 us -> 99.6 us (level)
  local copies, waits for them, and re-layouts: 4.4 us -> 0.03 us
  Pallas kernels: 10.2 us -> 14.3 us
  blocking collectives: 14.5 us -> 13 us
    unnamed x20 -> x10, local copies, waits for them, and re-layouts: 4.4 us -> 0.03 us
    pallas_call x8, Pallas kernels: 10.2 us -> 14.3 us  [call(): pl.pallas_call(kernel, out_shape=[make(shape, kind) for shape, kind in ou...]
    all_to_all x1, blocking collectives: 14.5 us -> 13 us  [spread(): return lax.all_to_all(copies, 'vert', 0, 0, tiled=True)]
where the time goes in v3:
time: 99.6 us; the launch traced here: 99.3 us
  waiting for transfers between devices  59.1 us (59%)
  Pallas kernels  14.3 us (14%)
  blocking collectives  13 us (13%)
  starting transfers between devices  12.7 us (13%)
    all_to_all x2, waiting for transfers between devices, spread(): return lax.all_to_all(copies, 'vert', 0, 0, tiled=True)  51.2 us
    pallas_call x8, Pallas kernels, call(): pl.pallas_call(kernel, out_shape=[make(shape, kind) for shape, kind in ou...  14.3 us
    all_to_all x1, blocking collectives, spread(): return lax.all_to_all(copies, 'vert', 0, 0, tiled=True)  13 us
    all_to_all x2, starting transfers between devices, spread(): return lax.all_to_all(copies, 'vert', 0, 0, tiled=True)  11.7 us
    ppermute x4, waiting for transfers between devices, sides(): return (lax.ppermute(low, 'gx', down), lax.ppermute(high, 'gx', up))  7.9 us
  transfers between devices with their start and end apart: 6, of which 6 were waited for; matrix products, arithmetic and copies ran while one was open for 0% of the time, Pallas kernels for 2%

profile of v3, /device:TPU:96, one launch (start us, length us, event | category | flops | bytes accessed | tf_op | source)
XLA Modules:
  0.0 99.3 jit_solution(3239224180553521415)
XLA Ops:
  0.0 2.7 %shard_map.57 = bf16[4096,256]{1,0:T(8,128)(2,1)} custom-call(f32[512,128]{1,0:T(8,128)} %bitcast.12), custom_call_target="tpu_custom_call" | custom-call | tf_op jit(solution)/shard_map/pallas_call | solution.py:368
  2.7 0.0 copy-start
  2.7 0.0 copy-start.1
  2.7 0.0 copy-start.3
  2.7 0.0 copy-start.4
  2.7 0.0 copy-start.2
  2.8 7.2 %all-to-all-start = ((bf16[16,256,256]{2,1,0:T(8,128)(2,1)}), bf16[16,256,256]{2,1,0:T(8,128)(2,1)}, u32[]{:S(2)}, u32[]{:S(2)}) async-start(bf16[16,256,256]{2,1,0:T(8,128)(2,1)} %bitcast.18), calls=%async_computation | async-start | bytes 4194304 | tf_op jit(solution)/shard_map/all_to_all | solution.py:386
  10.0 0.0 copy-done
  10.0 0.0 copy-done.1
  10.0 0.0 copy-done.3
  10.0 0.0 copy-done.4
  10.0 1.0 %shard_map.55 = (f32[128,256]{1,0:T(8,128)S(1)}, f32[128,256]{1,0:T(8,128)S(1)}, bf16[256,4096]{1,0:T(8,128)(2,1)S(1)}, f32[64,256]{1,0:T(8,128)S(1)}, f32[32,8,128]{2,1,0:T(8,128)S(1)}) custom-call(s32[2,12]{1,0:T(2,128)S(1)} %copy-done.3, f32[1]{0:T(128)} %bitcast.z_ref, f32[512,128]{1,0:T(8,128)S(1)} %bitcast.13, f32[1,256]{1,0:T(1,128)S(1)} %bitcast.16, ...), custom_call_target="tpu_custom_call" | custom-call | tf_op jit(solution)/shard_map/pallas_call | solution.py:368
  11.1 0.0 collective-permute-start
  11.1 0.5 collective-permute-start.1
  11.6 2.0 %collective-permute-done.above_ref = f32[128,256]{1,0:T(8,128)S(1)} collective-permute-done((f32[128,256]{1,0:T(8,128)S(1)}, f32[128,256]{1,0:T(8,128)S(1)}, u32[]{:S(2)}, u32[]{:S(2)}) %collective-permute-start) | collective-permute-done | bytes 131104 | tf_op jit(solution)/shard_map/ppermute | solution.py:382
  13.6 1.9 %collective-permute-done.1.below_ref = f32[128,256]{1,0:T(8,128)S(1)} collective-permute-done((f32[128,256]{1,0:T(8,128)S(1)}, f32[128,256]{1,0:T(8,128)S(1)}, u32[]{:S(2)}, u32[]{:S(2)}) %collective-permute-start.1) | collective-permute-done | bytes 131104 | tf_op jit(solution)/shard_map/ppermute | solution.py:382
  15.5 0.0 copy-done.2
  15.5 0.3 shard_map.56.base_ref
  15.8 25.9 %all-to-all-done = bf16[16,256,256]{2,1,0:T(8,128)(2,1)} async-done(((bf16[16,256,256]{2,1,0:T(8,128)(2,1)}), bf16[16,256,256]{2,1,0:T(8,128)(2,1)}, u32[]{:S(2)}, u32[]{:S(2)}) %all-to-all-start) | async-done | bytes 2097184 | tf_op jit(solution)/shard_map/all_to_all | solution.py:386
  41.7 3.1 %shard_map.58 = (f32[272,256]{1,0:T(8,128)S(1)}, f32[384,256]{1,0:T(8,128)S(1)}) custom-call(bf16[256,4096]{1,0:T(8,128)(2,1)S(1)} %get-tuple-element.15.dense_ref, f32[264,256]{1,0:T(8,128)S(1)} %shard_map.56.base_ref, f32[64,256]{1,0:T(8,128)S(1)} %get-tuple-element.18.phi_ref, f32[32,8,128]{2,1,0:T(8,128)S(1)} %get-tuple-element.19.wk_ref, ...), custom_call_target="tpu_custom_call" | custom-call | tf_op jit(solution)/shard_map/pallas_call | solution.py:368
  44.8 13.0 %all_to_all.33 = f32[16,24,256]{2,1,0:T(8,128)S(1)} all-to-all(f32[16,24,256]{2,1,0:T(8,128)S(1)} %bitcast.15), channel_id=1, replica_groups=mesh['gx'=32,'vert'=16] {'vert'}, dimensions={0} | all-to-all | bytes 786432 | tf_op jit(solution)/shard_map/all_to_all | solution.py:386
  57.8 2.3 %shard_map.61 = bf16[4352,256]{1,0:T(8,128)(2,1)} custom-call(f32[384,256]{1,0:T(8,128)S(1)} %bitcast.10, f32[272,256]{1,0:T(8,128)S(1)} %get-tuple-element.21.scaled_ref), custom_call_target="tpu_custom_call" | custom-call | tf_op jit(solution)/shard_map/pallas_call | solution.py:368
  60.1 4.5 %all-to-all-start.2 = ((bf16[16,272,256]{2,1,0:T(8,128)(2,1)}), bf16[16,272,256]{2,1,0:T(8,128)(2,1)}, u32[]{:S(2)}, u32[]{:S(2)}) async-start(bf16[16,272,256]{2,1,0:T(8,128)(2,1)} %bitcast.17), calls=%async_computation.2 | async-start | bytes 4456448 | tf_op jit(solution)/shard_map/all_to_all | solution.py:386
  64.6 0.6 shard_map.59
  65.2 0.0 collective-permute-start.2
  65.3 0.5 collective-permute-start.3
  65.8 2.1 %collective-permute-done.2.above_ref = f32[136,256]{1,0:T(8,128)S(1)} collective-permute-done((f32[136,256]{1,0:T(8,128)S(1)}, f32[136,256]{1,0:T(8,128)S(1)}, u32[]{:S(2)}, u32[]{:S(2)}) %collective-permute-start.2) | collective-permute-done | bytes 139296 | tf_op jit(solution)/shard_map/ppermute | solution.py:382
  67.9 1.9 %collective-permute-done.3.below_ref = f32[136,256]{1,0:T(8,128)S(1)} collective-permute-done((f32[136,256]{1,0:T(8,128)S(1)}, f32[136,256]{1,0:T(8,128)S(1)}, u32[]{:S(2)}, u32[]{:S(2)}) %collective-permute-start.3) | collective-permute-done | bytes 139296 | tf_op jit(solution)/shard_map/ppermute | solution.py:382
  69.8 0.3 shard_map.60.base_ref
  70.0 25.3 %all-to-all-done.2 = bf16[16,272,256]{2,1,0:T(8,128)(2,1)} async-done(((bf16[16,272,256]{2,1,0:T(8,128)(2,1)}), bf16[16,272,256]{2,1,0:T(8,128)(2,1)}, u32[]{:S(2)}, u32[]{:S(2)}) %all-to-all-start.2) | async-done | bytes 2228256 | tf_op jit(solution)/shard_map/all_to_all | solution.py:386
  95.4 3.9 %shard_map.62 = f32[512,128]{1,0:T(8,128)} custom-call(bf16[256,4096]{1,0:T(8,128)(2,1)S(1)} %get-tuple-element.15.dense_ref, f32[280,256]{1,0:T(8,128)S(1)} %shard_map.60.base_ref, bf16[4352,256]{1,0:T(8,128)(2,1)} %bitcast.8.gathered_ref), custom_call_target="tpu_custom_call" | custom-call | tf_op jit(solution)/shard_map/pallas_call | solution.py:368
Async XLA Ops:
  2.7 7.3 %copy-start = (f32[256,1,256]{2,1,0:T(1,128)S(1)}, f32[256,1,256]{2,1,0:T(1,128)}, u32[]{:S(2)}) copy-start(f32[256,1,256]{2,1,0:T(1,128)} %param.5) | copy-start | bytes 786436
  2.7 7.3 %copy-start.1 = (bf16[2,128,1536]{2,1,0:T(8,128)(2,1)S(1)}, bf16[2,128,1536]{2,1,0:T(8,128)(2,1)}, u32[]{:S(2)}) copy-start(bf16[2,128,1536]{2,1,0:T(8,128)(2,1)} %tiles_ref.1) | copy-start | bytes 2359300
  2.7 7.3 %copy-start.3 = (s32[2,12]{1,0:T(2,128)S(1)}, s32[2,12]{1,0:T(2,128)}, u32[]{:S(2)}) copy-start(s32[2,12]{1,0:T(2,128)} %cols_ref.1) | copy-start | bytes 292
  2.7 7.3 %copy-start.4 = (f32[256]{0:T(256)S(1)}, f32[256]{0:T(256)}, u32[]{:S(2)}) copy-start(f32[256]{0:T(256)} %param.7) | copy-start | bytes 3076
  2.7 12.8 %copy-start.2 = (f32[1,256]{1,0:T(1,128)S(1)}, f32[1,256]{1,0:T(1,128)}, u32[]{:S(2)}) copy-start(f32[1,256]{1,0:T(1,128)} %rate_ref.3) | copy-start | bytes 3076
  2.8 38.9 %all-to-all-start = ((bf16[16,256,256]{2,1,0:T(8,128)(2,1)}), bf16[16,256,256]{2,1,0:T(8,128)(2,1)}, u32[]{:S(2)}, u32[]{:S(2)}) async-start(bf16[16,256,256]{2,1,0:T(8,128)(2,1)} %bitcast.18), calls=%async_computation | async-start | bytes 4194304 | tf_op jit(solution)/shard_map/all_to_all | solution.py:386
  11.1 2.5 %collective-permute-start = (f32[128,256]{1,0:T(8,128)S(1)}, f32[128,256]{1,0:T(8,128)S(1)}, u32[]{:S(2)}, u32[]{:S(2)}) collective-permute-start(f32[128,256]{1,0:T(8,128)S(1)} %get-tuple-element.16), channel_id=1, source_target_pairs={{16,0},{32,16},{48,32},{64,48},{80,64},{96,80},{112,96},{128,112},... | collective-permute-start | bytes 393224 | tf_op jit(solution)/shard_map/ppermute | solution.py:382
  11.1 4.4 %collective-permute-start.1 = (f32[128,256]{1,0:T(8,128)S(1)}, f32[128,256]{1,0:T(8,128)S(1)}, u32[]{:S(2)}, u32[]{:S(2)}) collective-permute-start(f32[128,256]{1,0:T(8,128)S(1)} %get-tuple-element.17), channel_id=1, source_target_pairs={{0,16},{16,32},{32,48},{48,64},{64,80},{80,96},{96,112},{112,128},... | collective-permute-start | bytes 393224 | tf_op jit(solution)/shard_map/ppermute | solution.py:382
  60.1 35.2 %all-to-all-start.2 = ((bf16[16,272,256]{2,1,0:T(8,128)(2,1)}), bf16[16,272,256]{2,1,0:T(8,128)(2,1)}, u32[]{:S(2)}, u32[]{:S(2)}) async-start(bf16[16,272,256]{2,1,0:T(8,128)(2,1)} %bitcast.17), calls=%async_computation.2 | async-start | bytes 4456448 | tf_op jit(solution)/shard_map/all_to_all | solution.py:386
  65.2 2.6 %collective-permute-start.2 = (f32[136,256]{1,0:T(8,128)S(1)}, f32[136,256]{1,0:T(8,128)S(1)}, u32[]{:S(2)}, u32[]{:S(2)}) collective-permute-start(f32[136,256]{1,0:T(8,128)S(1)} %get-tuple-element.23), channel_id=1, source_target_pairs={{16,0},{32,16},{48,32},{64,48},{80,64},{96,80},{112,96},{128,112},... | collective-permute-start | bytes 417800 | tf_op jit(solution)/shard_map/ppermute | solution.py:382
  65.3 4.5 %collective-permute-start.3 = (f32[136,256]{1,0:T(8,128)S(1)}, f32[136,256]{1,0:T(8,128)S(1)}, u32[]{:S(2)}, u32[]{:S(2)}) collective-permute-start(f32[136,256]{1,0:T(8,128)S(1)} %get-tuple-element.24), channel_id=1, source_target_pairs={{0,16},{16,32},{32,48},{48,64},{64,80},{80,96},{96,112},{112,128},... | collective-permute-start | bytes 417800 | tf_op jit(solution)/shard_map/ppermute | solution.py:382

commit v4 on v3

--- a/solution.py
+++ b/solution.py
@@ -166,7 +166,7 @@
 
 def prepare_kernel(
     cols_ref, z_ref, state_ref, weight_ref, tiles_ref,
-    low_ref, high_ref, dense_ref, phi_ref, wk_ref,
+    low_ref, high_ref, wk_ref, phi_out_ref, phi_ref, sem,
 ):
     for m in range(Q):
         store_sides(m, load_state(state_ref, m), low_ref, high_ref)
@@ -179,7 +179,8 @@
         invariants, padded, (((1,), (1,)), ((), ())), precision=HIGHEST, preferred_element_type=F32
     )
     phi_ref[8 * GROUPS :, :] = jnp.concatenate([small, jnp.zeros((8, CELLS - TILE), F32)], axis=1)
-    dense_ref[...] = jnp.zeros_like(dense_ref)
+    copy = pltpu.make_async_copy(phi_ref, phi_out_ref, sem)
+    copy.start()
     wk_ref[...] = jnp.zeros_like(wk_ref)
     pieces = jnp.concatenate([p.astype(F32) for p in split(base, 3)], axis=0).astype(BF16)
     for r in range(2):
@@ -190,8 +191,7 @@
             at = slice(j * TILE, (j + 1) * TILE)
             col = cols_ref[r, j]
             wk_ref[col] = wk_ref[col] + part[:, at]
-            where = pl.ds(pl.multiple_of(col * TILE, TILE), TILE)
-            dense_ref[r * TILE : (r + 1) * TILE, where] = tiles_ref[r, :, at]
+    copy.wait()
 
 
 def step_rows(rate, z_speed):
@@ -212,34 +212,29 @@
     base_ref[NODES:, :] = step_rows(rate, z_speed)
 
 
-def fetch(gathered_ref, stride, held_ref, sems):
-    copies = []
-    for part in range(PARTS):
-        at = slice(part * NODES, (part + 1) * NODES)
-        source = gathered_ref.at[part * stride : part * stride + NODES]
-        copies.append(pltpu.make_async_copy(source, held_ref.at[at], sems.at[part]))
-        copies[-1].start()
-    return copies
-
-
-def product(dense_ref, held_ref, copies):
-    total = None
-    for i in range(4):
-        for copy in copies[4 * i : 4 * i + 4]:
-            copy.wait()
-        at = slice(4 * i * NODES, 4 * (i + 1) * NODES)
-        part = jnp.dot(dense_ref[:, at], held_ref[at, :], preferred_element_type=F32)
-        total = part if total is None else total + part
-    return total
+def kernel_product(cols_ref, tiles_ref, gathered_ref, stride, term_ref):
+    for r in range(2):
+        blocks = []
+        for j in range(NB):
+            col = cols_ref[r, j]
+            start = (col // 2) * stride + (col % 2) * TILE
+            blocks.append(gathered_ref[pl.ds(pl.multiple_of(start, 16), TILE), :])
+        term_ref[r * TILE : (r + 1) * TILE, :] = jnp.dot(
+            tiles_ref[r], jnp.concatenate(blocks, axis=0), preferred_element_type=F32
+        )
 
 
 def first_kernel(
-    dense_ref, base_ref, phi_ref, wk_ref, gathered_ref, scaled_ref, payload_ref, held_ref, sems
+    cols_ref, tiles_ref, gathered_ref, base_ref, wk_ref, phi_in_ref,
+    scaled_ref, payload_ref, term_ref, phi_ref, sem,
 ):
-    term = product(dense_ref, held_ref, fetch(gathered_ref, NODES, held_ref, sems))
-    scaled = base_ref[0:NODES, :] + base_ref[NODES : NODES + 1, :] * term
+    copy = pltpu.make_async_copy(phi_in_ref, phi_ref, sem)
+    copy.start()
+    kernel_product(cols_ref, tiles_ref, gathered_ref, NODES, term_ref)
+    scaled = base_ref[0:NODES, :] + base_ref[NODES : NODES + 1, :] * term_ref[...]
     scaled_ref[0:NODES, :] = scaled
     scaled_ref[NODES : NODES + 8, :] = base_ref[NODES:, :]
+    copy.wait()
     phi = phi_ref[0 : 8 * GROUPS, :]
     moments = jnp.dot(phi, scaled, precision=HIGHEST, preferred_element_type=F32)
     group = [moments[8 * t : 8 * t + 8] for t in range(GROUPS)]
@@ -330,23 +325,12 @@
     base_ref[NODES + 16 :, :] = step_rows(rate, z_speed)
 
 
-def last_kernel(
-    dense_ref, base_ref, gathered_ref, out_ref, term_ref, held_ref, own_ref, sems, own_sems
-):
+def last_kernel(cols_ref, tiles_ref, gathered_ref, base_ref, out_ref, term_ref):
     stride = NODES + EXTRA
-    copies = fetch(gathered_ref, stride, held_ref, sems)
-    extra = []
-    for part in range(PARTS):
-        source = gathered_ref.at[part * stride + NODES : (part + 1) * stride]
-        at = slice(part * EXTRA, (part + 1) * EXTRA)
-        extra.append(pltpu.make_async_copy(source, own_ref.at[at], own_sems.at[part]))
-        extra[-1].start()
-    term_ref[...] = product(dense_ref, held_ref, copies)
-    for copy in extra:
-        copy.wait()
+    kernel_product(cols_ref, tiles_ref, gathered_ref, stride, term_ref)
     total = base_ref[NODES : NODES + 8, :]
     for part in range(PARTS):
-        own = own_ref[part * EXTRA : (part + 1) * EXTRA, :].astype(F32)
+        own = gathered_ref[part * stride + NODES : (part + 1) * stride, :].astype(F32)
         total = total + (own[0:8] + own[8:16])
     rows = base_ref[NODES + 16 :, :]
     coeffs = rows[1:2] * apply_small(base_ref[NODES + 8 : NODES + 16, 0:128], 8, total)
@@ -362,14 +346,15 @@
 HBM = pl.BlockSpec(memory_space=pltpu.HBM)
 
 
-def call(kernel, scalars, arrays, outs, scratch=(), in_hbm=False, from_hbm=()):
-    make = pltpu.HBM if in_hbm else jax.ShapeDtypeStruct
+def call(kernel, scalars, arrays, outs, scratch=(), in_hbm=(), from_hbm=()):
     from_hbm = [pltpu.with_memory_space_constraint(a, pltpu.HBM) for a in from_hbm]
     return pl.pallas_call(
         kernel,
-        out_shape=[make(shape, kind) for shape, kind in outs],
+        out_shape=[
+            (pltpu.HBM if i in in_hbm else jax.ShapeDtypeStruct)(shape, kind) for i, (shape, kind) in enumerate(outs)
+        ],
         in_specs=[SMEM] * len(scalars) + [VMEM] * len(arrays) + [HBM] * len(from_hbm),
-        out_specs=[HBM if in_hbm else VMEM] * len(outs),
+        out_specs=[HBM if i in in_hbm else VMEM for i in range(len(outs))],
         scratch_shapes=list(scratch),
         compiler_params=pltpu.CompilerParams(vmem_limit_bytes=VMEM_BYTES),
     )(*scalars, *arrays, *from_hbm)
@@ -392,34 +377,37 @@
     z_speed = speed_of(lax.axis_index("vert")).reshape(1)
     half = NODES // 2
     block = pltpu.VMEM((NODES, CELLS), BF16)
-    held = pltpu.VMEM((PARTS * NODES, CELLS), BF16)
+    term = pltpu.VMEM((NODES, CELLS), F32)
     sems = pltpu.SemaphoreType.DMA((PARTS,))
+    phi_rows = pltpu.VMEM((8 * GROUPS + 8, NODES), F32)
+    dma = pltpu.SemaphoreType.DMA
     many = pltpu.SemaphoreType.DMA((PIECES, PARTS))
     one = pltpu.SemaphoreType.DMA((1, PARTS))
     (copies,) = call(
         copies_kernel, [], [], [((PARTS * NODES, CELLS), BF16)],
-        [pltpu.VMEM((2 * NODES, CELLS // 2), F32), block, sems, many], True, [state],
+        [pltpu.VMEM((2 * NODES, CELLS // 2), F32), block, sems, many], (0,), [state],
     )
     gathered = spread(copies)
-    low, high, dense, phi, wk = call(
+    low, high, wk, phi = call(
         prepare_kernel, [tile_cols, z_speed], [state, weight, kernel_tiles],
         [
-            ((half, CELLS), F32), ((half, CELLS), F32), ((NODES, PARTS * NODES), BF16),
-            ((8 * GROUPS + 8, NODES), F32), ((2 * PARTS, 8, TILE), F32),
+            ((half, CELLS), F32), ((half, CELLS), F32), ((2 * PARTS, 8, TILE), F32),
+            ((8 * GROUPS + 8, NODES), F32),
         ],
+        [phi_rows, dma], (3,),
     )
     above, below = sides(low, high)
     (base,) = call(
         base_kernel, [z_speed], [state, relax_rate, above, below], [((NODES + 8, CELLS), F32)]
     )
     scaled, payload = call(
-        first_kernel, [], [dense, base, phi, wk],
-        [((NODES + 16, CELLS), F32), ((PARTS * PAYLOAD, CELLS), F32)], [held, sems], False, [gathered],
+        first_kernel, [tile_cols], [kernel_tiles, gathered, base, wk],
+        [((NODES + 16, CELLS), F32), ((PARTS * PAYLOAD, CELLS), F32)], [term, phi_rows, dma], (), [phi],
     )
     payload = spread(payload)
     (copies,) = call(
         middle_kernel, [], [payload, scaled], [((PARTS * (NODES + EXTRA), CELLS), BF16)],
-        [block, pltpu.VMEM((EXTRA, CELLS), BF16), many, one], True,
+        [block, pltpu.VMEM((EXTRA, CELLS), BF16), many, one], (0,),
     )
     gathered = spread(copies)
     state, low, high = call(
@@ -432,11 +420,8 @@
         [((NODES + 24, CELLS), F32)],
     )
     (out,) = call(
-        last_kernel, [], [dense, base], [((2 * NODES, CELLS // 2), F32)],
-        [
-            pltpu.VMEM((NODES, CELLS), F32), held, pltpu.VMEM((PARTS * EXTRA, CELLS), BF16), sems, sems,
-        ],
-        False, [gathered],
+        last_kernel, [tile_cols], [kernel_tiles, gathered, base],
+        [((2 * NODES, CELLS // 2), F32)], [term],
     )
     return out.reshape(distribution.shape)
 

time: 99.6 us -> 95.5 us (0.959)
  the two profiles are of different devices: /device:TPU:96 before, /device:TPU:288 now
where the time goes in v4:
time: 95.5 us; the launch traced here: 95.2 us
  waiting for transfers between devices  57.7 us (60%)
  blocking collectives  13 us (14%)
  starting transfers between devices  11.9 us (12%)
  Pallas kernels  11.4 us (12%)
  local copies, waits for them, and re-layouts  0.98 us (1%)
    all_to_all x2, waiting for transfers between devices, spread(): return lax.all_to_all(copies, 'vert', 0, 0, tiled=True)  49.6 us
    all_to_all x1, blocking collectives, spread(): return lax.all_to_all(copies, 'vert', 0, 0, tiled=True)  13 us
    pallas_call x8, Pallas kernels, call(): pl.pallas_call(kernel, out_shape=[(pltpu.HBM if i in in_hbm else jax.Shap...  11.4 us
    all_to_all x2, starting transfers between devices, spread(): return lax.all_to_all(copies, 'vert', 0, 0, tiled=True)  10.9 us
    ppermute x4, waiting for transfers between devices, sides(): return (lax.ppermute(low, 'gx', down), lax.ppermute(high, 'gx', up))  8.04 us
  transfers between devices with their start and end apart: 6, of which 6 were waited for; matrix products, arithmetic and copies ran while one was open for 0% of the time, Pallas kernels for 3%

profile of v4, /device:TPU:288, one launch (start us, length us, event | category | flops | bytes accessed | tf_op | source)
XLA Modules:
  0.0 95.2 jit_solution(12187183074451854339)
XLA Ops:
  0.0 2.7 %shard_map.55 = bf16[4096,256]{1,0:T(8,128)(2,1)} custom-call(f32[512,128]{1,0:T(8,128)} %bitcast.14), custom_call_target="tpu_custom_call" | custom-call | tf_op jit(solution)/shard_map/pallas_call | solution.py:351
  2.7 0.0 copy-start
  2.7 0.0 copy-start.1
  2.7 0.0 copy-start.4
  2.7 0.0 copy-start.6
  2.7 0.0 copy-start.5
  2.7 7.2 %all-to-all-start = ((bf16[16,256,256]{2,1,0:T(8,128)(2,1)}), bf16[16,256,256]{2,1,0:T(8,128)(2,1)S(1)}, u32[]{:S(2)}, u32[]{:S(2)}) async-start(bf16[16,256,256]{2,1,0:T(8,128)(2,1)} %bitcast.20), calls=%async_computation | async-start | bytes 4194304 | tf_op jit(solution)/shard_map/all_to_all | solution.py:371
  9.9 0.0 copy-done
  9.9 0.0 copy-done.1
  10.0 0.0 copy-done.4
  10.0 0.0 copy-done.6
  10.0 1.4 %shard_map.56 = (f32[128,256]{1,0:T(8,128)S(1)}, f32[128,256]{1,0:T(8,128)S(1)}, f32[32,8,128]{2,1,0:T(8,128)S(1)}, f32[64,256]{1,0:T(8,128)}) custom-call(s32[2,12]{1,0:T(2,128)S(1)} %copy-done.4, f32[1]{0:T(128)} %bitcast.3.z_ref, f32[512,128]{1,0:T(8,128)S(1)} %bitcast.15, f32[1,256]{1,0:T(1,128)S(1)} %bitcast.18, bf16[2,128,1536]{2,1,0:T(8,128)(2,1)S(1)} %copy-done), custom_call_target="tpu_custom_call" | custom-call | tf_op jit(solution)/shard_map/pallas_call | solution.py:351
  11.4 0.2 collective-permute-start
  11.6 0.3 collective-permute-start.1
  11.9 2.2 %collective-permute-done.above_ref = f32[128,256]{1,0:T(8,128)S(1)} collective-permute-done((f32[128,256]{1,0:T(8,128)S(1)}, f32[128,256]{1,0:T(8,128)S(1)}, u32[]{:S(2)}, u32[]{:S(2)}) %collective-permute-start) | collective-permute-done | bytes 131104 | tf_op jit(solution)/shard_map/ppermute | solution.py:367
  14.1 1.9 %collective-permute-done.1.below_ref = f32[128,256]{1,0:T(8,128)S(1)} collective-permute-done((f32[128,256]{1,0:T(8,128)S(1)}, f32[128,256]{1,0:T(8,128)S(1)}, u32[]{:S(2)}, u32[]{:S(2)}) %collective-permute-start.1) | collective-permute-done | bytes 131104 | tf_op jit(solution)/shard_map/ppermute | solution.py:367
  16.0 0.0 copy-done.5
  16.0 0.3 shard_map.57.base_ref
  16.3 25.3 %all-to-all-done = bf16[16,256,256]{2,1,0:T(8,128)(2,1)S(1)} async-done(((bf16[16,256,256]{2,1,0:T(8,128)(2,1)}), bf16[16,256,256]{2,1,0:T(8,128)(2,1)S(1)}, u32[]{:S(2)}, u32[]{:S(2)}) %all-to-all-start) | async-done | bytes 2097184 | tf_op jit(solution)/shard_map/all_to_all | solution.py:371
  41.6 2.1 %shard_map.58 = (f32[272,256]{1,0:T(8,128)S(1)}, f32[384,256]{1,0:T(8,128)S(1)}) custom-call(s32[2,12]{1,0:T(2,128)S(1)} %copy-done.4, bf16[2,128,1536]{2,1,0:T(8,128)(2,1)S(1)} %copy-done, bf16[4096,256]{1,0:T(8,128)(2,1)S(1)} %bitcast.11, f32[264,256]{1,0:T(8,128)S(1)} %shard_map.57.base_ref, f32[32,8,128]{2,1,0:T(8,128)S(1)} %get-tuple-element.16.wk_ref, ...), custom_call_target="tpu_custom_call" | custom-call | tf_op jit(solution)/shard_map/pallas_call | solution.py:351
  43.7 0.0 copy-start.2
  43.7 13.0 %all_to_all.33 = f32[16,24,256]{2,1,0:T(8,128)S(1)} all-to-all(f32[16,24,256]{2,1,0:T(8,128)S(1)} %bitcast.17), channel_id=1, replica_groups=mesh['gx'=32,'vert'=16] {'vert'}, dimensions={0} | all-to-all | bytes 786432 | tf_op jit(solution)/shard_map/all_to_all | solution.py:371
  56.7 0.0 copy-done.2
  56.7 2.3 %shard_map.59 = bf16[4352,256]{1,0:T(8,128)(2,1)} custom-call(f32[384,256]{1,0:T(8,128)S(1)} %bitcast.12, f32[272,256]{1,0:T(8,128)S(1)} %get-tuple-element.19.scaled_ref), custom_call_target="tpu_custom_call" | custom-call | tf_op jit(solution)/shard_map/pallas_call | solution.py:351
  59.1 3.7 %all-to-all-start.2 = ((bf16[16,272,256]{2,1,0:T(8,128)(2,1)}), bf16[16,272,256]{2,1,0:T(8,128)(2,1)S(1)}, u32[]{:S(2)}, u32[]{:S(2)}) async-start(bf16[16,272,256]{2,1,0:T(8,128)(2,1)} %bitcast.19), calls=%async_computation.2 | async-start | bytes 4456448 | tf_op jit(solution)/shard_map/all_to_all | solution.py:371
  62.8 0.0 copy-start.3
  62.8 0.9 copy-done.3
  63.8 0.6 shard_map.60
  64.4 0.0 collective-permute-start.2
  64.4 0.5 collective-permute-start.3
  64.9 2.1 %collective-permute-done.2.above_ref = f32[136,256]{1,0:T(8,128)S(1)} collective-permute-done((f32[136,256]{1,0:T(8,128)S(1)}, f32[136,256]{1,0:T(8,128)S(1)}, u32[]{:S(2)}, u32[]{:S(2)}) %collective-permute-start.2) | collective-permute-done | bytes 139296 | tf_op jit(solution)/shard_map/ppermute | solution.py:367
  67.0 1.9 %collective-permute-done.3.below_ref = f32[136,256]{1,0:T(8,128)S(1)} collective-permute-done((f32[136,256]{1,0:T(8,128)S(1)}, f32[136,256]{1,0:T(8,128)S(1)}, u32[]{:S(2)}, u32[]{:S(2)}) %collective-permute-start.3) | collective-permute-done | bytes 139296 | tf_op jit(solution)/shard_map/ppermute | solution.py:367
  68.9 0.3 shard_map.61.base_ref
  69.2 24.3 %all-to-all-done.2 = bf16[16,272,256]{2,1,0:T(8,128)(2,1)S(1)} async-done(((bf16[16,272,256]{2,1,0:T(8,128)(2,1)}), bf16[16,272,256]{2,1,0:T(8,128)(2,1)S(1)}, u32[]{:S(2)}, u32[]{:S(2)}) %all-to-all-start.2) | async-done | bytes 2228256 | tf_op jit(solution)/shard_map/all_to_all | solution.py:371
  93.5 1.7 %shard_map.62 = f32[512,128]{1,0:T(8,128)} custom-call(s32[2,12]{1,0:T(2,128)S(1)} %copy-done.4, bf16[2,128,1536]{2,1,0:T(8,128)(2,1)S(1)} %copy-done, bf16[4352,256]{1,0:T(8,128)(2,1)S(1)} %bitcast.10, f32[280,256]{1,0:T(8,128)S(1)} %shard_map.61.base_ref), custom_call_target="tpu_custom_call" | custom-call | tf_op jit(solution)/shard_map/pallas_call | solution.py:351
Async XLA Ops:
  2.7 7.3 %copy-start = (bf16[2,128,1536]{2,1,0:T(8,128)(2,1)S(1)}, bf16[2,128,1536]{2,1,0:T(8,128)(2,1)}, u32[]{:S(2)}) copy-start(bf16[2,128,1536]{2,1,0:T(8,128)(2,1)} %tiles_ref.5) | copy-start | bytes 2359300
  2.7 7.3 %copy-start.1 = (f32[256,1,256]{2,1,0:T(1,128)S(1)}, f32[256,1,256]{2,1,0:T(1,128)}, u32[]{:S(2)}) copy-start(f32[256,1,256]{2,1,0:T(1,128)} %param.5) | copy-start | bytes 786436
  2.7 7.3 %copy-start.4 = (s32[2,12]{1,0:T(2,128)S(1)}, s32[2,12]{1,0:T(2,128)}, u32[]{:S(2)}) copy-start(s32[2,12]{1,0:T(2,128)} %cols_ref.5) | copy-start | bytes 292
  2.7 7.2 %copy-start.6 = (f32[256]{0:T(256)S(1)}, f32[256]{0:T(256)}, u32[]{:S(2)}) copy-start(f32[256]{0:T(256)} %param.7) | copy-start | bytes 3076
  2.7 13.3 %copy-start.5 = (f32[1,256]{1,0:T(1,128)S(1)}, f32[1,256]{1,0:T(1,128)}, u32[]{:S(2)}) copy-start(f32[1,256]{1,0:T(1,128)} %rate_ref.3) | copy-start | bytes 3076
  2.7 38.8 %all-to-all-start = ((bf16[16,256,256]{2,1,0:T(8,128)(2,1)}), bf16[16,256,256]{2,1,0:T(8,128)(2,1)S(1)}, u32[]{:S(2)}, u32[]{:S(2)}) async-start(bf16[16,256,256]{2,1,0:T(8,128)(2,1)} %bitcast.20), calls=%async_computation | async-start | bytes 4194304 | tf_op jit(solution)/shard_map/all_to_all | solution.py:371
  11.4 2.7 %collective-permute-start = (f32[128,256]{1,0:T(8,128)S(1)}, f32[128,256]{1,0:T(8,128)S(1)}, u32[]{:S(2)}, u32[]{:S(2)}) collective-permute-start(f32[128,256]{1,0:T(8,128)S(1)} %get-tuple-element.14), channel_id=1, source_target_pairs={{16,0},{32,16},{48,32},{64,48},{80,64},{96,80},{112,96},{128,112},... | collective-permute-start | bytes 393224 | tf_op jit(solution)/shard_map/ppermute | solution.py:367
  11.6 4.4 %collective-permute-start.1 = (f32[128,256]{1,0:T(8,128)S(1)}, f32[128,256]{1,0:T(8,128)S(1)}, u32[]{:S(2)}, u32[]{:S(2)}) collective-permute-start(f32[128,256]{1,0:T(8,128)S(1)} %get-tuple-element.15), channel_id=1, source_target_pairs={{0,16},{16,32},{32,48},{48,64},{64,80},{80,96},{96,112},{112,128},... | collective-permute-start | bytes 393224 | tf_op jit(solution)/shard_map/ppermute | solution.py:367
  43.7 13.0 %copy-start.2 = (f32[272,256]{1,0:T(8,128)}, f32[272,256]{1,0:T(8,128)S(1)}, u32[]{:S(2)}) copy-start(f32[272,256]{1,0:T(8,128)S(1)} %get-tuple-element.19.scaled_ref) | copy-start | bytes 835588
  59.1 34.5 %all-to-all-start.2 = ((bf16[16,272,256]{2,1,0:T(8,128)(2,1)}), bf16[16,272,256]{2,1,0:T(8,128)(2,1)S(1)}, u32[]{:S(2)}, u32[]{:S(2)}) async-start(bf16[16,272,256]{2,1,0:T(8,128)(2,1)} %bitcast.19), calls=%async_computation.2 | async-start | bytes 4456448 | tf_op jit(solution)/shard_map/all_to_all | solution.py:371
  62.8 1.0 %copy-start.3 = (f32[272,256]{1,0:T(8,128)S(1)}, f32[272,256]{1,0:T(8,128)}, u32[]{:S(2)}) copy-start(f32[272,256]{1,0:T(8,128)} %copy-done.2) | copy-start | bytes 835588
  64.4 2.6 %collective-permute-start.2 = (f32[136,256]{1,0:T(8,128)S(1)}, f32[136,256]{1,0:T(8,128)S(1)}, u32[]{:S(2)}, u32[]{:S(2)}) collective-permute-start(f32[136,256]{1,0:T(8,128)S(1)} %get-tuple-element.21), channel_id=1, source_target_pairs={{16,0},{32,16},{48,32},{64,48},{80,64},{96,80},{112,96},{128,112},... | collective-permute-start | bytes 417800 | tf_op jit(solution)/shard_map/ppermute | solution.py:367
  64.4 4.5 %collective-permute-start.3 = (f32[136,256]{1,0:T(8,128)S(1)}, f32[136,256]{1,0:T(8,128)S(1)}, u32[]{:S(2)}, u32[]{:S(2)}) collective-permute-start(f32[136,256]{1,0:T(8,128)S(1)} %get-tuple-element.22), channel_id=1, source_target_pairs={{0,16},{16,32},{32,48},{48,64},{64,80},{80,96},{96,112},{112,128},... | collective-permute-start | bytes 417800 | tf_op jit(solution)/shard_map/ppermute | solution.py:367

commit v5 on v4

--- a/solution.py
+++ b/solution.py
@@ -19,7 +19,7 @@
 MIDDLE = (Q - 1) / 2.0
 EXTRA = 16
 PAYLOAD = 24
-PIECES = 2
+SIDE = 4
 GROUPS = 7
 F32 = jnp.float32
 BF16 = jnp.bfloat16
@@ -69,7 +69,7 @@
     node = iota((8, NODES), 1)
     k = iota((8, NODES), 0)
     x, y = speed_of(node % Q), speed_of(node // Q)
-    z = jnp.full((8, NODES), z_speed)
+    z = jnp.broadcast_to(z_speed, (8, NODES))
     invariants = jnp.where(k == 0, 1.0, 0.0)
     for row, value in ((1, x), (2, y), (3, z), (4, x * x + y * y + z * z)):
         invariants = jnp.where(k == row, value, invariants)
@@ -78,6 +78,12 @@
         factors.append(COURANT_SCALE * jnp.maximum(speed, 0.0))
         factors.append(COURANT_SCALE * jnp.maximum(-speed, 0.0))
     return invariants, factors
+
+
+def weights_rows(z_speed, weight):
+    invariants, factors = node_rows(z_speed)
+    base = weight * invariants
+    return invariants, base, jnp.concatenate([base] + [base * f for f in factors[1:]], axis=0)
 
 
 def advected_rows(m, s, below, above, z_speed):
@@ -132,56 +138,35 @@
     high_ref[8 * m : 8 * m + 8, :] = s[8:16]
 
 
-def in_parts(rows_per_part, start, piece, pieces, block_ref, copies_ref, sems):
-    count = block_ref.shape[0] // pieces
-    copies = []
-    for part in range(PARTS):
-        at = part * rows_per_part + start + piece * count
-        copies.append(
-            pltpu.make_async_copy(
-                block_ref.at[piece * count : (piece + 1) * count],
-                copies_ref.at[at : at + count],
-                sems.at[piece, part],
-            )
-        )
-        copies[-1].start()
-    return copies
-
-
-def copies_kernel(state_ref, copies_ref, held_ref, block_ref, in_sems, sems):
-    pieces = []
-    for i in range(PIECES):
-        at = pl.ds(i * 2 * NODES // PIECES, 2 * NODES // PIECES)
-        pieces.append(pltpu.make_async_copy(state_ref.at[at], held_ref.at[at], in_sems.at[i]))
-        pieces[-1].start()
-    copies = []
-    for i in range(PIECES):
-        pieces[i].wait()
-        for m in range(i * Q // PIECES, (i + 1) * Q // PIECES):
-            block_ref[Q * m : Q * m + Q, :] = load_state(held_ref, m).astype(BF16)
-        copies += in_parts(NODES, 0, i, PIECES, block_ref, copies_ref, sems)
-    for copy in copies:
-        copy.wait()
+def copies_kernel(state_ref, copies_ref):
+    for m in range(Q):
+        rounded = load_state(state_ref, m).astype(BF16)
+        for part in range(SIDE):
+            copies_ref[part * NODES + Q * m : part * NODES + Q * m + Q, :] = rounded
+
+
+def arrival(place_ref, col):
+    first, y, x = place_ref[0], place_ref[1], place_ref[2]
+    from_y, from_x = col // (2 * SIDE), col // 2 % SIDE
+    bundle = jnp.where(first == 0, y - from_y, x - from_x)
+    bundle = jnp.where(bundle < 0, bundle + SIDE, bundle)
+    return (bundle * SIDE + jnp.where(first == 0, from_x, from_y)) * 2 + col % 2
 
 
 def prepare_kernel(
-    cols_ref, z_ref, state_ref, weight_ref, tiles_ref,
-    low_ref, high_ref, wk_ref, phi_out_ref, phi_ref, sem,
+    cols_ref, place_ref, z_ref, state_ref, weight_ref, tiles_ref,
+    low_ref, high_ref, dense_ref, wk_out_ref, wk_ref, sem,
 ):
     for m in range(Q):
         store_sides(m, load_state(state_ref, m), low_ref, high_ref)
-    invariants, factors = node_rows(z_ref[0])
-    base = weight_ref[...] * invariants
-    phi = jnp.concatenate([base] + [base * f for f in factors[1:]], axis=0)
-    phi_ref[0 : 8 * GROUPS, :] = phi
+    invariants, base, phi = weights_rows(z_ref[0], weight_ref[...])
     padded = jnp.concatenate([phi, jnp.zeros((TILE - 8 * GROUPS, NODES), F32)], axis=0)
     small = lax.dot_general(
         invariants, padded, (((1,), (1,)), ((), ())), precision=HIGHEST, preferred_element_type=F32
     )
-    phi_ref[8 * GROUPS :, :] = jnp.concatenate([small, jnp.zeros((8, CELLS - TILE), F32)], axis=1)
-    copy = pltpu.make_async_copy(phi_ref, phi_out_ref, sem)
-    copy.start()
     wk_ref[...] = jnp.zeros_like(wk_ref)
+    dense_ref[...] = jnp.zeros_like(dense_ref)
+    wk_ref[2 * PARTS] = small
     pieces = jnp.concatenate([p.astype(F32) for p in split(base, 3)], axis=0).astype(BF16)
     for r in range(2):
         part = three_sum(
@@ -191,6 +176,10 @@
             at = slice(j * TILE, (j + 1) * TILE)
             col = cols_ref[r, j]
             wk_ref[col] = wk_ref[col] + part[:, at]
+            where = pl.ds(pl.multiple_of(arrival(place_ref, col) * TILE, TILE), TILE)
+            dense_ref[r * TILE : (r + 1) * TILE, where] = tiles_ref[r, :, at]
+    copy = pltpu.make_async_copy(wk_ref, wk_out_ref, sem)
+    copy.start()
     copy.wait()
 
 
@@ -200,7 +189,7 @@
     return jnp.concatenate(rows + [jnp.zeros((4, CELLS), F32)], axis=0)
 
 
-def base_kernel(z_ref, state_ref, rate_ref, above_ref, below_ref, base_ref):
+def base_kernel(z_ref, state_ref, rate_ref, weight_ref, above_ref, below_ref, base_ref):
     z_speed = z_ref[0]
     rate = rate_ref[...]
     keep = 1.0 / (1.0 + rate)
@@ -210,32 +199,33 @@
         e = advected_rows(m, s, below_ref[half, :], above_ref[half, :], z_speed)
         base_ref[Q * m : Q * m + Q, :] = keep * e
     base_ref[NODES:, :] = step_rows(rate, z_speed)
-
-
-def kernel_product(cols_ref, tiles_ref, gathered_ref, stride, term_ref):
-    for r in range(2):
-        blocks = []
-        for j in range(NB):
-            col = cols_ref[r, j]
-            start = (col // 2) * stride + (col % 2) * TILE
-            blocks.append(gathered_ref[pl.ds(pl.multiple_of(start, 16), TILE), :])
-        term_ref[r * TILE : (r + 1) * TILE, :] = jnp.dot(
-            tiles_ref[r], jnp.concatenate(blocks, axis=0), preferred_element_type=F32
+    base_ref[NODES + 4 : NODES + 5, :] = weight_ref[...]
+
+
+def kernel_product(dense_ref, bundle_refs, stride):
+    total = None
+    for i, ref in enumerate(bundle_refs):
+        blocks = [ref[j * stride : j * stride + NODES, :] for j in range(SIDE)]
+        at = slice(i * SIDE * NODES, (i + 1) * SIDE * NODES)
+        part = jnp.dot(
+            dense_ref[:, at], jnp.concatenate(blocks, axis=0), preferred_element_type=F32
         )
+        total = part if total is None else total + part
+    return total
 
 
 def first_kernel(
-    cols_ref, tiles_ref, gathered_ref, base_ref, wk_ref, phi_in_ref,
-    scaled_ref, payload_ref, term_ref, phi_ref, sem,
+    dense_ref, base_ref, own_ref, near_ref, far_ref, back_ref, wk_in_ref,
+    scaled_ref, payload_ref, wk_ref, sem,
 ):
-    copy = pltpu.make_async_copy(phi_in_ref, phi_ref, sem)
+    copy = pltpu.make_async_copy(wk_in_ref, wk_ref, sem)
     copy.start()
-    kernel_product(cols_ref, tiles_ref, gathered_ref, NODES, term_ref)
-    scaled = base_ref[0:NODES, :] + base_ref[NODES : NODES + 1, :] * term_ref[...]
+    term = kernel_product(dense_ref, (own_ref, near_ref, far_ref, back_ref), NODES)
+    scaled = base_ref[0:NODES, :] + base_ref[NODES : NODES + 1, :] * term
     scaled_ref[0:NODES, :] = scaled
     scaled_ref[NODES : NODES + 8, :] = base_ref[NODES:, :]
-    copy.wait()
-    phi = phi_ref[0 : 8 * GROUPS, :]
+    rows = base_ref[NODES:, :]
+    _, _, phi = weights_rows(rows[3:4], rows[4:5])
     moments = jnp.dot(phi, scaled, precision=HIGHEST, preferred_element_type=F32)
     group = [moments[8 * t : 8 * t + 8] for t in range(GROUPS)]
     flux = group[1] + group[2]
@@ -245,7 +235,9 @@
     k = iota((8, CELLS), 0)
     first = group[0]
     second = jnp.where(k < 5, group[1], pltpu.roll(group[2], 6, 0))
-    third = jnp.where(k < 5, phi_ref[8 * GROUPS :, :], pltpu.roll(group[2], 3, 0))
+    copy.wait()
+    small = jnp.concatenate([wk_ref[2 * PARTS], jnp.zeros((8, CELLS - TILE), F32)], axis=1)
+    third = jnp.where(k < 5, small, pltpu.roll(group[2], 3, 0))
     for part in range(PARTS):
         wk = jnp.concatenate([wk_ref[2 * part], wk_ref[2 * part + 1]], axis=1)
         start = part * PAYLOAD
@@ -273,23 +265,24 @@
     return (first, second, down), wk, small, inverse, coeffs
 
 
-def middle_kernel(payload_ref, scaled_ref, copies_ref, block_ref, own_ref, sems, own_sems):
+def middle_kernel(payload_ref, scaled_ref, copies_ref, block_ref):
     group, wk, small, inverse, coeffs = totals_of(payload_ref, scaled_ref)
     z_speed = scaled_ref[NODES + 3 : NODES + 4, :]
-    copies = []
-    for i in range(PIECES):
-        for m in range(i * Q // PIECES, (i + 1) * Q // PIECES):
-            rows = slice(Q * m, Q * m + Q)
-            s = scaled_ref[rows, :] + equilibrium_rows(m, coeffs, z_speed)
-            block_ref[rows, :] = s.astype(BF16)
-        copies += in_parts(NODES + EXTRA, 0, i, PIECES, block_ref, copies_ref, sems)
+    for m in range(Q):
+        rows = slice(Q * m, Q * m + Q)
+        s = scaled_ref[rows, :] + equilibrium_rows(m, coeffs, z_speed)
+        rounded = s.astype(BF16)
+        block_ref[rows, :] = rounded
+        for part in range(SIDE):
+            start = part * (NODES + EXTRA) + Q * m
+            copies_ref[start : start + Q, :] = rounded
     pieces = jnp.concatenate([p.astype(F32) for p in split(wk, 3)], axis=0).astype(BF16)
     own = KERNEL_STEP * three_sum(jnp.dot(pieces, block_ref[...], preferred_element_type=F32))
     own = own - scaled_ref[NODES + 8 :, :]
-    own_ref[...] = jnp.concatenate([p.astype(F32) for p in split(own, 2)], axis=0).astype(BF16)
-    copies += in_parts(NODES + EXTRA, NODES, 0, 1, own_ref, copies_ref, own_sems)
-    for copy in copies:
-        copy.wait()
+    own = jnp.concatenate([p.astype(F32) for p in split(own, 2)], axis=0).astype(BF16)
+    for part in range(SIDE):
+        start = part * (NODES + EXTRA) + NODES
+        copies_ref[start : start + EXTRA, :] = own
 
 
 def state_kernel(payload_ref, scaled_ref, state_ref, low_ref, high_ref):
@@ -325,13 +318,15 @@
     base_ref[NODES + 16 :, :] = step_rows(rate, z_speed)
 
 
-def last_kernel(cols_ref, tiles_ref, gathered_ref, base_ref, out_ref, term_ref):
+def last_kernel(dense_ref, base_ref, own_ref, near_ref, far_ref, back_ref, out_ref, term_ref):
     stride = NODES + EXTRA
-    kernel_product(cols_ref, tiles_ref, gathered_ref, stride, term_ref)
+    bundles = (own_ref, near_ref, far_ref, back_ref)
+    term_ref[...] = kernel_product(dense_ref, bundles, stride)
     total = base_ref[NODES : NODES + 8, :]
-    for part in range(PARTS):
-        own = gathered_ref[part * stride + NODES : (part + 1) * stride, :].astype(F32)
-        total = total + (own[0:8] + own[8:16])
+    for ref in bundles:
+        for j in range(SIDE):
+            own = ref[j * stride + NODES : (j + 1) * stride, :].astype(F32)
+            total = total + (own[0:8] + own[8:16])
     rows = base_ref[NODES + 16 :, :]
     coeffs = rows[1:2] * apply_small(base_ref[NODES + 8 : NODES + 16, 0:128], 8, total)
     for m in range(Q):
@@ -371,45 +366,56 @@
     return lax.all_to_all(copies, "vert", 0, 0, tiled=True)
 
 
+def gather(copies):
+    slabs = lax.axis_size("gx")
+    groups, pairs = [], [[], [], []]
+    for g in range(slabs):
+        for i in range(SIDE):
+            line = [i * SIDE + j if g % 2 == 0 else j * SIDE + i for j in range(SIDE)]
+            groups.append([g * PARTS + v for v in line])
+            for j in range(SIDE):
+                for shift in (1, 2, 3):
+                    y, x = (i + shift) % SIDE, j
+                    ends = (i * SIDE + j, y * SIDE + x) if g % 2 == 0 else (j * SIDE + i, x * SIDE + y)
+                    pairs[shift - 1].append(tuple(g * PARTS + v for v in ends))
+    axes = ("gx", "vert")
+    bundle = lax.all_to_all(copies, axes, 0, 0, axis_index_groups=groups, tiled=True)
+    return [bundle] + [lax.ppermute(bundle, axes, p) for p in pairs]
+
+
 def per_device(distribution, relax_rate, node_weight, kernel_tiles, tile_cols):
     state = distribution.reshape(2 * NODES, CELLS // 2)
     weight = node_weight.reshape(1, NODES)
     z_speed = speed_of(lax.axis_index("vert")).reshape(1)
     half = NODES // 2
-    block = pltpu.VMEM((NODES, CELLS), BF16)
-    term = pltpu.VMEM((NODES, CELLS), F32)
-    sems = pltpu.SemaphoreType.DMA((PARTS,))
-    phi_rows = pltpu.VMEM((8 * GROUPS + 8, NODES), F32)
+    vert = lax.axis_index("vert")
+    place = jnp.stack([lax.axis_index("gx") % 2, vert // SIDE, vert % SIDE]).astype(jnp.int32)
+    wk_rows = (2 * PARTS + 1, 8, TILE)
     dma = pltpu.SemaphoreType.DMA
-    many = pltpu.SemaphoreType.DMA((PIECES, PARTS))
-    one = pltpu.SemaphoreType.DMA((1, PARTS))
-    (copies,) = call(
-        copies_kernel, [], [], [((PARTS * NODES, CELLS), BF16)],
-        [pltpu.VMEM((2 * NODES, CELLS // 2), F32), block, sems, many], (0,), [state],
-    )
-    gathered = spread(copies)
-    low, high, wk, phi = call(
-        prepare_kernel, [tile_cols, z_speed], [state, weight, kernel_tiles],
+    (copies,) = call(copies_kernel, [], [state], [((SIDE * NODES, CELLS), BF16)])
+    bundles = gather(copies)
+    low, high, dense, wk = call(
+        prepare_kernel, [tile_cols, place, z_speed], [state, weight, kernel_tiles],
         [
-            ((half, CELLS), F32), ((half, CELLS), F32), ((2 * PARTS, 8, TILE), F32),
-            ((8 * GROUPS + 8, NODES), F32),
+            ((half, CELLS), F32), ((half, CELLS), F32), ((NODES, PARTS * NODES), BF16), (wk_rows, F32),
         ],
-        [phi_rows, dma], (3,),
+        [pltpu.VMEM(wk_rows, F32), dma], (3,),
     )
     above, below = sides(low, high)
     (base,) = call(
-        base_kernel, [z_speed], [state, relax_rate, above, below], [((NODES + 8, CELLS), F32)]
+        base_kernel, [z_speed], [state, relax_rate, weight, above, below], [((NODES + 8, CELLS), F32)]
     )
     scaled, payload = call(
-        first_kernel, [tile_cols], [kernel_tiles, gathered, base, wk],
-        [((NODES + 16, CELLS), F32), ((PARTS * PAYLOAD, CELLS), F32)], [term, phi_rows, dma], (), [phi],
+        first_kernel, [], [dense, base, *bundles],
+        [((NODES + 16, CELLS), F32), ((PARTS * PAYLOAD, CELLS), F32)],
+        [pltpu.VMEM(wk_rows, F32), dma], (), [wk],
     )
     payload = spread(payload)
     (copies,) = call(
-        middle_kernel, [], [payload, scaled], [((PARTS * (NODES + EXTRA), CELLS), BF16)],
-        [block, pltpu.VMEM((EXTRA, CELLS), BF16), many, one], (0,),
-    )
-    gathered = spread(copies)
+        middle_kernel, [], [payload, scaled], [((SIDE * (NODES + EXTRA), CELLS), BF16)],
+        [pltpu.VMEM((NODES, CELLS), BF16)],
+    )
+    bundles = gather(copies)
     state, low, high = call(
         state_kernel, [], [payload, scaled],
         [((NODES + 16, CELLS), F32), ((half + 8, CELLS), F32), ((half + 8, CELLS), F32)],
@@ -420,8 +426,8 @@
         [((NODES + 24, CELLS), F32)],
     )
     (out,) = call(
-        last_kernel, [tile_cols], [kernel_tiles, gathered, base],
-        [((2 * NODES, CELLS // 2), F32)], [term],
+        last_kernel, [], [dense, base, *bundles], [((2 * NODES, CELLS // 2), F32)],
+        [pltpu.VMEM((NODES, CELLS), F32)],
     )
     return out.reshape(distribution.shape)
 

time: 95.5 us -> 90.8 us (0.951)
  the two profiles are of different devices: /device:TPU:288 before, /device:TPU:2 now
where the time goes in v5:
time: 90.8 us; the launch traced here: 90.4 us
  blocking collectives  40.7 us (45%)
  starting transfers between devices  23.2 us (26%)
  waiting for transfers between devices  17.4 us (19%)
  Pallas kernels  6.49 us (7%)
  local copies, waits for them, and re-layouts  2.33 us (3%)
    all_to_all x2, blocking collectives, gather(): lax.all_to_all(copies, axes, 0, 0, axis_index_groups=groups, tiled=True)  28.4 us
    ppermute x6, starting transfers between devices, gather(): return [bundle] + [lax.ppermute(bundle, axes, p) for p in pairs]  15.9 us
    all_to_all x1, blocking collectives, spread(): return lax.all_to_all(copies, 'vert', 0, 0, tiled=True)  12.4 us
    ppermute x4, waiting for transfers between devices, sides(): return (lax.ppermute(low, 'gx', down), lax.ppermute(high, 'gx', up))  10.8 us
    ppermute x4, starting transfers between devices, sides(): return (lax.ppermute(low, 'gx', down), lax.ppermute(high, 'gx', up))  7.33 us
    ppermute x6, waiting for transfers between devices, gather(): return [bundle] + [lax.ppermute(bundle, axes, p) for p in pairs]  6.6 us
    pallas_call x8, Pallas kernels, call(): pl.pallas_call(kernel, out_shape=[(pltpu.HBM if i in in_hbm else jax.Shap...  6.49 us
    unnamed x14, local copies, waits for them, and re-layouts  2.33 us
  transfers between devices with their start and end apart: 10, of which 6 were waited for; matrix products, arithmetic and copies ran while one was open for 0% of the time, Pallas kernels for 3%

profile of v5, /device:TPU:2, one launch (start us, length us, event | category | flops | bytes accessed | tf_op | source)
XLA Modules:
  0.0 90.4 jit_solution(5444434080394172912)
XLA Ops:
  0.0 0.0 copy-start.4
  0.0 0.0 copy-start
  0.0 1.0 %copy-done = f32[256,1,256]{2,1,0:T(1,128)S(1)} copy-done((f32[256,1,256]{2,1,0:T(1,128)S(1)}, f32[256,1,256]{2,1,0:T(1,128)}, u32[]{:S(2)}) %copy-start) | copy-done | bytes 262168
  1.0 0.0 copy-start.1
  1.0 0.0 copy-start.2
  1.0 0.0 copy-start.5
  1.0 15.1 %all_to_all.33 = bf16[4,256,256]{2,1,0:T(8,128)(2,1)S(1)} all-to-all(bf16[4,256,256]{2,1,0:T(8,128)(2,1)S(1)} %bitcast.23), channel_id=1, replica_groups={{0,1,2,3},{4,5,6,7},{8,9,10,11},{12,13,14,15},{16,20,24,28},{17,21,25,2..., dimensions={0} | all-to-all | bytes 1048576 | tf_op jit(solution)/shard_map/all_to_all | solution.py:382
  16.1 1.9 %collective-permute-start.4 = (bf16[1024,256]{1,0:T(8,128)(2,1)S(1)}, bf16[1024,256]{1,0:T(8,128)(2,1)S(1)}, u32[]{:S(2)}, u32[]{:S(2)}) collective-permute-start(bf16[1024,256]{1,0:T(8,128)(2,1)S(1)} %bitcast.24), channel_id=1, source_target_pairs={{0,12},{1,13},{2,14},{3,15},{4,0},{5,1},{6,2},{7,3},{8,4},{9,5},{1... | collective-permute-start | bytes 1572872 | tf_op jit(solution)/shard_map/ppermute | solution.py:383
  18.0 1.9 %collective-permute-start.3 = (bf16[1024,256]{1,0:T(8,128)(2,1)S(1)}, bf16[1024,256]{1,0:T(8,128)(2,1)S(1)}, u32[]{:S(2)}, u32[]{:S(2)}) collective-permute-start(bf16[1024,256]{1,0:T(8,128)(2,1)S(1)} %bitcast.25), channel_id=1, source_target_pairs={{0,8},{1,9},{2,10},{3,11},{4,12},{5,13},{6,14},{7,15},{8,0},{9,1},... | collective-permute-start | bytes 1572872 | tf_op jit(solution)/shard_map/ppermute | solution.py:383
  19.9 3.9 %collective-permute-start.2 = (bf16[1024,256]{1,0:T(8,128)(2,1)S(1)}, bf16[1024,256]{1,0:T(8,128)(2,1)S(1)}, u32[]{:S(2)}, u32[]{:S(2)}) collective-permute-start(bf16[1024,256]{1,0:T(8,128)(2,1)S(1)} %bitcast.26), channel_id=1, source_target_pairs={{0,4},{1,5},{2,6},{3,7},{4,8},{5,9},{6,10},{7,11},{8,12},{9,13},{1... | collective-permute-start | bytes 1572872 | tf_op jit(solution)/shard_map/ppermute | solution.py:383
  23.9 0.1 pad_add_fusion.place_ref
  24.0 0.0 copy-done.1
  24.0 0.0 copy-done.2
  24.0 0.0 copy-start.3
  24.0 0.7 copy-done.3
  24.6 0.0 copy-start.6
  24.6 0.7 copy-done.6
  25.3 1.8 %shard_map.55 = (f32[128,256]{1,0:T(8,128)S(1)}, f32[128,256]{1,0:T(8,128)S(1)}, bf16[256,4096]{1,0:T(8,128)(2,1)S(1)}, f32[33,8,128]{2,1,0:T(8,128)}) custom-call(s32[2,12]{1,0:T(2,128)S(1)} %copy-done.6, s32[3]{0:T(128)S(1)} %pad_add_fusion.place_ref, f32[1]{0:T(128)} %bitcast.3.z_ref, f32[512,128]{1,0:T(8,128)S(1)} %bitcast.16, f32[1,256]{1,0:T(1,128)S(1)} %bitcast.29, ...), custom_call_target="tpu_custom_call" | custom-call | tf_op jit(solution)/shard_map/pallas_call | solution.py:346
  27.2 6.8 %collective-permute-start = (f32[128,256]{1,0:T(8,128)S(1)}, f32[128,256]{1,0:T(8,128)S(1)}, u32[]{:S(2)}, u32[]{:S(2)}) collective-permute-start(f32[128,256]{1,0:T(8,128)S(1)} %get-tuple-element.15), channel_id=1, source_target_pairs={{16,0},{32,16},{48,32},{64,48},{80,64},{96,80},{112,96},{128,112},... | collective-permute-start | bytes 393224 | tf_op jit(solution)/shard_map/ppermute | solution.py:362
  34.0 0.0 collective-permute-start.1
  34.0 2.5 %collective-permute-done.above_ref = f32[128,256]{1,0:T(8,128)S(1)} collective-permute-done((f32[128,256]{1,0:T(8,128)S(1)}, f32[128,256]{1,0:T(8,128)S(1)}, u32[]{:S(2)}, u32[]{:S(2)}) %collective-permute-start) | collective-permute-done | bytes 131104 | tf_op jit(solution)/shard_map/ppermute | solution.py:362
  36.5 3.1 %collective-permute-done.1.below_ref = f32[128,256]{1,0:T(8,128)S(1)} collective-permute-done((f32[128,256]{1,0:T(8,128)S(1)}, f32[128,256]{1,0:T(8,128)S(1)}, u32[]{:S(2)}, u32[]{:S(2)}) %collective-permute-start.1) | collective-permute-done | bytes 131104 | tf_op jit(solution)/shard_map/ppermute | solution.py:362
  39.6 0.0 copy-done.4
  39.6 0.0 copy-done.5
  39.6 0.3 shard_map.56.base_ref
  39.9 0.0 collective-permute-done.4.back_ref
  39.9 0.0 collective-permute-done.3.far_ref
  39.9 0.0 collective-permute-done.2.near_ref
  39.9 1.3 %shard_map.58 = (f32[272,256]{1,0:T(8,128)S(1)}, f32[384,256]{1,0:T(8,128)S(1)}) custom-call(bf16[256,4096]{1,0:T(8,128)(2,1)S(1)} %get-tuple-element.14.dense_ref, f32[264,256]{1,0:T(8,128)S(1)} %shard_map.56.base_ref, bf16[1024,256]{1,0:T(8,128)(2,1)S(1)} %bitcast.27, bf16[1024,256]{1,0:T(8,128)(2,1)S(1)} %collective-permute-done.2.near_ref, ...), custom_call_target="tpu_custom_call" | custom-call | tf_op jit(solution)/shard_map/pallas_call | solution.py:346
  41.2 12.4 %all_to_all.34 = f32[16,24,256]{2,1,0:T(8,128)S(1)} all-to-all(f32[16,24,256]{2,1,0:T(8,128)S(1)} %bitcast.28), channel_id=1, replica_groups=mesh['gx'=32,'vert'=16] {'vert'}, dimensions={0} | all-to-all | bytes 786432 | tf_op jit(solution)/shard_map/all_to_all | solution.py:366
  53.6 0.7 shard_map.61
  54.3 13.3 %all_to_all.35 = bf16[4,272,256]{2,1,0:T(8,128)(2,1)S(1)} all-to-all(bf16[4,272,256]{2,1,0:T(8,128)(2,1)S(1)} %bitcast.22), channel_id=1, replica_groups={{0,1,2,3},{4,5,6,7},{8,9,10,11},{12,13,14,15},{16,20,24,28},{17,21,25,2..., dimensions={0} | all-to-all | bytes 1114112 | tf_op jit(solution)/shard_map/all_to_all | solution.py:382
  67.6 2.5 %collective-permute-start.9 = (bf16[1088,256]{1,0:T(8,128)(2,1)S(1)}, bf16[1088,256]{1,0:T(8,128)(2,1)S(1)}, u32[]{:S(2)}, u32[]{:S(2)}) collective-permute-start(bf16[1088,256]{1,0:T(8,128)(2,1)S(1)} %bitcast.18), channel_id=1, source_target_pairs={{0,12},{1,13},{2,14},{3,15},{4,0},{5,1},{6,2},{7,3},{8,4},{9,5},{1... | collective-permute-start | bytes 1671176 | tf_op jit(solution)/shard_map/ppermute | solution.py:383
  70.1 3.1 %collective-permute-start.8 = (bf16[1088,256]{1,0:T(8,128)(2,1)S(1)}, bf16[1088,256]{1,0:T(8,128)(2,1)S(1)}, u32[]{:S(2)}, u32[]{:S(2)}) collective-permute-start(bf16[1088,256]{1,0:T(8,128)(2,1)S(1)} %bitcast.19), channel_id=1, source_target_pairs={{0,8},{1,9},{2,10},{3,11},{4,12},{5,13},{6,14},{7,15},{8,0},{9,1},... | collective-permute-start | bytes 1671176 | tf_op jit(solution)/shard_map/ppermute | solution.py:383
  73.2 2.5 %collective-permute-start.7 = (bf16[1088,256]{1,0:T(8,128)(2,1)S(1)}, bf16[1088,256]{1,0:T(8,128)(2,1)S(1)}, u32[]{:S(2)}, u32[]{:S(2)}) collective-permute-start(bf16[1088,256]{1,0:T(8,128)(2,1)S(1)} %bitcast.20), channel_id=1, source_target_pairs={{0,4},{1,5},{2,6},{3,7},{4,8},{5,9},{6,10},{7,11},{8,12},{9,13},{1... | collective-permute-start | bytes 1671176 | tf_op jit(solution)/shard_map/ppermute | solution.py:383
  75.7 0.6 shard_map.59
  76.3 0.0 collective-permute-start.5
  76.4 0.5 collective-permute-start.6
  76.9 2.1 %collective-permute-done.5.above_ref = f32[136,256]{1,0:T(8,128)S(1)} collective-permute-done((f32[136,256]{1,0:T(8,128)S(1)}, f32[136,256]{1,0:T(8,128)S(1)}, u32[]{:S(2)}, u32[]{:S(2)}) %collective-permute-start.5) | collective-permute-done | bytes 139296 | tf_op jit(solution)/shard_map/ppermute | solution.py:362
  79.0 3.1 %collective-permute-done.6.below_ref = f32[136,256]{1,0:T(8,128)S(1)} collective-permute-done((f32[136,256]{1,0:T(8,128)S(1)}, f32[136,256]{1,0:T(8,128)S(1)}, u32[]{:S(2)}, u32[]{:S(2)}) %collective-permute-start.6) | collective-permute-done | bytes 139296 | tf_op jit(solution)/shard_map/ppermute | solution.py:362
  82.1 0.3 shard_map.60.base_ref
  82.4 0.0 collective-permute-done.9.back_ref
  82.4 0.7 collective-permute-done.8.far_ref
  83.1 5.9 %collective-permute-done.7.near_ref = bf16[1088,256]{1,0:T(8,128)(2,1)S(1)} collective-permute-done((bf16[1088,256]{1,0:T(8,128)(2,1)S(1)}, bf16[1088,256]{1,0:T(8,128)(2,1)S(1)}, u32[]{:S(2)}, u32[]{:S(2)}) %collective-permute-start.7) | collective-permute-done | bytes 557088 | tf_op jit(solution)/shard_map/ppermute | solution.py:383
  89.0 1.4 %shard_map.62 = f32[512,128]{1,0:T(8,128)} custom-call(bf16[256,4096]{1,0:T(8,128)(2,1)S(1)} %get-tuple-element.14.dense_ref, f32[280,256]{1,0:T(8,128)S(1)} %shard_map.60.base_ref, bf16[1088,256]{1,0:T(8,128)(2,1)S(1)} %bitcast.21, bf16[1088,256]{1,0:T(8,128)(2,1)S(1)} %collective-permute-done.7.near_ref, ...), custom_call_target="tpu_custom_call" | custom-call | tf_op jit(solution)/shard_map/pallas_call | solution.py:346
  (1 shorter events, 0.0 us)
Async XLA Ops:
  0.0 39.6 %copy-start.4 = (f32[256]{0:T(256)S(1)}, f32[256]{0:T(256)}, u32[]{:S(2)}) copy-start(f32[256]{0:T(256)} %param.7) | copy-start | bytes 3076
  0.0 1.0 %copy-start = (f32[256,1,256]{2,1,0:T(1,128)S(1)}, f32[256,1,256]{2,1,0:T(1,128)}, u32[]{:S(2)}) copy-start(f32[256,1,256]{2,1,0:T(1,128)} %param.5) | copy-start | bytes 786436
  1.0 23.0 %copy-start.1 = (f32[256,1,256]{2,1,0:T(1,128)S(1)}, f32[256,1,256]{2,1,0:T(1,128)}, u32[]{:S(2)}) copy-start(f32[256,1,256]{2,1,0:T(1,128)} %param.5) | copy-start | bytes 786436
  1.0 23.0 %copy-start.2 = (bf16[2,128,1536]{2,1,0:T(8,128)(2,1)S(1)}, bf16[2,128,1536]{2,1,0:T(8,128)(2,1)}, u32[]{:S(2)}) copy-start(bf16[2,128,1536]{2,1,0:T(8,128)(2,1)} %tiles_ref.1) | copy-start | bytes 2359300
  1.0 38.6 %copy-start.5 = (f32[1,256]{1,0:T(1,128)S(1)}, f32[1,256]{1,0:T(1,128)}, u32[]{:S(2)}) copy-start(f32[1,256]{1,0:T(1,128)} %rate_ref.3) | copy-start | bytes 3076
  16.1 23.8 %collective-permute-start.4 = (bf16[1024,256]{1,0:T(8,128)(2,1)S(1)}, bf16[1024,256]{1,0:T(8,128)(2,1)S(1)}, u32[]{:S(2)}, u32[]{:S(2)}) collective-permute-start(bf16[1024,256]{1,0:T(8,128)(2,1)S(1)} %bitcast.24), channel_id=1, source_target_pairs={{0,12},{1,13},{2,14},{3,15},{4,0},{5,1},{6,2},{7,3},{8,4},{9,5},{1... | collective-permute-start | bytes 1572872 | tf_op jit(solution)/shard_map/ppermute | solution.py:383
  18.0 21.9 %collective-permute-start.3 = (bf16[1024,256]{1,0:T(8,128)(2,1)S(1)}, bf16[1024,256]{1,0:T(8,128)(2,1)S(1)}, u32[]{:S(2)}, u32[]{:S(2)}) collective-permute-start(bf16[1024,256]{1,0:T(8,128)(2,1)S(1)} %bitcast.25), channel_id=1, source_target_pairs={{0,8},{1,9},{2,10},{3,11},{4,12},{5,13},{6,14},{7,15},{8,0},{9,1},... | collective-permute-start | bytes 1572872 | tf_op jit(solution)/shard_map/ppermute | solution.py:383
  19.9 20.0 %collective-permute-start.2 = (bf16[1024,256]{1,0:T(8,128)(2,1)S(1)}, bf16[1024,256]{1,0:T(8,128)(2,1)S(1)}, u32[]{:S(2)}, u32[]{:S(2)}) collective-permute-start(bf16[1024,256]{1,0:T(8,128)(2,1)S(1)} %bitcast.26), channel_id=1, source_target_pairs={{0,4},{1,5},{2,6},{3,7},{4,8},{5,9},{6,10},{7,11},{8,12},{9,13},{1... | collective-permute-start | bytes 1572872 | tf_op jit(solution)/shard_map/ppermute | solution.py:383
  24.0 0.7 copy-start.3
  24.6 0.7 copy-start.6
  27.2 9.3 %collective-permute-start = (f32[128,256]{1,0:T(8,128)S(1)}, f32[128,256]{1,0:T(8,128)S(1)}, u32[]{:S(2)}, u32[]{:S(2)}) collective-permute-start(f32[128,256]{1,0:T(8,128)S(1)} %get-tuple-element.15), channel_id=1, source_target_pairs={{16,0},{32,16},{48,32},{64,48},{80,64},{96,80},{112,96},{128,112},... | collective-permute-start | bytes 393224 | tf_op jit(solution)/shard_map/ppermute | solution.py:362
  34.0 5.6 %collective-permute-start.1 = (f32[128,256]{1,0:T(8,128)S(1)}, f32[128,256]{1,0:T(8,128)S(1)}, u32[]{:S(2)}, u32[]{:S(2)}) collective-permute-start(f32[128,256]{1,0:T(8,128)S(1)} %get-tuple-element.16), channel_id=1, source_target_pairs={{0,16},{16,32},{32,48},{48,64},{64,80},{80,96},{96,112},{112,128},... | collective-permute-start | bytes 393224 | tf_op jit(solution)/shard_map/ppermute | solution.py:362
  67.6 14.8 %collective-permute-start.9 = (bf16[1088,256]{1,0:T(8,128)(2,1)S(1)}, bf16[1088,256]{1,0:T(8,128)(2,1)S(1)}, u32[]{:S(2)}, u32[]{:S(2)}) collective-permute-start(bf16[1088,256]{1,0:T(8,128)(2,1)S(1)} %bitcast.18), channel_id=1, source_target_pairs={{0,12},{1,13},{2,14},{3,15},{4,0},{5,1},{6,2},{7,3},{8,4},{9,5},{1... | collective-permute-start | bytes 1671176 | tf_op jit(solution)/shard_map/ppermute | solution.py:383
  70.1 13.0 %collective-permute-start.8 = (bf16[1088,256]{1,0:T(8,128)(2,1)S(1)}, bf16[1088,256]{1,0:T(8,128)(2,1)S(1)}, u32[]{:S(2)}, u32[]{:S(2)}) collective-permute-start(bf16[1088,256]{1,0:T(8,128)(2,1)S(1)} %bitcast.19), channel_id=1, source_target_pairs={{0,8},{1,9},{2,10},{3,11},{4,12},{5,13},{6,14},{7,15},{8,0},{9,1},... | collective-permute-start | bytes 1671176 | tf_op jit(solution)/shard_map/ppermute | solution.py:383
  73.2 15.8 %collective-permute-start.7 = (bf16[1088,256]{1,0:T(8,128)(2,1)S(1)}, bf16[1088,256]{1,0:T(8,128)(2,1)S(1)}, u32[]{:S(2)}, u32[]{:S(2)}) collective-permute-start(bf16[1088,256]{1,0:T(8,128)(2,1)S(1)} %bitcast.20), channel_id=1, source_target_pairs={{0,4},{1,5},{2,6},{3,7},{4,8},{5,9},{6,10},{7,11},{8,12},{9,13},{1... | collective-permute-start | bytes 1671176 | tf_op jit(solution)/shard_map/ppermute | solution.py:383
  76.3 2.6 %collective-permute-start.5 = (f32[136,256]{1,0:T(8,128)S(1)}, f32[136,256]{1,0:T(8,128)S(1)}, u32[]{:S(2)}, u32[]{:S(2)}) collective-permute-start(f32[136,256]{1,0:T(8,128)S(1)} %get-tuple-element.21), channel_id=1, source_target_pairs={{16,0},{32,16},{48,32},{64,48},{80,64},{96,80},{112,96},{128,112},... | collective-permute-start | bytes 417800 | tf_op jit(solution)/shard_map/ppermute | solution.py:362
  76.4 5.7 %collective-permute-start.6 = (f32[136,256]{1,0:T(8,128)S(1)}, f32[136,256]{1,0:T(8,128)S(1)}, u32[]{:S(2)}, u32[]{:S(2)}) collective-permute-start(f32[136,256]{1,0:T(8,128)S(1)} %get-tuple-element.22), channel_id=1, source_target_pairs={{0,16},{16,32},{32,48},{48,64},{64,80},{80,96},{96,112},{112,128},... | collective-permute-start | bytes 417800 | tf_op jit(solution)/shard_map/ppermute | solution.py:362

commit v6 on v5

--- a/solution.py
+++ b/solution.py
@@ -138,9 +138,11 @@
     high_ref[8 * m : 8 * m + 8, :] = s[8:16]
 
 
-def copies_kernel(state_ref, copies_ref):
-    for m in range(Q):
-        rounded = load_state(state_ref, m).astype(BF16)
+def copies_kernel(state_ref, copies_ref, low_ref, high_ref):
+    for m in range(Q):
+        s = load_state(state_ref, m)
+        store_sides(m, s, low_ref, high_ref)
+        rounded = s.astype(BF16)
         for part in range(SIDE):
             copies_ref[part * NODES + Q * m : part * NODES + Q * m + Q, :] = rounded
 
@@ -154,11 +156,8 @@
 
 
 def prepare_kernel(
-    cols_ref, place_ref, z_ref, state_ref, weight_ref, tiles_ref,
-    low_ref, high_ref, dense_ref, wk_out_ref, wk_ref, sem,
+    cols_ref, place_ref, z_ref, weight_ref, tiles_ref, dense_ref, wk_out_ref, wk_ref, sem
 ):
-    for m in range(Q):
-        store_sides(m, load_state(state_ref, m), low_ref, high_ref)
     invariants, base, phi = weights_rows(z_ref[0], weight_ref[...])
     padded = jnp.concatenate([phi, jnp.zeros((TILE - 8 * GROUPS, NODES), F32)], axis=0)
     small = lax.dot_general(
@@ -392,14 +391,14 @@
     place = jnp.stack([lax.axis_index("gx") % 2, vert // SIDE, vert % SIDE]).astype(jnp.int32)
     wk_rows = (2 * PARTS + 1, 8, TILE)
     dma = pltpu.SemaphoreType.DMA
-    (copies,) = call(copies_kernel, [], [state], [((SIDE * NODES, CELLS), BF16)])
+    copies, low, high = call(
+        copies_kernel, [], [state],
+        [((SIDE * NODES, CELLS), BF16), ((half, CELLS), F32), ((half, CELLS), F32)],
+    )
     bundles = gather(copies)
-    low, high, dense, wk = call(
-        prepare_kernel, [tile_cols, place, z_speed], [state, weight, kernel_tiles],
-        [
-            ((half, CELLS), F32), ((half, CELLS), F32), ((NODES, PARTS * NODES), BF16), (wk_rows, F32),
-        ],
-        [pltpu.VMEM(wk_rows, F32), dma], (3,),
+    dense, wk = call(
+        prepare_kernel, [tile_cols, place, z_speed], [weight, kernel_tiles],
+        [((NODES, PARTS * NODES), BF16), (wk_rows, F32)], [pltpu.VMEM(wk_rows, F32), dma], (1,),
     )
     above, below = sides(low, high)
     (base,) = call(

time: 90.8 us -> 87.3 us (0.961)
  waiting for transfers between devices: 17.4 us -> 13 us
  local copies, waits for them, and re-layouts: 2.33 us -> 3.46 us
    ppermute x6, waiting for transfers between devices: 6.6 us -> 3.04 us  [gather(): return [bundle] + [lax.ppermute(bundle, axes, p) for p in pairs]]
    unnamed x14 -> x12, local copies, waits for them, and re-layouts: 2.33 us -> 3.46 us
  transfers between devices with their start and end apart: 10 -> 10, of which waited for: 6 -> 4; matrix products, arithmetic and copies ran while one was open for 0% -> 0% of each run, Pallas kernels for 3% -> 3%
where the time goes in v6:
time: 87.3 us; the launch traced here: 86.9 us
  blocking collectives  40.6 us (47%)
  starting transfers between devices  23.1 us (26%)
  waiting for transfers between devices  13 us (15%)
  Pallas kernels  6.5 us (7%)
  local copies, waits for them, and re-layouts  3.46 us (4%)
    all_to_all x2, blocking collectives, gather(): lax.all_to_all(copies, axes, 0, 0, axis_index_groups=groups, tiled=True)  28.2 us
    ppermute x6, starting transfers between devices, gather(): return [bundle] + [lax.ppermute(bundle, axes, p) for p in pairs]  15.8 us
    all_to_all x1, blocking collectives, spread(): return lax.all_to_all(copies, 'vert', 0, 0, tiled=True)  12.4 us
    ppermute x4, waiting for transfers between devices, sides(): return (lax.ppermute(low, 'gx', down), lax.ppermute(high, 'gx', up))  9.98 us
    ppermute x4, starting transfers between devices, sides(): return (lax.ppermute(low, 'gx', down), lax.ppermute(high, 'gx', up))  7.34 us
    pallas_call x8, Pallas kernels, call(): pl.pallas_call(kernel, out_shape=[(pltpu.HBM if i in in_hbm else jax.Shap...  6.5 us
    unnamed x12, local copies, waits for them, and re-layouts  3.46 us
    ppermute x6, waiting for transfers between devices, gather(): return [bundle] + [lax.ppermute(bundle, axes, p) for p in pairs]  3.04 us
  transfers between devices with their start and end apart: 10, of which 4 were waited for; matrix products, arithmetic and copies ran while one was open for 0% of the time, Pallas kernels for 3%

profile of v6, /device:TPU:2, one launch (start us, length us, event | category | flops | bytes accessed | tf_op | source)
XLA Modules:
  0.0 86.9 jit_solution(15295244492142106379)
XLA Ops:
  0.0 0.0 copy-start.4
  0.0 0.0 copy-start
  0.0 1.0 %copy-done = f32[256,1,256]{2,1,0:T(1,128)S(1)} copy-done((f32[256,1,256]{2,1,0:T(1,128)S(1)}, f32[256,1,256]{2,1,0:T(1,128)}, u32[]{:S(2)}) %copy-start) | copy-done | bytes 262168
  1.0 0.0 copy-start.1
  1.0 0.1 shard_map.56
  1.0 15.1 %all_to_all.33 = bf16[4,256,256]{2,1,0:T(8,128)(2,1)S(1)} all-to-all(bf16[4,256,256]{2,1,0:T(8,128)(2,1)S(1)} %bitcast.26), channel_id=1, replica_groups={{0,1,2,3},{4,5,6,7},{8,9,10,11},{12,13,14,15},{16,20,24,28},{17,21,25,2..., dimensions={0} | all-to-all | bytes 1048576 | tf_op jit(solution)/shard_map/all_to_all | solution.py:381
  16.1 1.9 %collective-permute-start.4 = (bf16[1024,256]{1,0:T(8,128)(2,1)S(1)}, bf16[1024,256]{1,0:T(8,128)(2,1)S(1)}, u32[]{:S(2)}, u32[]{:S(2)}) collective-permute-start(bf16[1024,256]{1,0:T(8,128)(2,1)S(1)} %bitcast.20), channel_id=1, source_target_pairs={{0,12},{1,13},{2,14},{3,15},{4,0},{5,1},{6,2},{7,3},{8,4},{9,5},{1... | collective-permute-start | bytes 1572872 | tf_op jit(solution)/shard_map/ppermute | solution.py:382
  18.0 1.9 %collective-permute-start.3 = (bf16[1024,256]{1,0:T(8,128)(2,1)S(1)}, bf16[1024,256]{1,0:T(8,128)(2,1)S(1)}, u32[]{:S(2)}, u32[]{:S(2)}) collective-permute-start(bf16[1024,256]{1,0:T(8,128)(2,1)S(1)} %bitcast.21), channel_id=1, source_target_pairs={{0,8},{1,9},{2,10},{3,11},{4,12},{5,13},{6,14},{7,15},{8,0},{9,1},... | collective-permute-start | bytes 1572872 | tf_op jit(solution)/shard_map/ppermute | solution.py:382
  19.9 3.9 %collective-permute-start.2 = (bf16[1024,256]{1,0:T(8,128)(2,1)S(1)}, bf16[1024,256]{1,0:T(8,128)(2,1)S(1)}, u32[]{:S(2)}, u32[]{:S(2)}) collective-permute-start(bf16[1024,256]{1,0:T(8,128)(2,1)S(1)} %bitcast.22), channel_id=1, source_target_pairs={{0,4},{1,5},{2,6},{3,7},{4,8},{5,9},{6,10},{7,11},{8,12},{9,13},{1... | collective-permute-start | bytes 1572872 | tf_op jit(solution)/shard_map/ppermute | solution.py:382
  23.9 6.8 %collective-permute-start = (f32[128,256]{1,0:T(8,128)S(1)}, f32[128,256]{1,0:T(8,128)S(1)}, u32[]{:S(2)}, u32[]{:S(2)}) collective-permute-start(f32[128,256]{1,0:T(8,128)S(1)} %get-tuple-element.16), channel_id=1, source_target_pairs={{16,0},{32,16},{48,32},{64,48},{80,64},{96,80},{112,96},{128,112},... | collective-permute-start | bytes 393224 | tf_op jit(solution)/shard_map/ppermute | solution.py:361
  30.7 0.0 collective-permute-start.1
  30.7 0.1 pad_add_fusion.place_ref
  30.8 0.0 copy-start.2
  30.8 1.1 %copy-done.2 = bf16[2,128,1536]{2,1,0:T(8,128)(2,1)S(1)} copy-done((bf16[2,128,1536]{2,1,0:T(8,128)(2,1)S(1)}, bf16[2,128,1536]{2,1,0:T(8,128)(2,1)}, u32[]{:S(2)}) %copy-start.2) | copy-done | bytes 786456
  31.9 0.0 copy-start.3
  31.9 0.7 copy-done.3
  32.6 0.0 copy-start.5
  32.6 0.7 copy-done.5
  33.2 1.8 %shard_map.55 = (bf16[256,4096]{1,0:T(8,128)(2,1)S(1)}, f32[33,8,128]{2,1,0:T(8,128)}) custom-call(s32[2,12]{1,0:T(2,128)S(1)} %copy-done.5, s32[3]{0:T(128)S(1)} %pad_add_fusion.place_ref, f32[1]{0:T(128)} %bitcast.3.z_ref, f32[1,256]{1,0:T(1,128)S(1)} %bitcast.28, bf16[2,128,1536]{2,1,0:T(8,128)(2,1)S(1)} %copy-done.2), custom_call_target="tpu_custom_call" | custom-call | tf_op jit(solution)/shard_map/pallas_call | solution.py:345
  35.1 0.0 collective-permute-done.above_ref
  35.1 1.2 %collective-permute-done.1.below_ref = f32[128,256]{1,0:T(8,128)S(1)} collective-permute-done((f32[128,256]{1,0:T(8,128)S(1)}, f32[128,256]{1,0:T(8,128)S(1)}, u32[]{:S(2)}, u32[]{:S(2)}) %collective-permute-start.1) | collective-permute-done | bytes 131104 | tf_op jit(solution)/shard_map/ppermute | solution.py:361
  36.3 0.0 copy-done.4
  36.3 0.0 copy-done.1
  36.3 0.3 shard_map.57.base_ref
  36.6 0.0 collective-permute-done.4.back_ref
  36.6 0.0 collective-permute-done.3.far_ref
  36.6 0.0 collective-permute-done.2.near_ref
  36.6 1.3 %shard_map.58 = (f32[272,256]{1,0:T(8,128)S(1)}, f32[384,256]{1,0:T(8,128)S(1)}) custom-call(bf16[256,4096]{1,0:T(8,128)(2,1)S(1)} %get-tuple-element.15.dense_ref, f32[264,256]{1,0:T(8,128)S(1)} %shard_map.57.base_ref, bf16[1024,256]{1,0:T(8,128)(2,1)S(1)} %bitcast.23, bf16[1024,256]{1,0:T(8,128)(2,1)S(1)} %collective-permute-done.2.near_ref, ...), custom_call_target="tpu_custom_call" | custom-call | tf_op jit(solution)/shard_map/pallas_call | solution.py:345
  37.9 12.4 %all_to_all.34 = f32[16,24,256]{2,1,0:T(8,128)S(1)} all-to-all(f32[16,24,256]{2,1,0:T(8,128)S(1)} %bitcast.27), channel_id=1, replica_groups=mesh['gx'=32,'vert'=16] {'vert'}, dimensions={0} | all-to-all | bytes 786432 | tf_op jit(solution)/shard_map/all_to_all | solution.py:365
  50.3 0.7 shard_map.61
  51.0 13.1 %all_to_all.35 = bf16[4,272,256]{2,1,0:T(8,128)(2,1)S(1)} all-to-all(bf16[4,272,256]{2,1,0:T(8,128)(2,1)S(1)} %bitcast.19), channel_id=1, replica_groups={{0,1,2,3},{4,5,6,7},{8,9,10,11},{12,13,14,15},{16,20,24,28},{17,21,25,2..., dimensions={0} | all-to-all | bytes 1114112 | tf_op jit(solution)/shard_map/all_to_all | solution.py:381
  64.1 2.4 %collective-permute-start.9 = (bf16[1088,256]{1,0:T(8,128)(2,1)S(1)}, bf16[1088,256]{1,0:T(8,128)(2,1)S(1)}, u32[]{:S(2)}, u32[]{:S(2)}) collective-permute-start(bf16[1088,256]{1,0:T(8,128)(2,1)S(1)} %bitcast.15), channel_id=1, source_target_pairs={{0,12},{1,13},{2,14},{3,15},{4,0},{5,1},{6,2},{7,3},{8,4},{9,5},{1... | collective-permute-start | bytes 1671176 | tf_op jit(solution)/shard_map/ppermute | solution.py:382
  66.5 3.1 %collective-permute-start.8 = (bf16[1088,256]{1,0:T(8,128)(2,1)S(1)}, bf16[1088,256]{1,0:T(8,128)(2,1)S(1)}, u32[]{:S(2)}, u32[]{:S(2)}) collective-permute-start(bf16[1088,256]{1,0:T(8,128)(2,1)S(1)} %bitcast.16), channel_id=1, source_target_pairs={{0,8},{1,9},{2,10},{3,11},{4,12},{5,13},{6,14},{7,15},{8,0},{9,1},... | collective-permute-start | bytes 1671176 | tf_op jit(solution)/shard_map/ppermute | solution.py:382
  69.6 2.5 %collective-permute-start.7 = (bf16[1088,256]{1,0:T(8,128)(2,1)S(1)}, bf16[1088,256]{1,0:T(8,128)(2,1)S(1)}, u32[]{:S(2)}, u32[]{:S(2)}) collective-permute-start(bf16[1088,256]{1,0:T(8,128)(2,1)S(1)} %bitcast.17), channel_id=1, source_target_pairs={{0,4},{1,5},{2,6},{3,7},{4,8},{5,9},{6,10},{7,11},{8,12},{9,13},{1... | collective-permute-start | bytes 1671176 | tf_op jit(solution)/shard_map/ppermute | solution.py:382
  72.2 0.6 shard_map.59
  72.8 0.4 collective-permute-start.5
  73.2 0.2 collective-permute-start.6
  73.3 2.4 %collective-permute-done.5.above_ref = f32[136,256]{1,0:T(8,128)S(1)} collective-permute-done((f32[136,256]{1,0:T(8,128)S(1)}, f32[136,256]{1,0:T(8,128)S(1)}, u32[]{:S(2)}, u32[]{:S(2)}) %collective-permute-start.5) | collective-permute-done | bytes 139296 | tf_op jit(solution)/shard_map/ppermute | solution.py:361
  75.8 6.3 %collective-permute-done.6.below_ref = f32[136,256]{1,0:T(8,128)S(1)} collective-permute-done((f32[136,256]{1,0:T(8,128)S(1)}, f32[136,256]{1,0:T(8,128)S(1)}, u32[]{:S(2)}, u32[]{:S(2)}) %collective-permute-start.6) | collective-permute-done | bytes 139296 | tf_op jit(solution)/shard_map/ppermute | solution.py:361
  82.1 0.3 shard_map.60.base_ref
  82.4 0.0 collective-permute-done.9.back_ref
  82.4 0.0 collective-permute-done.8.far_ref
  82.4 3.0 %collective-permute-done.7.near_ref = bf16[1088,256]{1,0:T(8,128)(2,1)S(1)} collective-permute-done((bf16[1088,256]{1,0:T(8,128)(2,1)S(1)}, bf16[1088,256]{1,0:T(8,128)(2,1)S(1)}, u32[]{:S(2)}, u32[]{:S(2)}) %collective-permute-start.7) | collective-permute-done | bytes 557088 | tf_op jit(solution)/shard_map/ppermute | solution.py:382
  85.4 1.4 %shard_map.62 = f32[512,128]{1,0:T(8,128)} custom-call(bf16[256,4096]{1,0:T(8,128)(2,1)S(1)} %get-tuple-element.15.dense_ref, f32[280,256]{1,0:T(8,128)S(1)} %shard_map.60.base_ref, bf16[1088,256]{1,0:T(8,128)(2,1)S(1)} %bitcast.18, bf16[1088,256]{1,0:T(8,128)(2,1)S(1)} %collective-permute-done.7.near_ref, ...), custom_call_target="tpu_custom_call" | custom-call | tf_op jit(solution)/shard_map/pallas_call | solution.py:345
Async XLA Ops:
  0.0 36.3 %copy-start.4 = (f32[1,256]{1,0:T(1,128)S(1)}, f32[1,256]{1,0:T(1,128)}, u32[]{:S(2)}) copy-start(f32[1,256]{1,0:T(1,128)} %rate_ref.3) | copy-start | bytes 3076
  0.0 1.0 %copy-start = (f32[256,1,256]{2,1,0:T(1,128)S(1)}, f32[256,1,256]{2,1,0:T(1,128)}, u32[]{:S(2)}) copy-start(f32[256,1,256]{2,1,0:T(1,128)} %param.5) | copy-start | bytes 786436
  1.0 35.3 %copy-start.1 = (f32[256,1,256]{2,1,0:T(1,128)S(1)}, f32[256,1,256]{2,1,0:T(1,128)}, u32[]{:S(2)}) copy-start(f32[256,1,256]{2,1,0:T(1,128)} %param.5) | copy-start | bytes 786436
  16.1 20.5 %collective-permute-start.4 = (bf16[1024,256]{1,0:T(8,128)(2,1)S(1)}, bf16[1024,256]{1,0:T(8,128)(2,1)S(1)}, u32[]{:S(2)}, u32[]{:S(2)}) collective-permute-start(bf16[1024,256]{1,0:T(8,128)(2,1)S(1)} %bitcast.20), channel_id=1, source_target_pairs={{0,12},{1,13},{2,14},{3,15},{4,0},{5,1},{6,2},{7,3},{8,4},{9,5},{1... | collective-permute-start | bytes 1572872 | tf_op jit(solution)/shard_map/ppermute | solution.py:382
  18.0 18.6 %collective-permute-start.3 = (bf16[1024,256]{1,0:T(8,128)(2,1)S(1)}, bf16[1024,256]{1,0:T(8,128)(2,1)S(1)}, u32[]{:S(2)}, u32[]{:S(2)}) collective-permute-start(bf16[1024,256]{1,0:T(8,128)(2,1)S(1)} %bitcast.21), channel_id=1, source_target_pairs={{0,8},{1,9},{2,10},{3,11},{4,12},{5,13},{6,14},{7,15},{8,0},{9,1},... | collective-permute-start | bytes 1572872 | tf_op jit(solution)/shard_map/ppermute | solution.py:382
  19.9 16.7 %collective-permute-start.2 = (bf16[1024,256]{1,0:T(8,128)(2,1)S(1)}, bf16[1024,256]{1,0:T(8,128)(2,1)S(1)}, u32[]{:S(2)}, u32[]{:S(2)}) collective-permute-start(bf16[1024,256]{1,0:T(8,128)(2,1)S(1)} %bitcast.22), channel_id=1, source_target_pairs={{0,4},{1,5},{2,6},{3,7},{4,8},{5,9},{6,10},{7,11},{8,12},{9,13},{1... | collective-permute-start | bytes 1572872 | tf_op jit(solution)/shard_map/ppermute | solution.py:382
  23.9 11.2 %collective-permute-start = (f32[128,256]{1,0:T(8,128)S(1)}, f32[128,256]{1,0:T(8,128)S(1)}, u32[]{:S(2)}, u32[]{:S(2)}) collective-permute-start(f32[128,256]{1,0:T(8,128)S(1)} %get-tuple-element.16), channel_id=1, source_target_pairs={{16,0},{32,16},{48,32},{64,48},{80,64},{96,80},{112,96},{128,112},... | collective-permute-start | bytes 393224 | tf_op jit(solution)/shard_map/ppermute | solution.py:361
  30.7 5.6 %collective-permute-start.1 = (f32[128,256]{1,0:T(8,128)S(1)}, f32[128,256]{1,0:T(8,128)S(1)}, u32[]{:S(2)}, u32[]{:S(2)}) collective-permute-start(f32[128,256]{1,0:T(8,128)S(1)} %get-tuple-element.17), channel_id=1, source_target_pairs={{0,16},{16,32},{32,48},{48,64},{64,80},{80,96},{96,112},{112,128},... | collective-permute-start | bytes 393224 | tf_op jit(solution)/shard_map/ppermute | solution.py:361
  30.8 1.1 %copy-start.2 = (bf16[2,128,1536]{2,1,0:T(8,128)(2,1)S(1)}, bf16[2,128,1536]{2,1,0:T(8,128)(2,1)}, u32[]{:S(2)}) copy-start(bf16[2,128,1536]{2,1,0:T(8,128)(2,1)} %tiles_ref.1) | copy-start | bytes 2359300
  31.9 0.7 copy-start.3
  32.6 0.7 copy-start.5
  64.1 18.3 %collective-permute-start.9 = (bf16[1088,256]{1,0:T(8,128)(2,1)S(1)}, bf16[1088,256]{1,0:T(8,128)(2,1)S(1)}, u32[]{:S(2)}, u32[]{:S(2)}) collective-permute-start(bf16[1088,256]{1,0:T(8,128)(2,1)S(1)} %bitcast.15), channel_id=1, source_target_pairs={{0,12},{1,13},{2,14},{3,15},{4,0},{5,1},{6,2},{7,3},{8,4},{9,5},{1... | collective-permute-start | bytes 1671176 | tf_op jit(solution)/shard_map/ppermute | solution.py:382
  66.5 15.9 %collective-permute-start.8 = (bf16[1088,256]{1,0:T(8,128)(2,1)S(1)}, bf16[1088,256]{1,0:T(8,128)(2,1)S(1)}, u32[]{:S(2)}, u32[]{:S(2)}) collective-permute-start(bf16[1088,256]{1,0:T(8,128)(2,1)S(1)} %bitcast.16), channel_id=1, source_target_pairs={{0,8},{1,9},{2,10},{3,11},{4,12},{5,13},{6,14},{7,15},{8,0},{9,1},... | collective-permute-start | bytes 1671176 | tf_op jit(solution)/shard_map/ppermute | solution.py:382
  69.6 15.8 %collective-permute-start.7 = (bf16[1088,256]{1,0:T(8,128)(2,1)S(1)}, bf16[1088,256]{1,0:T(8,128)(2,1)S(1)}, u32[]{:S(2)}, u32[]{:S(2)}) collective-permute-start(bf16[1088,256]{1,0:T(8,128)(2,1)S(1)} %bitcast.17), channel_id=1, source_target_pairs={{0,4},{1,5},{2,6},{3,7},{4,8},{5,9},{6,10},{7,11},{8,12},{9,13},{1... | collective-permute-start | bytes 1671176 | tf_op jit(solution)/shard_map/ppermute | solution.py:382
  72.8 3.0 %collective-permute-start.5 = (f32[136,256]{1,0:T(8,128)S(1)}, f32[136,256]{1,0:T(8,128)S(1)}, u32[]{:S(2)}, u32[]{:S(2)}) collective-permute-start(f32[136,256]{1,0:T(8,128)S(1)} %get-tuple-element.23), channel_id=1, source_target_pairs={{16,0},{32,16},{48,32},{64,48},{80,64},{96,80},{112,96},{128,112},... | collective-permute-start | bytes 417800 | tf_op jit(solution)/shard_map/ppermute | solution.py:361
  73.2 8.9 %collective-permute-start.6 = (f32[136,256]{1,0:T(8,128)S(1)}, f32[136,256]{1,0:T(8,128)S(1)}, u32[]{:S(2)}, u32[]{:S(2)}) collective-permute-start(f32[136,256]{1,0:T(8,128)S(1)} %get-tuple-element.24), channel_id=1, source_target_pairs={{0,16},{16,32},{32,48},{48,64},{64,80},{80,96},{96,112},{112,128},... | collective-permute-start | bytes 417800 | tf_op jit(solution)/shard_map/ppermute | solution.py:361

commit v7 on v6

--- a/solution.py
+++ b/solution.py
@@ -370,12 +370,12 @@
     groups, pairs = [], [[], [], []]
     for g in range(slabs):
         for i in range(SIDE):
-            line = [i * SIDE + j if g % 2 == 0 else j * SIDE + i for j in range(SIDE)]
+            line = [i * SIDE + j if g % 2 == 1 else j * SIDE + i for j in range(SIDE)]
             groups.append([g * PARTS + v for v in line])
             for j in range(SIDE):
                 for shift in (1, 2, 3):
                     y, x = (i + shift) % SIDE, j
-                    ends = (i * SIDE + j, y * SIDE + x) if g % 2 == 0 else (j * SIDE + i, x * SIDE + y)
+                    ends = (i * SIDE + j, y * SIDE + x) if g % 2 == 1 else (j * SIDE + i, x * SIDE + y)
                     pairs[shift - 1].append(tuple(g * PARTS + v for v in ends))
     axes = ("gx", "vert")
     bundle = lax.all_to_all(copies, axes, 0, 0, axis_index_groups=groups, tiled=True)
@@ -388,7 +388,7 @@
     z_speed = speed_of(lax.axis_index("vert")).reshape(1)
     half = NODES // 2
     vert = lax.axis_index("vert")
-    place = jnp.stack([lax.axis_index("gx") % 2, vert // SIDE, vert % SIDE]).astype(jnp.int32)
+    place = jnp.stack([1 - lax.axis_index("gx") % 2, vert // SIDE, vert % SIDE]).astype(jnp.int32)
     wk_rows = (2 * PARTS + 1, 8, TILE)
     dma = pltpu.SemaphoreType.DMA
     copies, low, high = call(

time: 87.3 us -> 86.9 us (level)
  the two profiles are of different devices: /device:TPU:2 before, /device:TPU:8 now
where the time goes in v7:
time: 86.9 us; the launch traced here: 86.5 us
  blocking collectives  40.3 us (46%)
  starting transfers between devices  23.6 us (27%)
  waiting for transfers between devices  12.4 us (14%)
  Pallas kernels  6.5 us (7%)
  local copies, waits for them, and re-layouts  3.46 us (4%)
    all_to_all x2, blocking collectives, gather(): lax.all_to_all(copies, axes, 0, 0, axis_index_groups=groups, tiled=True)  28.8 us
    ppermute x6, starting transfers between devices, gather(): return [bundle] + [lax.ppermute(bundle, axes, p) for p in pairs]  16.1 us
    all_to_all x1, blocking collectives, spread(): return lax.all_to_all(copies, 'vert', 0, 0, tiled=True)  11.5 us
    ppermute x4, waiting for transfers between devices, sides(): return (lax.ppermute(low, 'gx', down), lax.ppermute(high, 'gx', up))  9.75 us
    ppermute x4, starting transfers between devices, sides(): return (lax.ppermute(low, 'gx', down), lax.ppermute(high, 'gx', up))  7.46 us
    pallas_call x8, Pallas kernels, call(): pl.pallas_call(kernel, out_shape=[(pltpu.HBM if i in in_hbm else jax.Shap...  6.5 us
    unnamed x12, local copies, waits for them, and re-layouts  3.46 us
    ppermute x6, waiting for transfers between devices, gather(): return [bundle] + [lax.ppermute(bundle, axes, p) for p in pairs]  2.63 us
  transfers between devices with their start and end apart: 10, of which 4 were waited for; matrix products, arithmetic and copies ran while one was open for 0% of the time, Pallas kernels for 3%

profile of v7, /device:TPU:8, one launch (start us, length us, event | category | flops | bytes accessed | tf_op | source)
XLA Modules:
  0.0 86.5 jit_solution(6057252904581912227)
XLA Ops:
  0.0 0.0 copy-start.4
  0.0 0.0 copy-start
  0.0 1.0 %copy-done = f32[256,1,256]{2,1,0:T(1,128)S(1)} copy-done((f32[256,1,256]{2,1,0:T(1,128)S(1)}, f32[256,1,256]{2,1,0:T(1,128)}, u32[]{:S(2)}) %copy-start) | copy-done | bytes 262168
  1.0 0.0 copy-start.1
  1.0 0.1 shard_map.56
  1.0 15.0 %all_to_all.33 = bf16[4,256,256]{2,1,0:T(8,128)(2,1)S(1)} all-to-all(bf16[4,256,256]{2,1,0:T(8,128)(2,1)S(1)} %bitcast.26), channel_id=1, replica_groups={{0,4,8,12},{1,5,9,13},{2,6,10,14},{3,7,11,15},{16,17,18,19},{20,21,22,2..., dimensions={0} | all-to-all | bytes 1048576 | tf_op jit(solution)/shard_map/all_to_all | solution.py:381
  16.0 1.9 %collective-permute-start.4 = (bf16[1024,256]{1,0:T(8,128)(2,1)S(1)}, bf16[1024,256]{1,0:T(8,128)(2,1)S(1)}, u32[]{:S(2)}, u32[]{:S(2)}) collective-permute-start(bf16[1024,256]{1,0:T(8,128)(2,1)S(1)} %bitcast.20), channel_id=1, source_target_pairs={{0,3},{4,7},{8,11},{12,15},{1,0},{5,4},{9,8},{13,12},{2,1},{6,5},{... | collective-permute-start | bytes 1572872 | tf_op jit(solution)/shard_map/ppermute | solution.py:382
  17.9 1.9 %collective-permute-start.3 = (bf16[1024,256]{1,0:T(8,128)(2,1)S(1)}, bf16[1024,256]{1,0:T(8,128)(2,1)S(1)}, u32[]{:S(2)}, u32[]{:S(2)}) collective-permute-start(bf16[1024,256]{1,0:T(8,128)(2,1)S(1)} %bitcast.21), channel_id=1, source_target_pairs={{0,2},{4,6},{8,10},{12,14},{1,3},{5,7},{9,11},{13,15},{2,0},{6,4},... | collective-permute-start | bytes 1572872 | tf_op jit(solution)/shard_map/ppermute | solution.py:382
  19.9 3.9 %collective-permute-start.2 = (bf16[1024,256]{1,0:T(8,128)(2,1)S(1)}, bf16[1024,256]{1,0:T(8,128)(2,1)S(1)}, u32[]{:S(2)}, u32[]{:S(2)}) collective-permute-start(bf16[1024,256]{1,0:T(8,128)(2,1)S(1)} %bitcast.22), channel_id=1, source_target_pairs={{0,1},{4,5},{8,9},{12,13},{1,2},{5,6},{9,10},{13,14},{2,3},{6,7},{... | collective-permute-start | bytes 1572872 | tf_op jit(solution)/shard_map/ppermute | solution.py:382
  23.8 6.9 %collective-permute-start = (f32[128,256]{1,0:T(8,128)S(1)}, f32[128,256]{1,0:T(8,128)S(1)}, u32[]{:S(2)}, u32[]{:S(2)}) collective-permute-start(f32[128,256]{1,0:T(8,128)S(1)} %get-tuple-element.16), channel_id=1, source_target_pairs={{16,0},{32,16},{48,32},{64,48},{80,64},{96,80},{112,96},{128,112},... | collective-permute-start | bytes 393224 | tf_op jit(solution)/shard_map/ppermute | solution.py:361
  30.7 0.0 collective-permute-start.1
  30.7 0.1 pad_add_fusion.place_ref
  30.8 0.0 copy-start.2
  30.8 1.1 %copy-done.2 = bf16[2,128,1536]{2,1,0:T(8,128)(2,1)S(1)} copy-done((bf16[2,128,1536]{2,1,0:T(8,128)(2,1)S(1)}, bf16[2,128,1536]{2,1,0:T(8,128)(2,1)}, u32[]{:S(2)}) %copy-start.2) | copy-done | bytes 786456
  31.9 0.0 copy-start.3
  31.9 0.7 copy-done.3
  32.6 0.0 copy-start.5
  32.6 0.7 copy-done.5
  33.3 1.8 %shard_map.55 = (bf16[256,4096]{1,0:T(8,128)(2,1)S(1)}, f32[33,8,128]{2,1,0:T(8,128)}) custom-call(s32[2,12]{1,0:T(2,128)S(1)} %copy-done.5, s32[3]{0:T(128)S(1)} %pad_add_fusion.place_ref, f32[1]{0:T(128)} %bitcast.3.z_ref, f32[1,256]{1,0:T(1,128)S(1)} %bitcast.28, bf16[2,128,1536]{2,1,0:T(8,128)(2,1)S(1)} %copy-done.2), custom_call_target="tpu_custom_call" | custom-call | tf_op jit(solution)/shard_map/pallas_call | solution.py:345
  35.1 0.0 collective-permute-done.above_ref
  35.1 1.2 %collective-permute-done.1.below_ref = f32[128,256]{1,0:T(8,128)S(1)} collective-permute-done((f32[128,256]{1,0:T(8,128)S(1)}, f32[128,256]{1,0:T(8,128)S(1)}, u32[]{:S(2)}, u32[]{:S(2)}) %collective-permute-start.1) | collective-permute-done | bytes 131104 | tf_op jit(solution)/shard_map/ppermute | solution.py:361
  36.3 0.0 copy-done.4
  36.3 0.0 copy-done.1
  36.3 0.3 shard_map.57.base_ref
  36.6 0.0 collective-permute-done.4.back_ref
  36.6 0.0 collective-permute-done.3.far_ref
  36.6 0.0 collective-permute-done.2.near_ref
  36.6 1.3 %shard_map.58 = (f32[272,256]{1,0:T(8,128)S(1)}, f32[384,256]{1,0:T(8,128)S(1)}) custom-call(bf16[256,4096]{1,0:T(8,128)(2,1)S(1)} %get-tuple-element.15.dense_ref, f32[264,256]{1,0:T(8,128)S(1)} %shard_map.57.base_ref, bf16[1024,256]{1,0:T(8,128)(2,1)S(1)} %bitcast.23, bf16[1024,256]{1,0:T(8,128)(2,1)S(1)} %collective-permute-done.2.near_ref, ...), custom_call_target="tpu_custom_call" | custom-call | tf_op jit(solution)/shard_map/pallas_call | solution.py:345
  37.9 11.5 %all_to_all.34 = f32[16,24,256]{2,1,0:T(8,128)S(1)} all-to-all(f32[16,24,256]{2,1,0:T(8,128)S(1)} %bitcast.27), channel_id=1, replica_groups=mesh['gx'=32,'vert'=16] {'vert'}, dimensions={0} | all-to-all | bytes 786432 | tf_op jit(solution)/shard_map/all_to_all | solution.py:365
  49.4 0.7 shard_map.61
  50.1 13.9 %all_to_all.35 = bf16[4,272,256]{2,1,0:T(8,128)(2,1)S(1)} all-to-all(bf16[4,272,256]{2,1,0:T(8,128)(2,1)S(1)} %bitcast.19), channel_id=1, replica_groups={{0,4,8,12},{1,5,9,13},{2,6,10,14},{3,7,11,15},{16,17,18,19},{20,21,22,2..., dimensions={0} | all-to-all | bytes 1114112 | tf_op jit(solution)/shard_map/all_to_all | solution.py:381
  64.0 2.1 %collective-permute-start.9 = (bf16[1088,256]{1,0:T(8,128)(2,1)S(1)}, bf16[1088,256]{1,0:T(8,128)(2,1)S(1)}, u32[]{:S(2)}, u32[]{:S(2)}) collective-permute-start(bf16[1088,256]{1,0:T(8,128)(2,1)S(1)} %bitcast.15), channel_id=1, source_target_pairs={{0,3},{4,7},{8,11},{12,15},{1,0},{5,4},{9,8},{13,12},{2,1},{6,5},{... | collective-permute-start | bytes 1671176 | tf_op jit(solution)/shard_map/ppermute | solution.py:382
  66.1 4.3 %collective-permute-start.8 = (bf16[1088,256]{1,0:T(8,128)(2,1)S(1)}, bf16[1088,256]{1,0:T(8,128)(2,1)S(1)}, u32[]{:S(2)}, u32[]{:S(2)}) collective-permute-start(bf16[1088,256]{1,0:T(8,128)(2,1)S(1)} %bitcast.16), channel_id=1, source_target_pairs={{0,2},{4,6},{8,10},{12,14},{1,3},{5,7},{9,11},{13,15},{2,0},{6,4},... | collective-permute-start | bytes 1671176 | tf_op jit(solution)/shard_map/ppermute | solution.py:382
  70.5 1.9 %collective-permute-start.7 = (bf16[1088,256]{1,0:T(8,128)(2,1)S(1)}, bf16[1088,256]{1,0:T(8,128)(2,1)S(1)}, u32[]{:S(2)}, u32[]{:S(2)}) collective-permute-start(bf16[1088,256]{1,0:T(8,128)(2,1)S(1)} %bitcast.17), channel_id=1, source_target_pairs={{0,1},{4,5},{8,9},{12,13},{1,2},{5,6},{9,10},{13,14},{2,3},{6,7},{... | collective-permute-start | bytes 1671176 | tf_op jit(solution)/shard_map/ppermute | solution.py:382
  72.4 0.6 shard_map.59
  73.0 0.5 collective-permute-start.5
  73.5 0.0 collective-permute-start.6
  73.5 2.6 %collective-permute-done.5.above_ref = f32[136,256]{1,0:T(8,128)S(1)} collective-permute-done((f32[136,256]{1,0:T(8,128)S(1)}, f32[136,256]{1,0:T(8,128)S(1)}, u32[]{:S(2)}, u32[]{:S(2)}) %collective-permute-start.5) | collective-permute-done | bytes 139296 | tf_op jit(solution)/shard_map/ppermute | solution.py:361
  76.1 6.0 %collective-permute-done.6.below_ref = f32[136,256]{1,0:T(8,128)S(1)} collective-permute-done((f32[136,256]{1,0:T(8,128)S(1)}, f32[136,256]{1,0:T(8,128)S(1)}, u32[]{:S(2)}, u32[]{:S(2)}) %collective-permute-start.6) | collective-permute-done | bytes 139296 | tf_op jit(solution)/shard_map/ppermute | solution.py:361
  82.1 0.3 shard_map.60.base_ref
  82.4 0.0 collective-permute-done.9.back_ref
  82.4 0.0 collective-permute-done.8.far_ref
  82.4 2.6 %collective-permute-done.7.near_ref = bf16[1088,256]{1,0:T(8,128)(2,1)S(1)} collective-permute-done((bf16[1088,256]{1,0:T(8,128)(2,1)S(1)}, bf16[1088,256]{1,0:T(8,128)(2,1)S(1)}, u32[]{:S(2)}, u32[]{:S(2)}) %collective-permute-start.7) | collective-permute-done | bytes 557088 | tf_op jit(solution)/shard_map/ppermute | solution.py:382
  85.0 1.4 %shard_map.62 = f32[512,128]{1,0:T(8,128)} custom-call(bf16[256,4096]{1,0:T(8,128)(2,1)S(1)} %get-tuple-element.15.dense_ref, f32[280,256]{1,0:T(8,128)S(1)} %shard_map.60.base_ref, bf16[1088,256]{1,0:T(8,128)(2,1)S(1)} %bitcast.18, bf16[1088,256]{1,0:T(8,128)(2,1)S(1)} %collective-permute-done.7.near_ref, ...), custom_call_target="tpu_custom_call" | custom-call | tf_op jit(solution)/shard_map/pallas_call | solution.py:345
Async XLA Ops:
  0.0 36.3 %copy-start.4 = (f32[1,256]{1,0:T(1,128)S(1)}, f32[1,256]{1,0:T(1,128)}, u32[]{:S(2)}) copy-start(f32[1,256]{1,0:T(1,128)} %rate_ref.3) | copy-start | bytes 3076
  0.0 1.0 %copy-start = (f32[256,1,256]{2,1,0:T(1,128)S(1)}, f32[256,1,256]{2,1,0:T(1,128)}, u32[]{:S(2)}) copy-start(f32[256,1,256]{2,1,0:T(1,128)} %param.5) | copy-start | bytes 786436
  1.0 35.4 %copy-start.1 = (f32[256,1,256]{2,1,0:T(1,128)S(1)}, f32[256,1,256]{2,1,0:T(1,128)}, u32[]{:S(2)}) copy-start(f32[256,1,256]{2,1,0:T(1,128)} %param.5) | copy-start | bytes 786436
  16.0 20.6 %collective-permute-start.4 = (bf16[1024,256]{1,0:T(8,128)(2,1)S(1)}, bf16[1024,256]{1,0:T(8,128)(2,1)S(1)}, u32[]{:S(2)}, u32[]{:S(2)}) collective-permute-start(bf16[1024,256]{1,0:T(8,128)(2,1)S(1)} %bitcast.20), channel_id=1, source_target_pairs={{0,3},{4,7},{8,11},{12,15},{1,0},{5,4},{9,8},{13,12},{2,1},{6,5},{... | collective-permute-start | bytes 1572872 | tf_op jit(solution)/shard_map/ppermute | solution.py:382
  17.9 18.7 %collective-permute-start.3 = (bf16[1024,256]{1,0:T(8,128)(2,1)S(1)}, bf16[1024,256]{1,0:T(8,128)(2,1)S(1)}, u32[]{:S(2)}, u32[]{:S(2)}) collective-permute-start(bf16[1024,256]{1,0:T(8,128)(2,1)S(1)} %bitcast.21), channel_id=1, source_target_pairs={{0,2},{4,6},{8,10},{12,14},{1,3},{5,7},{9,11},{13,15},{2,0},{6,4},... | collective-permute-start | bytes 1572872 | tf_op jit(solution)/shard_map/ppermute | solution.py:382
  19.9 16.8 %collective-permute-start.2 = (bf16[1024,256]{1,0:T(8,128)(2,1)S(1)}, bf16[1024,256]{1,0:T(8,128)(2,1)S(1)}, u32[]{:S(2)}, u32[]{:S(2)}) collective-permute-start(bf16[1024,256]{1,0:T(8,128)(2,1)S(1)} %bitcast.22), channel_id=1, source_target_pairs={{0,1},{4,5},{8,9},{12,13},{1,2},{5,6},{9,10},{13,14},{2,3},{6,7},{... | collective-permute-start | bytes 1572872 | tf_op jit(solution)/shard_map/ppermute | solution.py:382
  23.8 11.3 %collective-permute-start = (f32[128,256]{1,0:T(8,128)S(1)}, f32[128,256]{1,0:T(8,128)S(1)}, u32[]{:S(2)}, u32[]{:S(2)}) collective-permute-start(f32[128,256]{1,0:T(8,128)S(1)} %get-tuple-element.16), channel_id=1, source_target_pairs={{16,0},{32,16},{48,32},{64,48},{80,64},{96,80},{112,96},{128,112},... | collective-permute-start | bytes 393224 | tf_op jit(solution)/shard_map/ppermute | solution.py:361
  30.7 5.6 %collective-permute-start.1 = (f32[128,256]{1,0:T(8,128)S(1)}, f32[128,256]{1,0:T(8,128)S(1)}, u32[]{:S(2)}, u32[]{:S(2)}) collective-permute-start(f32[128,256]{1,0:T(8,128)S(1)} %get-tuple-element.17), channel_id=1, source_target_pairs={{0,16},{16,32},{32,48},{48,64},{64,80},{80,96},{96,112},{112,128},... | collective-permute-start | bytes 393224 | tf_op jit(solution)/shard_map/ppermute | solution.py:361
  30.8 1.1 %copy-start.2 = (bf16[2,128,1536]{2,1,0:T(8,128)(2,1)S(1)}, bf16[2,128,1536]{2,1,0:T(8,128)(2,1)}, u32[]{:S(2)}) copy-start(bf16[2,128,1536]{2,1,0:T(8,128)(2,1)} %tiles_ref.1) | copy-start | bytes 2359300
  31.9 0.7 copy-start.3
  32.6 0.7 copy-start.5
  64.0 18.4 %collective-permute-start.9 = (bf16[1088,256]{1,0:T(8,128)(2,1)S(1)}, bf16[1088,256]{1,0:T(8,128)(2,1)S(1)}, u32[]{:S(2)}, u32[]{:S(2)}) collective-permute-start(bf16[1088,256]{1,0:T(8,128)(2,1)S(1)} %bitcast.15), channel_id=1, source_target_pairs={{0,3},{4,7},{8,11},{12,15},{1,0},{5,4},{9,8},{13,12},{2,1},{6,5},{... | collective-permute-start | bytes 1671176 | tf_op jit(solution)/shard_map/ppermute | solution.py:382
  66.1 16.3 %collective-permute-start.8 = (bf16[1088,256]{1,0:T(8,128)(2,1)S(1)}, bf16[1088,256]{1,0:T(8,128)(2,1)S(1)}, u32[]{:S(2)}, u32[]{:S(2)}) collective-permute-start(bf16[1088,256]{1,0:T(8,128)(2,1)S(1)} %bitcast.16), channel_id=1, source_target_pairs={{0,2},{4,6},{8,10},{12,14},{1,3},{5,7},{9,11},{13,15},{2,0},{6,4},... | collective-permute-start | bytes 1671176 | tf_op jit(solution)/shard_map/ppermute | solution.py:382
  70.5 14.6 %collective-permute-start.7 = (bf16[1088,256]{1,0:T(8,128)(2,1)S(1)}, bf16[1088,256]{1,0:T(8,128)(2,1)S(1)}, u32[]{:S(2)}, u32[]{:S(2)}) collective-permute-start(bf16[1088,256]{1,0:T(8,128)(2,1)S(1)} %bitcast.17), channel_id=1, source_target_pairs={{0,1},{4,5},{8,9},{12,13},{1,2},{5,6},{9,10},{13,14},{2,3},{6,7},{... | collective-permute-start | bytes 1671176 | tf_op jit(solution)/shard_map/ppermute | solution.py:382
  73.0 3.1 %collective-permute-start.5 = (f32[136,256]{1,0:T(8,128)S(1)}, f32[136,256]{1,0:T(8,128)S(1)}, u32[]{:S(2)}, u32[]{:S(2)}) collective-permute-start(f32[136,256]{1,0:T(8,128)S(1)} %get-tuple-element.23), channel_id=1, source_target_pairs={{16,0},{32,16},{48,32},{64,48},{80,64},{96,80},{112,96},{128,112},... | collective-permute-start | bytes 417800 | tf_op jit(solution)/shard_map/ppermute | solution.py:361
  73.5 8.6 %collective-permute-start.6 = (f32[136,256]{1,0:T(8,128)S(1)}, f32[136,256]{1,0:T(8,128)S(1)}, u32[]{:S(2)}, u32[]{:S(2)}) collective-permute-start(f32[136,256]{1,0:T(8,128)S(1)} %get-tuple-element.24), channel_id=1, source_target_pairs={{0,16},{16,32},{32,48},{48,64},{64,80},{80,96},{96,112},{112,128},... | collective-permute-start | bytes 417800 | tf_op jit(solution)/shard_map/ppermute | solution.py:361

commit v8 on v7

--- a/solution.py
+++ b/solution.py
@@ -19,6 +19,7 @@
 MIDDLE = (Q - 1) / 2.0
 EXTRA = 16
 PAYLOAD = 24
+OUT_STEP = 4
 SIDE = 4
 GROUPS = 7
 F32 = jnp.float32
@@ -317,7 +318,7 @@
     base_ref[NODES + 16 :, :] = step_rows(rate, z_speed)
 
 
-def last_kernel(dense_ref, base_ref, own_ref, near_ref, far_ref, back_ref, out_ref, term_ref):
+def last_kernel(dense_ref, base_ref, own_ref, near_ref, far_ref, back_ref, out_ref, term_ref, new_ref, sems):
     stride = NODES + EXTRA
     bundles = (own_ref, near_ref, far_ref, back_ref)
     term_ref[...] = kernel_product(dense_ref, bundles, stride)
@@ -328,11 +329,20 @@
             total = total + (own[0:8] + own[8:16])
     rows = base_ref[NODES + 16 :, :]
     coeffs = rows[1:2] * apply_small(base_ref[NODES + 8 : NODES + 16, 0:128], 8, total)
+    copies = []
     for m in range(Q):
         at = slice(Q * m, Q * m + Q)
         new = base_ref[at, :] + rows[0:1] * term_ref[at, :] + equilibrium_rows(m, coeffs, rows[3:4])
         for h in range(2):
-            out_ref[pl.ds(2 * Q * m + h, Q, stride=2), :] = new[:, 128 * h : 128 * h + 128]
+            new_ref[pl.ds(2 * Q * m + h, Q, stride=2), :] = new[:, 128 * h : 128 * h + 128]
+        if m % OUT_STEP == OUT_STEP - 1:
+            at = slice(2 * Q * (m + 1 - OUT_STEP), 2 * Q * (m + 1))
+            copies.append(
+                pltpu.make_async_copy(new_ref.at[at], out_ref.at[at], sems.at[m // OUT_STEP])
+            )
+            copies[-1].start()
+    for copy in copies:
+        copy.wait()
 
 
 VMEM = pl.BlockSpec(memory_space=pltpu.VMEM)
@@ -426,7 +436,11 @@
     )
     (out,) = call(
         last_kernel, [], [dense, base, *bundles], [((2 * NODES, CELLS // 2), F32)],
-        [pltpu.VMEM((NODES, CELLS), F32)],
+        [
+            pltpu.VMEM((NODES, CELLS), F32), pltpu.VMEM((2 * NODES, CELLS // 2), F32),
+            pltpu.SemaphoreType.DMA((Q // OUT_STEP,)),
+        ],
+        (0,),
     )
     return out.reshape(distribution.shape)
 

time: 86.9 us -> 86.9 us (level)
  no operation moved by 1% of the time
where the time goes in v8:
time: 86.9 us; the launch traced here: 86.4 us
  blocking collectives  40.3 us (46%)
  starting transfers between devices  23.6 us (27%)
  waiting for transfers between devices  12.4 us (14%)
  Pallas kernels  6.47 us (7%)
  local copies, waits for them, and re-layouts  3.46 us (4%)
    all_to_all x2, blocking collectives, gather(): lax.all_to_all(copies, axes, 0, 0, axis_index_groups=groups, tiled=True)  28.8 us
    ppermute x6, starting transfers between devices, gather(): return [bundle] + [lax.ppermute(bundle, axes, p) for p in pairs]  16.1 us
    all_to_all x1, blocking collectives, spread(): return lax.all_to_all(copies, 'vert', 0, 0, tiled=True)  11.5 us
    ppermute x4, waiting for transfers between devices, sides(): return (lax.ppermute(low, 'gx', down), lax.ppermute(high, 'gx', up))  9.75 us
    ppermute x4, starting transfers between devices, sides(): return (lax.ppermute(low, 'gx', down), lax.ppermute(high, 'gx', up))  7.46 us
    pallas_call x8, Pallas kernels, call(): pl.pallas_call(kernel, out_shape=[(pltpu.HBM if i in in_hbm else jax.Shap...  6.47 us
    unnamed x12, local copies, waits for them, and re-layouts  3.46 us
    ppermute x6, waiting for transfers between devices, gather(): return [bundle] + [lax.ppermute(bundle, axes, p) for p in pairs]  2.63 us
  transfers between devices with their start and end apart: 10, of which 4 were waited for; matrix products, arithmetic and copies ran while one was open for 0% of the time, Pallas kernels for 3%

profile of v8, /device:TPU:8, one launch (start us, length us, event | category | flops | bytes accessed | tf_op | source)
XLA Modules:
  0.0 86.4 jit_solution(15437125067972024442)
XLA Ops:
  0.0 0.0 copy-start.4
  0.0 0.0 copy-start
  0.0 1.0 %copy-done = f32[256,1,256]{2,1,0:T(1,128)S(1)} copy-done((f32[256,1,256]{2,1,0:T(1,128)S(1)}, f32[256,1,256]{2,1,0:T(1,128)}, u32[]{:S(2)}) %copy-start) | copy-done | bytes 262168
  1.0 0.0 copy-start.1
  1.0 0.1 shard_map.56
  1.0 15.0 %all_to_all.33 = bf16[4,256,256]{2,1,0:T(8,128)(2,1)S(1)} all-to-all(bf16[4,256,256]{2,1,0:T(8,128)(2,1)S(1)} %bitcast.26), channel_id=1, replica_groups={{0,4,8,12},{1,5,9,13},{2,6,10,14},{3,7,11,15},{16,17,18,19},{20,21,22,2..., dimensions={0} | all-to-all | bytes 1048576 | tf_op jit(solution)/shard_map/all_to_all | solution.py:391
  16.0 1.9 %collective-permute-start.4 = (bf16[1024,256]{1,0:T(8,128)(2,1)S(1)}, bf16[1024,256]{1,0:T(8,128)(2,1)S(1)}, u32[]{:S(2)}, u32[]{:S(2)}) collective-permute-start(bf16[1024,256]{1,0:T(8,128)(2,1)S(1)} %bitcast.20), channel_id=1, source_target_pairs={{0,3},{4,7},{8,11},{12,15},{1,0},{5,4},{9,8},{13,12},{2,1},{6,5},{... | collective-permute-start | bytes 1572872 | tf_op jit(solution)/shard_map/ppermute | solution.py:392
  17.9 1.9 %collective-permute-start.3 = (bf16[1024,256]{1,0:T(8,128)(2,1)S(1)}, bf16[1024,256]{1,0:T(8,128)(2,1)S(1)}, u32[]{:S(2)}, u32[]{:S(2)}) collective-permute-start(bf16[1024,256]{1,0:T(8,128)(2,1)S(1)} %bitcast.21), channel_id=1, source_target_pairs={{0,2},{4,6},{8,10},{12,14},{1,3},{5,7},{9,11},{13,15},{2,0},{6,4},... | collective-permute-start | bytes 1572872 | tf_op jit(solution)/shard_map/ppermute | solution.py:392
  19.9 3.9 %collective-permute-start.2 = (bf16[1024,256]{1,0:T(8,128)(2,1)S(1)}, bf16[1024,256]{1,0:T(8,128)(2,1)S(1)}, u32[]{:S(2)}, u32[]{:S(2)}) collective-permute-start(bf16[1024,256]{1,0:T(8,128)(2,1)S(1)} %bitcast.22), channel_id=1, source_target_pairs={{0,1},{4,5},{8,9},{12,13},{1,2},{5,6},{9,10},{13,14},{2,3},{6,7},{... | collective-permute-start | bytes 1572872 | tf_op jit(solution)/shard_map/ppermute | solution.py:392
  23.8 6.9 %collective-permute-start = (f32[128,256]{1,0:T(8,128)S(1)}, f32[128,256]{1,0:T(8,128)S(1)}, u32[]{:S(2)}, u32[]{:S(2)}) collective-permute-start(f32[128,256]{1,0:T(8,128)S(1)} %get-tuple-element.16), channel_id=1, source_target_pairs={{16,0},{32,16},{48,32},{64,48},{80,64},{96,80},{112,96},{128,112},... | collective-permute-start | bytes 393224 | tf_op jit(solution)/shard_map/ppermute | solution.py:371
  30.7 0.0 collective-permute-start.1
  30.7 0.1 pad_add_fusion.place_ref
  30.8 0.0 copy-start.2
  30.8 1.1 %copy-done.2 = bf16[2,128,1536]{2,1,0:T(8,128)(2,1)S(1)} copy-done((bf16[2,128,1536]{2,1,0:T(8,128)(2,1)S(1)}, bf16[2,128,1536]{2,1,0:T(8,128)(2,1)}, u32[]{:S(2)}) %copy-start.2) | copy-done | bytes 786456
  31.9 0.0 copy-start.3
  31.9 0.7 copy-done.3
  32.6 0.0 copy-start.5
  32.6 0.7 copy-done.5
  33.3 1.8 %shard_map.55 = (bf16[256,4096]{1,0:T(8,128)(2,1)S(1)}, f32[33,8,128]{2,1,0:T(8,128)}) custom-call(s32[2,12]{1,0:T(2,128)S(1)} %copy-done.5, s32[3]{0:T(128)S(1)} %pad_add_fusion.place_ref, f32[1]{0:T(128)} %bitcast.3.z_ref, f32[1,256]{1,0:T(1,128)S(1)} %bitcast.28, bf16[2,128,1536]{2,1,0:T(8,128)(2,1)S(1)} %copy-done.2), custom_call_target="tpu_custom_call" | custom-call | tf_op jit(solution)/shard_map/pallas_call | solution.py:355
  35.1 0.0 collective-permute-done.above_ref
  35.1 1.2 %collective-permute-done.1.below_ref = f32[128,256]{1,0:T(8,128)S(1)} collective-permute-done((f32[128,256]{1,0:T(8,128)S(1)}, f32[128,256]{1,0:T(8,128)S(1)}, u32[]{:S(2)}, u32[]{:S(2)}) %collective-permute-start.1) | collective-permute-done | bytes 131104 | tf_op jit(solution)/shard_map/ppermute | solution.py:371
  36.3 0.0 copy-done.4
  36.3 0.0 copy-done.1
  36.3 0.3 shard_map.57.base_ref
  36.6 0.0 collective-permute-done.4.back_ref
  36.6 0.0 collective-permute-done.3.far_ref
  36.6 0.0 collective-permute-done.2.near_ref
  36.6 1.3 %shard_map.58 = (f32[272,256]{1,0:T(8,128)S(1)}, f32[384,256]{1,0:T(8,128)S(1)}) custom-call(bf16[256,4096]{1,0:T(8,128)(2,1)S(1)} %get-tuple-element.15.dense_ref, f32[264,256]{1,0:T(8,128)S(1)} %shard_map.57.base_ref, bf16[1024,256]{1,0:T(8,128)(2,1)S(1)} %bitcast.23, bf16[1024,256]{1,0:T(8,128)(2,1)S(1)} %collective-permute-done.2.near_ref, ...), custom_call_target="tpu_custom_call" | custom-call | tf_op jit(solution)/shard_map/pallas_call | solution.py:355
  37.9 11.5 %all_to_all.34 = f32[16,24,256]{2,1,0:T(8,128)S(1)} all-to-all(f32[16,24,256]{2,1,0:T(8,128)S(1)} %bitcast.27), channel_id=1, replica_groups=mesh['gx'=32,'vert'=16] {'vert'}, dimensions={0} | all-to-all | bytes 786432 | tf_op jit(solution)/shard_map/all_to_all | solution.py:375
  49.4 0.7 shard_map.61
  50.1 13.9 %all_to_all.35 = bf16[4,272,256]{2,1,0:T(8,128)(2,1)S(1)} all-to-all(bf16[4,272,256]{2,1,0:T(8,128)(2,1)S(1)} %bitcast.19), channel_id=1, replica_groups={{0,4,8,12},{1,5,9,13},{2,6,10,14},{3,7,11,15},{16,17,18,19},{20,21,22,2..., dimensions={0} | all-to-all | bytes 1114112 | tf_op jit(solution)/shard_map/all_to_all | solution.py:391
  64.0 2.1 %collective-permute-start.9 = (bf16[1088,256]{1,0:T(8,128)(2,1)S(1)}, bf16[1088,256]{1,0:T(8,128)(2,1)S(1)}, u32[]{:S(2)}, u32[]{:S(2)}) collective-permute-start(bf16[1088,256]{1,0:T(8,128)(2,1)S(1)} %bitcast.15), channel_id=1, source_target_pairs={{0,3},{4,7},{8,11},{12,15},{1,0},{5,4},{9,8},{13,12},{2,1},{6,5},{... | collective-permute-start | bytes 1671176 | tf_op jit(solution)/shard_map/ppermute | solution.py:392
  66.1 4.3 %collective-permute-start.8 = (bf16[1088,256]{1,0:T(8,128)(2,1)S(1)}, bf16[1088,256]{1,0:T(8,128)(2,1)S(1)}, u32[]{:S(2)}, u32[]{:S(2)}) collective-permute-start(bf16[1088,256]{1,0:T(8,128)(2,1)S(1)} %bitcast.16), channel_id=1, source_target_pairs={{0,2},{4,6},{8,10},{12,14},{1,3},{5,7},{9,11},{13,15},{2,0},{6,4},... | collective-permute-start | bytes 1671176 | tf_op jit(solution)/shard_map/ppermute | solution.py:392
  70.5 1.9 %collective-permute-start.7 = (bf16[1088,256]{1,0:T(8,128)(2,1)S(1)}, bf16[1088,256]{1,0:T(8,128)(2,1)S(1)}, u32[]{:S(2)}, u32[]{:S(2)}) collective-permute-start(bf16[1088,256]{1,0:T(8,128)(2,1)S(1)} %bitcast.17), channel_id=1, source_target_pairs={{0,1},{4,5},{8,9},{12,13},{1,2},{5,6},{9,10},{13,14},{2,3},{6,7},{... | collective-permute-start | bytes 1671176 | tf_op jit(solution)/shard_map/ppermute | solution.py:392
  72.4 0.6 shard_map.59
  73.0 0.5 collective-permute-start.5
  73.5 0.0 collective-permute-start.6
  73.5 2.6 %collective-permute-done.5.above_ref = f32[136,256]{1,0:T(8,128)S(1)} collective-permute-done((f32[136,256]{1,0:T(8,128)S(1)}, f32[136,256]{1,0:T(8,128)S(1)}, u32[]{:S(2)}, u32[]{:S(2)}) %collective-permute-start.5) | collective-permute-done | bytes 139296 | tf_op jit(solution)/shard_map/ppermute | solution.py:371
  76.1 6.0 %collective-permute-done.6.below_ref = f32[136,256]{1,0:T(8,128)S(1)} collective-permute-done((f32[136,256]{1,0:T(8,128)S(1)}, f32[136,256]{1,0:T(8,128)S(1)}, u32[]{:S(2)}, u32[]{:S(2)}) %collective-permute-start.6) | collective-permute-done | bytes 139296 | tf_op jit(solution)/shard_map/ppermute | solution.py:371
  82.1 0.3 shard_map.60.base_ref
  82.4 0.0 collective-permute-done.9.back_ref
  82.4 0.0 collective-permute-done.8.far_ref
  82.4 2.6 %collective-permute-done.7.near_ref = bf16[1088,256]{1,0:T(8,128)(2,1)S(1)} collective-permute-done((bf16[1088,256]{1,0:T(8,128)(2,1)S(1)}, bf16[1088,256]{1,0:T(8,128)(2,1)S(1)}, u32[]{:S(2)}, u32[]{:S(2)}) %collective-permute-start.7) | collective-permute-done | bytes 557088 | tf_op jit(solution)/shard_map/ppermute | solution.py:392
  85.0 1.4 %shard_map.62 = f32[512,128]{1,0:T(8,128)} custom-call(bf16[256,4096]{1,0:T(8,128)(2,1)S(1)} %get-tuple-element.15.dense_ref, f32[280,256]{1,0:T(8,128)S(1)} %shard_map.60.base_ref, bf16[1088,256]{1,0:T(8,128)(2,1)S(1)} %bitcast.18, bf16[1088,256]{1,0:T(8,128)(2,1)S(1)} %collective-permute-done.7.near_ref, ...), custom_call_target="tpu_custom_call" | custom-call | tf_op jit(solution)/shard_map/pallas_call | solution.py:355
Async XLA Ops:
  0.0 36.3 %copy-start.4 = (f32[1,256]{1,0:T(1,128)S(1)}, f32[1,256]{1,0:T(1,128)}, u32[]{:S(2)}) copy-start(f32[1,256]{1,0:T(1,128)} %rate_ref.3) | copy-start | bytes 3076
  0.0 1.0 %copy-start = (f32[256,1,256]{2,1,0:T(1,128)S(1)}, f32[256,1,256]{2,1,0:T(1,128)}, u32[]{:S(2)}) copy-start(f32[256,1,256]{2,1,0:T(1,128)} %param.5) | copy-start | bytes 786436
  1.0 35.4 %copy-start.1 = (f32[256,1,256]{2,1,0:T(1,128)S(1)}, f32[256,1,256]{2,1,0:T(1,128)}, u32[]{:S(2)}) copy-start(f32[256,1,256]{2,1,0:T(1,128)} %param.5) | copy-start | bytes 786436
  16.0 20.6 %collective-permute-start.4 = (bf16[1024,256]{1,0:T(8,128)(2,1)S(1)}, bf16[1024,256]{1,0:T(8,128)(2,1)S(1)}, u32[]{:S(2)}, u32[]{:S(2)}) collective-permute-start(bf16[1024,256]{1,0:T(8,128)(2,1)S(1)} %bitcast.20), channel_id=1, source_target_pairs={{0,3},{4,7},{8,11},{12,15},{1,0},{5,4},{9,8},{13,12},{2,1},{6,5},{... | collective-permute-start | bytes 1572872 | tf_op jit(solution)/shard_map/ppermute | solution.py:392
  17.9 18.7 %collective-permute-start.3 = (bf16[1024,256]{1,0:T(8,128)(2,1)S(1)}, bf16[1024,256]{1,0:T(8,128)(2,1)S(1)}, u32[]{:S(2)}, u32[]{:S(2)}) collective-permute-start(bf16[1024,256]{1,0:T(8,128)(2,1)S(1)} %bitcast.21), channel_id=1, source_target_pairs={{0,2},{4,6},{8,10},{12,14},{1,3},{5,7},{9,11},{13,15},{2,0},{6,4},... | collective-permute-start | bytes 1572872 | tf_op jit(solution)/shard_map/ppermute | solution.py:392
  19.9 16.8 %collective-permute-start.2 = (bf16[1024,256]{1,0:T(8,128)(2,1)S(1)}, bf16[1024,256]{1,0:T(8,128)(2,1)S(1)}, u32[]{:S(2)}, u32[]{:S(2)}) collective-permute-start(bf16[1024,256]{1,0:T(8,128)(2,1)S(1)} %bitcast.22), channel_id=1, source_target_pairs={{0,1},{4,5},{8,9},{12,13},{1,2},{5,6},{9,10},{13,14},{2,3},{6,7},{... | collective-permute-start | bytes 1572872 | tf_op jit(solution)/shard_map/ppermute | solution.py:392
  23.8 11.3 %collective-permute-start = (f32[128,256]{1,0:T(8,128)S(1)}, f32[128,256]{1,0:T(8,128)S(1)}, u32[]{:S(2)}, u32[]{:S(2)}) collective-permute-start(f32[128,256]{1,0:T(8,128)S(1)} %get-tuple-element.16), channel_id=1, source_target_pairs={{16,0},{32,16},{48,32},{64,48},{80,64},{96,80},{112,96},{128,112},... | collective-permute-start | bytes 393224 | tf_op jit(solution)/shard_map/ppermute | solution.py:371
  30.7 5.6 %collective-permute-start.1 = (f32[128,256]{1,0:T(8,128)S(1)}, f32[128,256]{1,0:T(8,128)S(1)}, u32[]{:S(2)}, u32[]{:S(2)}) collective-permute-start(f32[128,256]{1,0:T(8,128)S(1)} %get-tuple-element.17), channel_id=1, source_target_pairs={{0,16},{16,32},{32,48},{48,64},{64,80},{80,96},{96,112},{112,128},... | collective-permute-start | bytes 393224 | tf_op jit(solution)/shard_map/ppermute | solution.py:371
  30.8 1.1 %copy-start.2 = (bf16[2,128,1536]{2,1,0:T(8,128)(2,1)S(1)}, bf16[2,128,1536]{2,1,0:T(8,128)(2,1)}, u32[]{:S(2)}) copy-start(bf16[2,128,1536]{2,1,0:T(8,128)(2,1)} %tiles_ref.1) | copy-start | bytes 2359300
  31.9 0.7 copy-start.3
  32.6 0.7 copy-start.5
  64.0 18.4 %collective-permute-start.9 = (bf16[1088,256]{1,0:T(8,128)(2,1)S(1)}, bf16[1088,256]{1,0:T(8,128)(2,1)S(1)}, u32[]{:S(2)}, u32[]{:S(2)}) collective-permute-start(bf16[1088,256]{1,0:T(8,128)(2,1)S(1)} %bitcast.15), channel_id=1, source_target_pairs={{0,3},{4,7},{8,11},{12,15},{1,0},{5,4},{9,8},{13,12},{2,1},{6,5},{... | collective-permute-start | bytes 1671176 | tf_op jit(solution)/shard_map/ppermute | solution.py:392
  66.1 16.3 %collective-permute-start.8 = (bf16[1088,256]{1,0:T(8,128)(2,1)S(1)}, bf16[1088,256]{1,0:T(8,128)(2,1)S(1)}, u32[]{:S(2)}, u32[]{:S(2)}) collective-permute-start(bf16[1088,256]{1,0:T(8,128)(2,1)S(1)} %bitcast.16), channel_id=1, source_target_pairs={{0,2},{4,6},{8,10},{12,14},{1,3},{5,7},{9,11},{13,15},{2,0},{6,4},... | collective-permute-start | bytes 1671176 | tf_op jit(solution)/shard_map/ppermute | solution.py:392
  70.5 14.6 %collective-permute-start.7 = (bf16[1088,256]{1,0:T(8,128)(2,1)S(1)}, bf16[1088,256]{1,0:T(8,128)(2,1)S(1)}, u32[]{:S(2)}, u32[]{:S(2)}) collective-permute-start(bf16[1088,256]{1,0:T(8,128)(2,1)S(1)} %bitcast.17), channel_id=1, source_target_pairs={{0,1},{4,5},{8,9},{12,13},{1,2},{5,6},{9,10},{13,14},{2,3},{6,7},{... | collective-permute-start | bytes 1671176 | tf_op jit(solution)/shard_map/ppermute | solution.py:392
  73.0 3.1 %collective-permute-start.5 = (f32[136,256]{1,0:T(8,128)S(1)}, f32[136,256]{1,0:T(8,128)S(1)}, u32[]{:S(2)}, u32[]{:S(2)}) collective-permute-start(f32[136,256]{1,0:T(8,128)S(1)} %get-tuple-element.23), channel_id=1, source_target_pairs={{16,0},{32,16},{48,32},{64,48},{80,64},{96,80},{112,96},{128,112},... | collective-permute-start | bytes 417800 | tf_op jit(solution)/shard_map/ppermute | solution.py:371
  73.5 8.6 %collective-permute-start.6 = (f32[136,256]{1,0:T(8,128)S(1)}, f32[136,256]{1,0:T(8,128)S(1)}, u32[]{:S(2)}, u32[]{:S(2)}) collective-permute-start(f32[136,256]{1,0:T(8,128)S(1)} %get-tuple-element.24), channel_id=1, source_target_pairs={{0,16},{16,32},{32,48},{48,64},{64,80},{80,96},{96,112},{112,128},... | collective-permute-start | bytes 417800 | tf_op jit(solution)/shard_map/ppermute | solution.py:371

commit v9 on v7

--- a/solution.py
+++ b/solution.py
@@ -264,12 +264,16 @@
     return (first, second, down), wk, small, inverse, coeffs
 
 
-def middle_kernel(payload_ref, scaled_ref, copies_ref, block_ref):
+def middle_kernel(
+    payload_ref, scaled_ref, copies_ref, state_ref, low_ref, high_ref, block_ref
+):
     group, wk, small, inverse, coeffs = totals_of(payload_ref, scaled_ref)
     z_speed = scaled_ref[NODES + 3 : NODES + 4, :]
     for m in range(Q):
         rows = slice(Q * m, Q * m + Q)
         s = scaled_ref[rows, :] + equilibrium_rows(m, coeffs, z_speed)
+        state_ref[rows, :] = s
+        store_sides(m, s, low_ref, high_ref)
         rounded = s.astype(BF16)
         block_ref[rows, :] = rounded
         for part in range(SIDE):
@@ -282,22 +286,12 @@
     for part in range(SIDE):
         start = part * (NODES + EXTRA) + NODES
         copies_ref[start : start + EXTRA, :] = own
-
-
-def state_kernel(payload_ref, scaled_ref, state_ref, low_ref, high_ref):
-    group, wk, small, inverse, coeffs = totals_of(payload_ref, scaled_ref)
-    z_speed = scaled_ref[NODES + 3 : NODES + 4, :]
     from_eq = [apply_small(small, 8 * t, coeffs) for t in range(GROUPS)]
     flux = from_eq[1] + from_eq[2]
     for t, shift in ((3, from_below_y), (4, from_above_y), (5, from_below_z), (6, from_above_z)):
         flux = flux + (from_eq[t] - shift(from_eq[t]))
     high_ref[NODES // 2 :, :] = group[1] + from_eq[1]
     low_ref[NODES // 2 :, :] = group[2] + from_eq[2]
-    for m in range(Q):
-        rows = slice(Q * m, Q * m + Q)
-        s = scaled_ref[rows, :] + equilibrium_rows(m, coeffs, z_speed)
-        state_ref[rows, :] = s
-        store_sides(m, s, low_ref, high_ref)
     state_ref[NODES : NODES + 8, :] = group[0] + from_eq[0] - flux
     state_ref[NODES + 8 :, :] = jnp.concatenate([inverse, inverse], axis=1)
 
@@ -410,15 +404,15 @@
         [pltpu.VMEM(wk_rows, F32), dma], (), [wk],
     )
     payload = spread(payload)
-    (copies,) = call(
-        middle_kernel, [], [payload, scaled], [((SIDE * (NODES + EXTRA), CELLS), BF16)],
+    copies, state, low, high = call(
+        middle_kernel, [], [payload, scaled],
+        [
+            ((SIDE * (NODES + EXTRA), CELLS), BF16), ((NODES + 16, CELLS), F32),
+            ((half + 8, CELLS), F32), ((half + 8, CELLS), F32),
+        ],
         [pltpu.VMEM((NODES, CELLS), BF16)],
     )
     bundles = gather(copies)
-    state, low, high = call(
-        state_kernel, [], [payload, scaled],
-        [((NODES + 16, CELLS), F32), ((half + 8, CELLS), F32), ((half + 8, CELLS), F32)],
-    )
     above, below = sides(low, high)
     (base,) = call(
         second_base_kernel, [z_speed], [state, relax_rate, above, below],

time: 86.9 us -> 86.9 us (level)
    pallas_call x8 -> x7, Pallas kernels: 6.5 us -> 5.89 us  [call(): pl.pallas_call(kernel, out_shape=[(pltpu.HBM if i in in_hbm else jax.Shap...]
where the time goes in v9:
time: 86.9 us; the launch traced here: 86.5 us
  blocking collectives  40.3 us (46%)
  starting transfers between devices  23.6 us (27%)
  waiting for transfers between devices  13 us (15%)
  Pallas kernels  5.89 us (7%)
  local copies, waits for them, and re-layouts  3.46 us (4%)
    all_to_all x2, blocking collectives, gather(): lax.all_to_all(copies, axes, 0, 0, axis_index_groups=groups, tiled=True)  28.8 us
    ppermute x6, starting transfers between devices, gather(): return [bundle] + [lax.ppermute(bundle, axes, p) for p in pairs]  16.1 us
    all_to_all x1, blocking collectives, spread(): return lax.all_to_all(copies, 'vert', 0, 0, tiled=True)  11.5 us
    ppermute x4, waiting for transfers between devices, sides(): return (lax.ppermute(low, 'gx', down), lax.ppermute(high, 'gx', up))  9.75 us
    ppermute x4, starting transfers between devices, sides(): return (lax.ppermute(low, 'gx', down), lax.ppermute(high, 'gx', up))  7.46 us
    pallas_call x7, Pallas kernels, call(): pl.pallas_call(kernel, out_shape=[(pltpu.HBM if i in in_hbm else jax.Shap...  5.89 us
    unnamed x12, local copies, waits for them, and re-layouts  3.46 us
    ppermute x6, waiting for transfers between devices, gather(): return [bundle] + [lax.ppermute(bundle, axes, p) for p in pairs]  3.26 us
  transfers between devices with their start and end apart: 10, of which 4 were waited for; matrix products, arithmetic and copies ran while one was open for 0% of the time, Pallas kernels for 3%

profile of v9, /device:TPU:8, one launch (start us, length us, event | category | flops | bytes accessed | tf_op | source)
XLA Modules:
  0.0 86.5 jit_solution(9824500342727841851)
XLA Ops:
  0.0 0.0 copy-start.4
  0.0 0.0 copy-start
  0.0 1.0 %copy-done = f32[256,1,256]{2,1,0:T(1,128)S(1)} copy-done((f32[256,1,256]{2,1,0:T(1,128)S(1)}, f32[256,1,256]{2,1,0:T(1,128)}, u32[]{:S(2)}) %copy-start) | copy-done | bytes 262168
  1.0 0.0 copy-start.1
  1.0 0.1 shard_map.56
  1.0 15.0 %all_to_all.33 = bf16[4,256,256]{2,1,0:T(8,128)(2,1)S(1)} all-to-all(bf16[4,256,256]{2,1,0:T(8,128)(2,1)S(1)} %bitcast.25), channel_id=1, replica_groups={{0,4,8,12},{1,5,9,13},{2,6,10,14},{3,7,11,15},{16,17,18,19},{20,21,22,2..., dimensions={0} | all-to-all | bytes 1048576 | tf_op jit(solution)/shard_map/all_to_all | solution.py:375
  16.0 1.9 %collective-permute-start.4 = (bf16[1024,256]{1,0:T(8,128)(2,1)S(1)}, bf16[1024,256]{1,0:T(8,128)(2,1)S(1)}, u32[]{:S(2)}, u32[]{:S(2)}) collective-permute-start(bf16[1024,256]{1,0:T(8,128)(2,1)S(1)} %bitcast.17), channel_id=1, source_target_pairs={{0,3},{4,7},{8,11},{12,15},{1,0},{5,4},{9,8},{13,12},{2,1},{6,5},{... | collective-permute-start | bytes 1572872 | tf_op jit(solution)/shard_map/ppermute | solution.py:376
  17.9 1.9 %collective-permute-start.3 = (bf16[1024,256]{1,0:T(8,128)(2,1)S(1)}, bf16[1024,256]{1,0:T(8,128)(2,1)S(1)}, u32[]{:S(2)}, u32[]{:S(2)}) collective-permute-start(bf16[1024,256]{1,0:T(8,128)(2,1)S(1)} %bitcast.18), channel_id=1, source_target_pairs={{0,2},{4,6},{8,10},{12,14},{1,3},{5,7},{9,11},{13,15},{2,0},{6,4},... | collective-permute-start | bytes 1572872 | tf_op jit(solution)/shard_map/ppermute | solution.py:376
  19.9 3.9 %collective-permute-start.2 = (bf16[1024,256]{1,0:T(8,128)(2,1)S(1)}, bf16[1024,256]{1,0:T(8,128)(2,1)S(1)}, u32[]{:S(2)}, u32[]{:S(2)}) collective-permute-start(bf16[1024,256]{1,0:T(8,128)(2,1)S(1)} %bitcast.19), channel_id=1, source_target_pairs={{0,1},{4,5},{8,9},{12,13},{1,2},{5,6},{9,10},{13,14},{2,3},{6,7},{... | collective-permute-start | bytes 1572872 | tf_op jit(solution)/shard_map/ppermute | solution.py:376
  23.8 6.9 %collective-permute-start = (f32[128,256]{1,0:T(8,128)S(1)}, f32[128,256]{1,0:T(8,128)S(1)}, u32[]{:S(2)}, u32[]{:S(2)}) collective-permute-start(f32[128,256]{1,0:T(8,128)S(1)} %get-tuple-element.17), channel_id=1, source_target_pairs={{16,0},{32,16},{48,32},{64,48},{80,64},{96,80},{112,96},{128,112},... | collective-permute-start | bytes 393224 | tf_op jit(solution)/shard_map/ppermute | solution.py:355
  30.7 0.0 collective-permute-start.1
  30.7 0.1 pad_add_fusion.place_ref
  30.8 0.0 copy-start.2
  30.8 1.1 %copy-done.2 = bf16[2,128,1536]{2,1,0:T(8,128)(2,1)S(1)} copy-done((bf16[2,128,1536]{2,1,0:T(8,128)(2,1)S(1)}, bf16[2,128,1536]{2,1,0:T(8,128)(2,1)}, u32[]{:S(2)}) %copy-start.2) | copy-done | bytes 786456
  31.9 0.0 copy-start.3
  31.9 0.7 copy-done.3
  32.6 0.0 copy-start.5
  32.6 0.7 copy-done.5
  33.3 1.8 %shard_map.55 = (bf16[256,4096]{1,0:T(8,128)(2,1)S(1)}, f32[33,8,128]{2,1,0:T(8,128)}) custom-call(s32[2,12]{1,0:T(2,128)S(1)} %copy-done.5, s32[3]{0:T(128)S(1)} %pad_add_fusion.place_ref, f32[1]{0:T(128)} %bitcast.3.z_ref, f32[1,256]{1,0:T(1,128)S(1)} %bitcast.27, bf16[2,128,1536]{2,1,0:T(8,128)(2,1)S(1)} %copy-done.2), custom_call_target="tpu_custom_call" | custom-call | tf_op jit(solution)/shard_map/pallas_call | solution.py:339
  35.1 0.0 collective-permute-done.above_ref
  35.1 1.2 %collective-permute-done.1.below_ref = f32[128,256]{1,0:T(8,128)S(1)} collective-permute-done((f32[128,256]{1,0:T(8,128)S(1)}, f32[128,256]{1,0:T(8,128)S(1)}, u32[]{:S(2)}, u32[]{:S(2)}) %collective-permute-start.1) | collective-permute-done | bytes 131104 | tf_op jit(solution)/shard_map/ppermute | solution.py:355
  36.3 0.0 copy-done.4
  36.3 0.0 copy-done.1
  36.3 0.3 shard_map.57.base_ref
  36.6 0.0 collective-permute-done.4.back_ref
  36.6 0.0 collective-permute-done.3.far_ref
  36.6 0.0 collective-permute-done.2.near_ref
  36.6 1.3 %shard_map.58 = (f32[272,256]{1,0:T(8,128)S(1)}, f32[384,256]{1,0:T(8,128)S(1)}) custom-call(bf16[256,4096]{1,0:T(8,128)(2,1)S(1)} %get-tuple-element.16.dense_ref, f32[264,256]{1,0:T(8,128)S(1)} %shard_map.57.base_ref, bf16[1024,256]{1,0:T(8,128)(2,1)S(1)} %bitcast.20, bf16[1024,256]{1,0:T(8,128)(2,1)S(1)} %collective-permute-done.2.near_ref, ...), custom_call_target="tpu_custom_call" | custom-call | tf_op jit(solution)/shard_map/pallas_call | solution.py:339
  37.9 11.5 %all_to_all.34 = f32[16,24,256]{2,1,0:T(8,128)S(1)} all-to-all(f32[16,24,256]{2,1,0:T(8,128)S(1)} %bitcast.26), channel_id=1, replica_groups=mesh['gx'=32,'vert'=16] {'vert'}, dimensions={0} | all-to-all | bytes 786432 | tf_op jit(solution)/shard_map/all_to_all | solution.py:359
  49.4 0.7 shard_map.59
  50.1 13.9 %all_to_all.35 = bf16[4,272,256]{2,1,0:T(8,128)(2,1)S(1)} all-to-all(bf16[4,272,256]{2,1,0:T(8,128)(2,1)S(1)} %bitcast.24), channel_id=1, replica_groups={{0,4,8,12},{1,5,9,13},{2,6,10,14},{3,7,11,15},{16,17,18,19},{20,21,22,2..., dimensions={0} | all-to-all | bytes 1114112 | tf_op jit(solution)/shard_map/all_to_all | solution.py:375
  64.0 2.1 %collective-permute-start.9 = (bf16[1088,256]{1,0:T(8,128)(2,1)S(1)}, bf16[1088,256]{1,0:T(8,128)(2,1)S(1)}, u32[]{:S(2)}, u32[]{:S(2)}) collective-permute-start(bf16[1088,256]{1,0:T(8,128)(2,1)S(1)} %bitcast.13), channel_id=1, source_target_pairs={{0,3},{4,7},{8,11},{12,15},{1,0},{5,4},{9,8},{13,12},{2,1},{6,5},{... | collective-permute-start | bytes 1671176 | tf_op jit(solution)/shard_map/ppermute | solution.py:376
  66.1 4.3 %collective-permute-start.8 = (bf16[1088,256]{1,0:T(8,128)(2,1)S(1)}, bf16[1088,256]{1,0:T(8,128)(2,1)S(1)}, u32[]{:S(2)}, u32[]{:S(2)}) collective-permute-start(bf16[1088,256]{1,0:T(8,128)(2,1)S(1)} %bitcast.14), channel_id=1, source_target_pairs={{0,2},{4,6},{8,10},{12,14},{1,3},{5,7},{9,11},{13,15},{2,0},{6,4},... | collective-permute-start | bytes 1671176 | tf_op jit(solution)/shard_map/ppermute | solution.py:376
  70.5 1.9 %collective-permute-start.7 = (bf16[1088,256]{1,0:T(8,128)(2,1)S(1)}, bf16[1088,256]{1,0:T(8,128)(2,1)S(1)}, u32[]{:S(2)}, u32[]{:S(2)}) collective-permute-start(bf16[1088,256]{1,0:T(8,128)(2,1)S(1)} %bitcast.15), channel_id=1, source_target_pairs={{0,1},{4,5},{8,9},{12,13},{1,2},{5,6},{9,10},{13,14},{2,3},{6,7},{... | collective-permute-start | bytes 1671176 | tf_op jit(solution)/shard_map/ppermute | solution.py:376
  72.4 0.5 collective-permute-start.5
  72.9 0.0 collective-permute-start.6
  72.9 2.6 %collective-permute-done.5.above_ref = f32[136,256]{1,0:T(8,128)S(1)} collective-permute-done((f32[136,256]{1,0:T(8,128)S(1)}, f32[136,256]{1,0:T(8,128)S(1)}, u32[]{:S(2)}, u32[]{:S(2)}) %collective-permute-start.5) | collective-permute-done | bytes 139296 | tf_op jit(solution)/shard_map/ppermute | solution.py:355
  75.5 6.0 %collective-permute-done.6.below_ref = f32[136,256]{1,0:T(8,128)S(1)} collective-permute-done((f32[136,256]{1,0:T(8,128)S(1)}, f32[136,256]{1,0:T(8,128)S(1)}, u32[]{:S(2)}, u32[]{:S(2)}) %collective-permute-start.6) | collective-permute-done | bytes 139296 | tf_op jit(solution)/shard_map/ppermute | solution.py:355
  81.5 0.3 shard_map.60.base_ref
  81.7 0.0 collective-permute-done.9.back_ref
  81.8 0.0 collective-permute-done.8.far_ref
  81.8 3.2 %collective-permute-done.7.near_ref = bf16[1088,256]{1,0:T(8,128)(2,1)S(1)} collective-permute-done((bf16[1088,256]{1,0:T(8,128)(2,1)S(1)}, bf16[1088,256]{1,0:T(8,128)(2,1)S(1)}, u32[]{:S(2)}, u32[]{:S(2)}) %collective-permute-start.7) | collective-permute-done | bytes 557088 | tf_op jit(solution)/shard_map/ppermute | solution.py:376
  85.0 1.5 %shard_map.61 = f32[512,128]{1,0:T(8,128)} custom-call(bf16[256,4096]{1,0:T(8,128)(2,1)S(1)} %get-tuple-element.16.dense_ref, f32[280,256]{1,0:T(8,128)S(1)} %shard_map.60.base_ref, bf16[1088,256]{1,0:T(8,128)(2,1)S(1)} %bitcast.16, bf16[1088,256]{1,0:T(8,128)(2,1)S(1)} %collective-permute-done.7.near_ref, ...), custom_call_target="tpu_custom_call" | custom-call | tf_op jit(solution)/shard_map/pallas_call | solution.py:339
Async XLA Ops:
  0.0 36.3 %copy-start.4 = (f32[1,256]{1,0:T(1,128)S(1)}, f32[1,256]{1,0:T(1,128)}, u32[]{:S(2)}) copy-start(f32[1,256]{1,0:T(1,128)} %rate_ref.3) | copy-start | bytes 3076
  0.0 1.0 %copy-start = (f32[256,1,256]{2,1,0:T(1,128)S(1)}, f32[256,1,256]{2,1,0:T(1,128)}, u32[]{:S(2)}) copy-start(f32[256,1,256]{2,1,0:T(1,128)} %param.5) | copy-start | bytes 786436
  1.0 35.4 %copy-start.1 = (f32[256,1,256]{2,1,0:T(1,128)S(1)}, f32[256,1,256]{2,1,0:T(1,128)}, u32[]{:S(2)}) copy-start(f32[256,1,256]{2,1,0:T(1,128)} %param.5) | copy-start | bytes 786436
  16.0 20.6 %collective-permute-start.4 = (bf16[1024,256]{1,0:T(8,128)(2,1)S(1)}, bf16[1024,256]{1,0:T(8,128)(2,1)S(1)}, u32[]{:S(2)}, u32[]{:S(2)}) collective-permute-start(bf16[1024,256]{1,0:T(8,128)(2,1)S(1)} %bitcast.17), channel_id=1, source_target_pairs={{0,3},{4,7},{8,11},{12,15},{1,0},{5,4},{9,8},{13,12},{2,1},{6,5},{... | collective-permute-start | bytes 1572872 | tf_op jit(solution)/shard_map/ppermute | solution.py:376
  17.9 18.7 %collective-permute-start.3 = (bf16[1024,256]{1,0:T(8,128)(2,1)S(1)}, bf16[1024,256]{1,0:T(8,128)(2,1)S(1)}, u32[]{:S(2)}, u32[]{:S(2)}) collective-permute-start(bf16[1024,256]{1,0:T(8,128)(2,1)S(1)} %bitcast.18), channel_id=1, source_target_pairs={{0,2},{4,6},{8,10},{12,14},{1,3},{5,7},{9,11},{13,15},{2,0},{6,4},... | collective-permute-start | bytes 1572872 | tf_op jit(solution)/shard_map/ppermute | solution.py:376
  19.9 16.8 %collective-permute-start.2 = (bf16[1024,256]{1,0:T(8,128)(2,1)S(1)}, bf16[1024,256]{1,0:T(8,128)(2,1)S(1)}, u32[]{:S(2)}, u32[]{:S(2)}) collective-permute-start(bf16[1024,256]{1,0:T(8,128)(2,1)S(1)} %bitcast.19), channel_id=1, source_target_pairs={{0,1},{4,5},{8,9},{12,13},{1,2},{5,6},{9,10},{13,14},{2,3},{6,7},{... | collective-permute-start | bytes 1572872 | tf_op jit(solution)/shard_map/ppermute | solution.py:376
  23.8 11.3 %collective-permute-start = (f32[128,256]{1,0:T(8,128)S(1)}, f32[128,256]{1,0:T(8,128)S(1)}, u32[]{:S(2)}, u32[]{:S(2)}) collective-permute-start(f32[128,256]{1,0:T(8,128)S(1)} %get-tuple-element.17), channel_id=1, source_target_pairs={{16,0},{32,16},{48,32},{64,48},{80,64},{96,80},{112,96},{128,112},... | collective-permute-start | bytes 393224 | tf_op jit(solution)/shard_map/ppermute | solution.py:355
  30.7 5.6 %collective-permute-start.1 = (f32[128,256]{1,0:T(8,128)S(1)}, f32[128,256]{1,0:T(8,128)S(1)}, u32[]{:S(2)}, u32[]{:S(2)}) collective-permute-start(f32[128,256]{1,0:T(8,128)S(1)} %get-tuple-element.18), channel_id=1, source_target_pairs={{0,16},{16,32},{32,48},{48,64},{64,80},{80,96},{96,112},{112,128},... | collective-permute-start | bytes 393224 | tf_op jit(solution)/shard_map/ppermute | solution.py:355
  30.8 1.1 %copy-start.2 = (bf16[2,128,1536]{2,1,0:T(8,128)(2,1)S(1)}, bf16[2,128,1536]{2,1,0:T(8,128)(2,1)}, u32[]{:S(2)}) copy-start(bf16[2,128,1536]{2,1,0:T(8,128)(2,1)} %tiles_ref.1) | copy-start | bytes 2359300
  31.9 0.7 copy-start.3
  32.6 0.7 copy-start.5
  64.0 17.7 %collective-permute-start.9 = (bf16[1088,256]{1,0:T(8,128)(2,1)S(1)}, bf16[1088,256]{1,0:T(8,128)(2,1)S(1)}, u32[]{:S(2)}, u32[]{:S(2)}) collective-permute-start(bf16[1088,256]{1,0:T(8,128)(2,1)S(1)} %bitcast.13), channel_id=1, source_target_pairs={{0,3},{4,7},{8,11},{12,15},{1,0},{5,4},{9,8},{13,12},{2,1},{6,5},{... | collective-permute-start | bytes 1671176 | tf_op jit(solution)/shard_map/ppermute | solution.py:376
  66.1 15.6 %collective-permute-start.8 = (bf16[1088,256]{1,0:T(8,128)(2,1)S(1)}, bf16[1088,256]{1,0:T(8,128)(2,1)S(1)}, u32[]{:S(2)}, u32[]{:S(2)}) collective-permute-start(bf16[1088,256]{1,0:T(8,128)(2,1)S(1)} %bitcast.14), channel_id=1, source_target_pairs={{0,2},{4,6},{8,10},{12,14},{1,3},{5,7},{9,11},{13,15},{2,0},{6,4},... | collective-permute-start | bytes 1671176 | tf_op jit(solution)/shard_map/ppermute | solution.py:376
  70.5 14.6 %collective-permute-start.7 = (bf16[1088,256]{1,0:T(8,128)(2,1)S(1)}, bf16[1088,256]{1,0:T(8,128)(2,1)S(1)}, u32[]{:S(2)}, u32[]{:S(2)}) collective-permute-start(bf16[1088,256]{1,0:T(8,128)(2,1)S(1)} %bitcast.15), channel_id=1, source_target_pairs={{0,1},{4,5},{8,9},{12,13},{1,2},{5,6},{9,10},{13,14},{2,3},{6,7},{... | collective-permute-start | bytes 1671176 | tf_op jit(solution)/shard_map/ppermute | solution.py:376
  72.4 3.1 %collective-permute-start.5 = (f32[136,256]{1,0:T(8,128)S(1)}, f32[136,256]{1,0:T(8,128)S(1)}, u32[]{:S(2)}, u32[]{:S(2)}) collective-permute-start(f32[136,256]{1,0:T(8,128)S(1)} %get-tuple-element.24), channel_id=1, source_target_pairs={{16,0},{32,16},{48,32},{64,48},{80,64},{96,80},{112,96},{128,112},... | collective-permute-start | bytes 417800 | tf_op jit(solution)/shard_map/ppermute | solution.py:355
  72.9 8.6 %collective-permute-start.6 = (f32[136,256]{1,0:T(8,128)S(1)}, f32[136,256]{1,0:T(8,128)S(1)}, u32[]{:S(2)}, u32[]{:S(2)}) collective-permute-start(f32[136,256]{1,0:T(8,128)S(1)} %get-tuple-element.25), channel_id=1, source_target_pairs={{0,16},{16,32},{32,48},{48,64},{64,80},{80,96},{96,112},{112,128},... | collective-permute-start | bytes 417800 | tf_op jit(solution)/shard_map/ppermute | solution.py:355
